TPU v7x, 512 devices: a whole 4x8x8 slice. The times are simulated.
512 devices in a mesh: dom: 64 (over x, z, core), cls: 8 (over y).
Axes of the slice: x: 4, y: 8, z: 8, core: 2. Of those that a mesh axis runs over, the one named last changes fastest.
Arguments:
- images: bfloat16 [2048, 9216], P(('dom', 'cls')), may hold values from -64 to 64
- ctf: float32 [2048, 64], P(('dom', 'cls')), may hold values from 0.2 to 1
- inv_noise: float32 [64], replicated, may hold values from 0.5 to 2
- classes: bfloat16 [400, 9216], P('cls'), may hold values from -0.25 to 0.25
- candidates: int32 [2048, 2], P(('dom', 'cls')), may hold values from 0 to 399, as said below
Outputs:
- class_sums: float32 [9216, 400], P('dom', 'cls')
- weight_sums: float32 [400, 64], P('cls')
- evidence: float32 [2048], P(('dom', 'cls'))
Inputs may be any that keep to these rules, and one draw needn't show every extreme that they name: `candidates`: each row names 2 different classes. Among the 4 particles of one device, at most 2 name a class of any one block b (classes b * 50 to (b + 1) * 50 - 1); for each index along dom, the 8 devices that share it have one common block that exactly 2 particles of each of them name.
All inputs are finite; a program needn't handle non-finite values.
Results may differ from a plain program's by a relative error of at most 0.0053.
Values may be sent and summed in bfloat16 or wider, within the bound.
No kernel may reach another device: no remote copies, remote signals or barrier semaphores. Data moves between devices by JAX's collectives and lax.ppermute only.
A program may use at most 64 MiB of HBM per device.

v0:
```python
import math

import jax
import jax.numpy as jnp
from jax import lax
from jax.sharding import PartitionSpec as P

ANGLES = 72
ROTATIONS = 36
TOP_CAND = 2


NEGATIVE = -1e30


def shards(images, ctf, inv_noise, classes, candidates):
    cls_count = lax.axis_size("cls")
    my_index = lax.axis_index("cls")
    part_dev = images.shape[0]
    class_block = classes.shape[0]
    features = images.shape[1]
    cycles = ctf.shape[1]
    capacity = min(5 * part_dev * TOP_CAND // (2 * cls_count), part_dev)
    group_size = cls_count * part_dev
    shift = features // ANGLES * (ANGLES // ROTATIONS)
    turn_ids = jnp.arange(ROTATIONS, dtype=jnp.int32)
    ctf_noise = ctf * inv_noise[None, :]
    weighted = (images.astype(jnp.float32) * jnp.tile(ctf_noise, (1, features // cycles))).astype(
        jnp.bfloat16
    )
    quadratic = (ctf * ctf * inv_noise[None, :]).astype(jnp.bfloat16)
    everyone = lax.all_gather(candidates, "cls", axis=0, tiled=True)
    block_ids = jnp.arange(class_block, dtype=jnp.int32) + my_index * class_block
    cand_mask = jnp.any(everyone[:, :, None] == block_ids[None, None, :], axis=1).astype(
        jnp.float32
    )
    owner_ids = jnp.arange(cls_count, dtype=jnp.int32)
    routed = jnp.any(
        (everyone // class_block)[:, :, None] == owner_ids[None, None, :], axis=1
    ).astype(jnp.int32)
    by_source = routed.reshape(cls_count, part_dev, cls_count)
    slot_of = jnp.cumsum(by_source, axis=1) - by_source
    slot_ids = jnp.arange(capacity, dtype=jnp.int32)
    mine_routed = lax.dynamic_index_in_dim(by_source, my_index, 0, keepdims=False)
    mine_slot = lax.dynamic_index_in_dim(slot_of, my_index, 0, keepdims=False)
    packing = (mine_routed.T[:, None, :] == 1) & (
        mine_slot.T[:, None, :] == slot_ids[None, :, None]
    )
    packing = packing.reshape(cls_count * capacity, part_dev).astype(jnp.bfloat16)
    send_data = jnp.dot(packing, weighted, preferred_element_type=jnp.float32).astype(jnp.bfloat16)
    send_quad = jnp.dot(packing, quadratic, preferred_element_type=jnp.float32).astype(jnp.bfloat16)
    row_data, row_quad = (
        lax.all_to_all(send_data, "cls", split_axis=0, concat_axis=0, tiled=True),
        lax.all_to_all(send_quad, "cls", split_axis=0, concat_axis=0, tiled=True),
    )
    into_mine = lax.dynamic_index_in_dim(by_source, my_index, 2, keepdims=False)
    slot_mine = lax.dynamic_index_in_dim(slot_of, my_index, 2, keepdims=False)
    selected = (into_mine[:, None, :] == 1) & (slot_mine[:, None, :] == slot_ids[None, :, None])
    diagonal = jnp.eye(cls_count, dtype=jnp.float32)
    unpack = (selected.astype(jnp.float32)[:, :, None, :] * diagonal[:, None, :, None]).reshape(
        cls_count * capacity, group_size
    )
    row_mask = jnp.dot(unpack, cand_mask, precision=lax.Precision.HIGHEST)
    row_count = row_data.shape[0]
    energy = jnp.sum(
        jnp.square(classes.astype(jnp.float32)).reshape(class_block, features // cycles, cycles),
        axis=1,
    )
    quad_wide = row_quad.astype(jnp.float32)
    norm_term = jnp.dot(quad_wide, energy.T, precision=lax.Precision.HIGHEST)
    twin_classes = jnp.concatenate([classes, classes], axis=1)
    feat_block = math.gcd(features, 1152)

    def add_block(block_index, running):
        offset = block_index * feat_block
        rotated = jax.vmap(
            lambda rotation: lax.dynamic_slice_in_dim(
                twin_classes, offset - rotation * shift + features, feat_block, 1
            )
        )(turn_ids)
        section = lax.dynamic_slice_in_dim(row_data, offset, feat_block, 1)
        return running + lax.dot_general(
            section, rotated, (((1,), (2,)), ((), ())), preferred_element_type=jnp.float32
        )

    cross = lax.fori_loop(
        0,
        features // feat_block,
        add_block,
        jnp.zeros((row_count, ROTATIONS, class_block), jnp.float32),
    )
    logits = cross - 0.5 * norm_term[:, None, :]
    live = jnp.broadcast_to(row_mask[:, None, :] > 0.5, logits.shape)
    masked = jnp.where(live, logits, NEGATIVE)
    peak = jnp.max(masked, axis=(1, 2))
    part_total = jnp.sum(jnp.where(live, jnp.exp(masked - peak[:, None, None]), 0.0), axis=(1, 2))
    group_peak = jnp.max(jnp.where(unpack > 0.5, peak[:, None], NEGATIVE), axis=0)
    group_total = jnp.sum(unpack * part_total[:, None], axis=0)
    back_peak, back_total = (
        lax.all_to_all(group_peak, "cls", split_axis=0, concat_axis=0, tiled=True),
        lax.all_to_all(group_total, "cls", split_axis=0, concat_axis=0, tiled=True),
    )
    back_peak = back_peak.reshape(cls_count, part_dev)
    back_total = back_total.reshape(cls_count, part_dev)
    highest = jnp.max(back_peak, axis=0)
    own_evidence = highest + jnp.log(
        jnp.sum(back_total * jnp.exp(back_peak - highest[None, :]), axis=0)
    )
    group_evidence = lax.all_gather(own_evidence, "cls", axis=0, tiled=True)
    row_evidence = jnp.dot(unpack, group_evidence, precision=lax.Precision.HIGHEST)
    posterior = jnp.where(live, jnp.exp(logits - row_evidence[:, None, None]), 0.0).astype(
        jnp.bfloat16
    )
    weight_total = jnp.sum(posterior.astype(jnp.float32), axis=1)
    ctf_part = jnp.dot(weight_total.T, quad_wide, precision=lax.Precision.HIGHEST)
    weight_sums = lax.psum(ctf_part, "dom")
    twin_rows = jnp.concatenate([row_data, row_data], axis=1)

    def add_sums(block_index, running):
        offset = block_index * feat_block
        stacked = jax.vmap(
            lambda rotation: lax.dynamic_slice_in_dim(
                twin_rows, offset + rotation * shift, feat_block, 1
            )
        )(turn_ids)
        block_sum = lax.dot_general(
            posterior, stacked, (((0, 1), (1, 0)), ((), ())), preferred_element_type=jnp.float32
        )
        return lax.dynamic_update_slice_in_dim(running, block_sum, offset, 1)

    summed = lax.fori_loop(
        0, features // feat_block, add_sums, jnp.zeros((class_block, features), jnp.float32)
    )
    full_term = summed.T
    class_sums = lax.psum_scatter(full_term, "dom", scatter_dimension=0, tiled=True)
    return (class_sums, weight_sums, own_evidence)


def solution(mesh):
    in_specs = (
        P(("dom", "cls"), None),
        P(("dom", "cls"), None),
        P(),
        P("cls", None),
        P(("dom", "cls"), None),
    )
    out_specs = (P("dom", "cls"), P("cls", None), P(("dom", "cls")))
    return jax.shard_map(shards, mesh=mesh, in_specs=in_specs, out_specs=out_specs, check_vma=False)
```

profile of v0, /device:TPU:1, one launch (start us, length us, event | category | flops | bytes accessed | tf_op | source)
XLA Modules:
  0.0 1587.2 jit_solution(15716616764184638410)
XLA Ops:
  7.2 14.2 all-gather
  23.6 4.1 all-to-all-start.1
  28.5 2.7 convert_multiply_fusion
  32.4 3.6 reshape.161
  36.9 2.3 reduce_sum.45
  39.2 6.7 all-to-all-start
  46.2 9.4 all-to-all-done
  55.7 612.1 %while.39 = (s32[]{:T(128)}, f32[16,36,50]{2,0,1:T(8,128)S(1)}, bf16[16,9216]{1,0:T(8,128)(2,1)S(1)}, bf16[50,18432]{1,0:T(8,128)(2,1)S(1)}, s32[]{:T(128)}, /*index=5*/s32[]{:T(128)}, s32[]{:T(128)}, s32[]{:T(128)}, s32[]{:T(128)}) while((s32[]{:T(128)}, f32[16,36,50]{2,0,1:T(8,128)S(1)}, bf16[16,9216]{1,0:T(8,128)(2,1)S(1)}, ...), condition=%wide.region_4.5_spmd.clone, body=%wide.region_3.4_spmd.clone.sunk | while | flops 66413024 | bytes 4840298 | solution.py:86
  55.7 71.9 %while.41 = (s32[]{:T(128)}, bf16[50,18432]{1,0:T(8,128)(2,1)S(1)}, s32[36,2]{0,1:T(2,128)S(1)}, bf16[36,50,1152]{2,1,0:T(8,128)(2,1)}, s32[]{:T(128)}) while((s32[]{:T(128)}, bf16[50,18432]{1,0:T(8,128)(2,1)S(1)}, s32[36,2]{0,1:T(2,128)S(1)}, bf16[36,50,1152]{2,1,0:T(8,128)(2,1)}, s32[]{:T(128)}) %tuple.108), condition=%wide.while_cond, body=%wide.while_body.sunk | while | flops 2 | bytes 245337 | solution.py:77
  127.6 4.6 convolution_add_fusion.2
  132.2 71.9 %while.41 = (s32[]{:T(128)}, bf16[50,18432]{1,0:T(8,128)(2,1)S(1)}, s32[36,2]{0,1:T(2,128)S(1)}, bf16[36,50,1152]{2,1,0:T(8,128)(2,1)}, s32[]{:T(128)}) while((s32[]{:T(128)}, bf16[50,18432]{1,0:T(8,128)(2,1)S(1)}, s32[36,2]{0,1:T(2,128)S(1)}, bf16[36,50,1152]{2,1,0:T(8,128)(2,1)}, s32[]{:T(128)}) %tuple.108), condition=%wide.while_cond, body=%wide.while_body.sunk | while | flops 2 | bytes 245337 | solution.py:77
  204.1 4.6 convolution_add_fusion.2
  208.7 71.9 %while.41 = (s32[]{:T(128)}, bf16[50,18432]{1,0:T(8,128)(2,1)S(1)}, s32[36,2]{0,1:T(2,128)S(1)}, bf16[36,50,1152]{2,1,0:T(8,128)(2,1)}, s32[]{:T(128)}) while((s32[]{:T(128)}, bf16[50,18432]{1,0:T(8,128)(2,1)S(1)}, s32[36,2]{0,1:T(2,128)S(1)}, bf16[36,50,1152]{2,1,0:T(8,128)(2,1)}, s32[]{:T(128)}) %tuple.108), condition=%wide.while_cond, body=%wide.while_body.sunk | while | flops 2 | bytes 245337 | solution.py:77
  280.6 4.6 convolution_add_fusion.2
  285.2 71.9 %while.41 = (s32[]{:T(128)}, bf16[50,18432]{1,0:T(8,128)(2,1)S(1)}, s32[36,2]{0,1:T(2,128)S(1)}, bf16[36,50,1152]{2,1,0:T(8,128)(2,1)}, s32[]{:T(128)}) while((s32[]{:T(128)}, bf16[50,18432]{1,0:T(8,128)(2,1)S(1)}, s32[36,2]{0,1:T(2,128)S(1)}, bf16[36,50,1152]{2,1,0:T(8,128)(2,1)}, s32[]{:T(128)}) %tuple.108), condition=%wide.while_cond, body=%wide.while_body.sunk | while | flops 2 | bytes 245337 | solution.py:77
  357.1 4.6 convolution_add_fusion.2
  361.7 71.9 %while.41 = (s32[]{:T(128)}, bf16[50,18432]{1,0:T(8,128)(2,1)S(1)}, s32[36,2]{0,1:T(2,128)S(1)}, bf16[36,50,1152]{2,1,0:T(8,128)(2,1)}, s32[]{:T(128)}) while((s32[]{:T(128)}, bf16[50,18432]{1,0:T(8,128)(2,1)S(1)}, s32[36,2]{0,1:T(2,128)S(1)}, bf16[36,50,1152]{2,1,0:T(8,128)(2,1)}, s32[]{:T(128)}) %tuple.108), condition=%wide.while_cond, body=%wide.while_body.sunk | while | flops 2 | bytes 245337 | solution.py:77
  433.6 4.6 convolution_add_fusion.2
  438.2 71.9 %while.41 = (s32[]{:T(128)}, bf16[50,18432]{1,0:T(8,128)(2,1)S(1)}, s32[36,2]{0,1:T(2,128)S(1)}, bf16[36,50,1152]{2,1,0:T(8,128)(2,1)}, s32[]{:T(128)}) while((s32[]{:T(128)}, bf16[50,18432]{1,0:T(8,128)(2,1)S(1)}, s32[36,2]{0,1:T(2,128)S(1)}, bf16[36,50,1152]{2,1,0:T(8,128)(2,1)}, s32[]{:T(128)}) %tuple.108), condition=%wide.while_cond, body=%wide.while_body.sunk | while | flops 2 | bytes 245337 | solution.py:77
  510.1 4.6 convolution_add_fusion.2
  514.8 71.9 %while.41 = (s32[]{:T(128)}, bf16[50,18432]{1,0:T(8,128)(2,1)S(1)}, s32[36,2]{0,1:T(2,128)S(1)}, bf16[36,50,1152]{2,1,0:T(8,128)(2,1)}, s32[]{:T(128)}) while((s32[]{:T(128)}, bf16[50,18432]{1,0:T(8,128)(2,1)S(1)}, s32[36,2]{0,1:T(2,128)S(1)}, bf16[36,50,1152]{2,1,0:T(8,128)(2,1)}, s32[]{:T(128)}) %tuple.108), condition=%wide.while_cond, body=%wide.while_body.sunk | while | flops 2 | bytes 245337 | solution.py:77
  586.6 4.6 convolution_add_fusion.2
  591.3 71.9 %while.41 = (s32[]{:T(128)}, bf16[50,18432]{1,0:T(8,128)(2,1)S(1)}, s32[36,2]{0,1:T(2,128)S(1)}, bf16[36,50,1152]{2,1,0:T(8,128)(2,1)}, s32[]{:T(128)}) while((s32[]{:T(128)}, bf16[50,18432]{1,0:T(8,128)(2,1)S(1)}, s32[36,2]{0,1:T(2,128)S(1)}, bf16[36,50,1152]{2,1,0:T(8,128)(2,1)}, s32[]{:T(128)}) %tuple.108), condition=%wide.while_cond, body=%wide.while_body.sunk | while | flops 2 | bytes 245337 | solution.py:77
  663.1 4.6 convolution_add_fusion.2
  669.0 3.3 all-to-all-start.3
  674.3 4.5 all-to-all-done.3
  678.7 3.3 all-to-all-start.2
  683.0 5.4 all-to-all-done.2
  689.3 11.4 all-reduce.2
  701.1 614.8 %while.37 = (s32[]{:T(128)}, f32[50,9216]{1,0:T(8,128)S(1)}, bf16[16,18432]{1,0:T(8,128)(2,1)}, bf16[16,36,50]{2,0,1:T(8,128)(2,1)S(1)}, s32[]{:T(128)}, /*index=5*/s32[]{:T(128)}, s32[]{:T(128)}, s32[]{:T(128)}, s32[]{:T(128)}) while((s32[]{:T(128)}, f32[50,9216]{1,0:T(8,128)S(1)}, bf16[16,18432]{1,0:T(8,128)(2,1)}, ...), condition=%wide.region_13.14_spmd.clone, body=%wide.region_12.13_spmd.clone.sunk | while | flops 66355388 | bytes 1807208 | solution.py:131
  701.1 76.4 %while.40 = (s32[]{:T(128)}, bf16[16,18432]{1,0:T(8,128)(2,1)}, s32[36,2]{0,1:T(2,128)S(1)}, bf16[36,16,1152]{2,1,0:T(8,128)(2,1)S(1)}, s32[]{:T(128)}) while((s32[]{:T(128)}, bf16[16,18432]{1,0:T(8,128)(2,1)}, s32[36,2]{0,1:T(2,128)S(1)}, bf16[36,16,1152]{2,1,0:T(8,128)(2,1)S(1)}, s32[]{:T(128)}) %tuple.111), condition=%wide.while_cond.1, body=%wide.while_body.1.sunk | while | flops 2 | bytes 73825 | solution.py:122
  701.7 1.5 bitcast_dynamic-update-slice_fusion.5
  710.2 1.5 bitcast_dynamic-update-slice_fusion.5
  733.6 1.5 bitcast_dynamic-update-slice_fusion.5
  742.1 1.5 bitcast_dynamic-update-slice_fusion.5
  750.5 1.5 bitcast_dynamic-update-slice_fusion.5
  773.9 1.5 bitcast_dynamic-update-slice_fusion.5
  778.0 76.4 %while.40 = (s32[]{:T(128)}, bf16[16,18432]{1,0:T(8,128)(2,1)}, s32[36,2]{0,1:T(2,128)S(1)}, bf16[36,16,1152]{2,1,0:T(8,128)(2,1)S(1)}, s32[]{:T(128)}) while((s32[]{:T(128)}, bf16[16,18432]{1,0:T(8,128)(2,1)}, s32[36,2]{0,1:T(2,128)S(1)}, bf16[36,16,1152]{2,1,0:T(8,128)(2,1)S(1)}, s32[]{:T(128)}) %tuple.111), condition=%wide.while_cond.1, body=%wide.while_body.1.sunk | while | flops 2 | bytes 73825 | solution.py:122
  789.2 1.5 bitcast_dynamic-update-slice_fusion.5
  854.8 76.4 %while.40 = (s32[]{:T(128)}, bf16[16,18432]{1,0:T(8,128)(2,1)}, s32[36,2]{0,1:T(2,128)S(1)}, bf16[36,16,1152]{2,1,0:T(8,128)(2,1)S(1)}, s32[]{:T(128)}) while((s32[]{:T(128)}, bf16[16,18432]{1,0:T(8,128)(2,1)}, s32[36,2]{0,1:T(2,128)S(1)}, bf16[36,16,1152]{2,1,0:T(8,128)(2,1)S(1)}, s32[]{:T(128)}) %tuple.111), condition=%wide.while_cond.1, body=%wide.while_body.1.sunk | while | flops 2 | bytes 73825 | solution.py:122
  931.7 76.4 %while.40 = (s32[]{:T(128)}, bf16[16,18432]{1,0:T(8,128)(2,1)}, s32[36,2]{0,1:T(2,128)S(1)}, bf16[36,16,1152]{2,1,0:T(8,128)(2,1)S(1)}, s32[]{:T(128)}) while((s32[]{:T(128)}, bf16[16,18432]{1,0:T(8,128)(2,1)}, s32[36,2]{0,1:T(2,128)S(1)}, bf16[36,16,1152]{2,1,0:T(8,128)(2,1)S(1)}, s32[]{:T(128)}) %tuple.111), condition=%wide.while_cond.1, body=%wide.while_body.1.sunk | while | flops 2 | bytes 73825 | solution.py:122
  1008.5 76.4 %while.40 = (s32[]{:T(128)}, bf16[16,18432]{1,0:T(8,128)(2,1)}, s32[36,2]{0,1:T(2,128)S(1)}, bf16[36,16,1152]{2,1,0:T(8,128)(2,1)S(1)}, s32[]{:T(128)}) while((s32[]{:T(128)}, bf16[16,18432]{1,0:T(8,128)(2,1)}, s32[36,2]{0,1:T(2,128)S(1)}, bf16[36,16,1152]{2,1,0:T(8,128)(2,1)S(1)}, s32[]{:T(128)}) %tuple.111), condition=%wide.while_cond.1, body=%wide.while_body.1.sunk | while | flops 2 | bytes 73825 | solution.py:122
  1085.4 76.4 %while.40 = (s32[]{:T(128)}, bf16[16,18432]{1,0:T(8,128)(2,1)}, s32[36,2]{0,1:T(2,128)S(1)}, bf16[36,16,1152]{2,1,0:T(8,128)(2,1)S(1)}, s32[]{:T(128)}) while((s32[]{:T(128)}, bf16[16,18432]{1,0:T(8,128)(2,1)}, s32[36,2]{0,1:T(2,128)S(1)}, bf16[36,16,1152]{2,1,0:T(8,128)(2,1)S(1)}, s32[]{:T(128)}) %tuple.111), condition=%wide.while_cond.1, body=%wide.while_body.1.sunk | while | flops 2 | bytes 73825 | solution.py:122
  1162.2 76.4 %while.40 = (s32[]{:T(128)}, bf16[16,18432]{1,0:T(8,128)(2,1)}, s32[36,2]{0,1:T(2,128)S(1)}, bf16[36,16,1152]{2,1,0:T(8,128)(2,1)S(1)}, s32[]{:T(128)}) while((s32[]{:T(128)}, bf16[16,18432]{1,0:T(8,128)(2,1)}, s32[36,2]{0,1:T(2,128)S(1)}, bf16[36,16,1152]{2,1,0:T(8,128)(2,1)S(1)}, s32[]{:T(128)}) %tuple.111), condition=%wide.while_cond.1, body=%wide.while_body.1.sunk | while | flops 2 | bytes 73825 | solution.py:122
  1239.1 76.4 %while.40 = (s32[]{:T(128)}, bf16[16,18432]{1,0:T(8,128)(2,1)}, s32[36,2]{0,1:T(2,128)S(1)}, bf16[36,16,1152]{2,1,0:T(8,128)(2,1)S(1)}, s32[]{:T(128)}) while((s32[]{:T(128)}, bf16[16,18432]{1,0:T(8,128)(2,1)}, s32[36,2]{0,1:T(2,128)S(1)}, bf16[36,16,1152]{2,1,0:T(8,128)(2,1)S(1)}, s32[]{:T(128)}) %tuple.111), condition=%wide.while_cond.1, body=%wide.while_body.1.sunk | while | flops 2 | bytes 73825 | solution.py:122
  1315.9 3.4 copy.77
  1319.5 259.2 %psum.7 = f32[50,64]{1,0:T(8,128)} all-reduce(f32[50,64]{1,0:T(8,128)S(1)} %fusion.19), channel_id=1, replica_groups=mesh['dom'=64,'cls'=8] {'dom'}, use_global_device_ids=true, to_apply=%region_16.17 | all-reduce | flops 3200 | bytes 25600 | tf_op jit(solution)/shard_map/psum | solution.py:116
  1578.7 1.6 copy.78
  (1843 shorter events, 1183.8 us)
Async XLA Ops:
  7.2 24.0 %copy-start = (bf16[50,9216]{1,0:T(8,128)(2,1)S(1)}, bf16[50,9216]{1,0:T(8,128)(2,1)}, u32[]{:S(2)}) copy-start(bf16[50,9216]{1,0:T(8,128)(2,1)} %param.12) | copy-start | bytes 2764804
  23.6 15.6 all-to-all-start.1
  31.1 0.9 copy-start.1
  39.2 16.3 %all-to-all-start = ((bf16[8,2,9216]{2,1,0:T(2,128)(2,1)}), bf16[8,2,9216]{2,1,0:T(2,128)(2,1)S(1)}, u32[]{:S(2)}, u32[]{:S(2)}) async-start(bf16[8,2,9216]{2,1,0:T(2,128)(2,1)} %all_to_all.28), calls=%async_computation | async-start | bytes 589824 | tf_op jit(solution)/shard_map/all_to_all | solution.py:53
  669.0 9.7 all-to-all-start.3
  678.7 9.7 all-to-all-start.2
  682.0 896.7 %reduce-scatter.4.cloned.1.call-start = ((), (), s32[]{:S(2)}) async-start(), calls=%async_computation.5 | async-start | bytes 4792320
Sparse Core Ops, SparseCore 0:
  1319.5 161.8 reduce-scatter.3
where the time goes:
time: 1620 us; the launch traced here: 1590 us
  local copies, waits for them, and re-layouts  1190 us (73%)
  blocking collectives  285 us (18%)
  matrix products  42.2 us (3%)
  waiting for transfers between devices  19.2 us (1%)
  starting transfers between devices  17.4 us (1%)
    gather x1728, local copies, waits for them, and re-layouts  1180 us
    psum x1, blocking collectives, shards(): weight_sums = lax.psum(ctf_part, 'dom')  259 us
    dot_general x8, matrix products, add_block(): lax.dot_general(section, rotated, (((1,), (2,)), ((), ())), preferred_ele...  36.8 us
  transfers between devices with their start and end apart: 5, of which 3 were waited for; matrix products, arithmetic and copies ran while one was open for 1% of the time, Pallas kernels for 0%

commit v1 on v0

v1 whole, which is shorter than its diff:
```python
import jax
import jax.numpy as jnp
from jax import lax
from jax.experimental import pallas as pl
from jax.experimental.pallas import tpu as pltpu
from jax.sharding import Mesh, PartitionSpec as P

CYCLES = 64
ROTATIONS = 36
BLOCK = 256
FEATURES = ROTATIONS * BLOCK
LANES = 128
HALF = 64
ROWS = 16
GROUPS = 64
SLICE = FEATURES // GROUPS
CHUNKS = SLICE // 16
PAY_ROWS = SLICE // 2
NEGATIVE = -1e30
P_LANE = 120
F32 = jnp.float32
BF16 = jnp.bfloat16
HIGH = lax.Precision.HIGHEST


def lanes_of(shape):
    return lax.broadcasted_iota(jnp.int32, shape, len(shape) - 1)


def rows_of(shape):
    return lax.broadcasted_iota(jnp.int32, shape, len(shape) - 2)


def call(body, outs, *args):
    return pl.pallas_call(
        body,
        out_shape=outs,
        compiler_params=pltpu.CompilerParams(vmem_limit_bytes=48 * 1024 * 1024),
    )(*args)


def pack_body(class_block, images_ref, ctf_ref, noise_ref, cands_ref, out_ref):
    part = images_ref.shape[0]
    ctf = ctf_ref[...]
    noise = noise_ref[...]
    ctf_noise = ctf * noise
    factor = jnp.concatenate([ctf_noise, ctf_noise], axis=1)
    quad = (ctf * ctf * noise).astype(BF16)
    quad = jnp.concatenate([quad, quad], axis=1)
    cands = cands_ref[...]
    first = jnp.broadcast_to(cands[0:1, :], (ROWS, part))
    second = jnp.broadcast_to(cands[1:2, :], (ROWS, part))
    row = rows_of((ROWS, part))
    low = (row // 2) * class_block
    hit = ((first >= low) & (first < low + class_block)) | (
        (second >= low) & (second < low + class_block)
    )
    hit = hit.astype(F32)
    taken = jnp.zeros((ROWS, 1), F32)
    columns = []
    slot = (rows_of((ROWS, 1)) % 2).astype(F32)
    for p in range(part):
        now = hit[:, p : p + 1]
        columns.append(now * (taken == slot).astype(F32))
        taken = taken + now
    packing = jnp.concatenate(columns, axis=1)
    valid = jnp.sum(packing, axis=1, keepdims=True)
    own = jnp.sum(packing * lanes_of((ROWS, part)).astype(F32), axis=1, keepdims=True)
    base = low[:, 0:1].astype(F32)
    id_a = jnp.sum(packing * first.astype(F32), axis=1, keepdims=True) - base
    id_b = jnp.sum(packing * second.astype(F32), axis=1, keepdims=True) - base
    lane = lanes_of((ROWS, LANES))
    klane = (lane - HALF).astype(F32)
    in_block = (lane >= HALF) & (lane < HALF + class_block)
    flags = (in_block & ((klane == id_a) | (klane == id_b))) | (
        (lane - P_LANE).astype(F32) == own
    )
    flags = flags.astype(F32) * (valid > 0.5).astype(F32)
    packing = packing.astype(BF16)
    quad_rows = jnp.dot(packing, quad, preferred_element_type=F32)
    out_ref[:, FEATURES : FEATURES + LANES] = jnp.where(lane < HALF, quad_rows, flags).astype(BF16)
    wide = jnp.concatenate([factor] * 4, axis=1)
    step = 4 * LANES
    for t in range(FEATURES // step):
        part_w = (images_ref[:, t * step : (t + 1) * step].astype(F32) * wide).astype(BF16)
        out_ref[:, t * step : (t + 1) * step] = jnp.dot(
            packing, part_w, preferred_element_type=F32
        ).astype(BF16)


def prep_body(classes_ref, table_ref, energy_ref):
    count = classes_ref.shape[0]
    acc = jnp.zeros((count, LANES), F32)
    for b in range(ROTATIONS):
        block = classes_ref[:, b * BLOCK : (b + 1) * BLOCK]
        table_ref[b * HALF : b * HALF + count, :] = block
        table_ref[b * HALF + count : (b + 1) * HALF, :] = jnp.zeros((HALF - count, BLOCK), BF16)
        wide = block.astype(F32)
        square = wide * wide
        acc = acc + square[:, :LANES] + square[:, LANES:]
    acc = acc + pltpu.roll(acc, HALF, 1)
    energy_ref[...] = jnp.zeros((LANES, LANES), F32)
    energy_ref[0:count, :] = acc
    energy_ref[HALF : HALF + count, :] = acc


def row_facts(meta):
    lane = lanes_of(meta.shape)
    flags = jnp.where((lane >= HALF) & (lane < P_LANE), meta, 0.0)
    live = (flags + pltpu.roll(flags, HALF, 1)) > 0.5
    marks = jnp.where(lane >= P_LANE, meta, 0.0)
    valid = jnp.sum(marks, axis=1, keepdims=True)
    own = jnp.sum(marks * (lane - P_LANE).astype(F32), axis=1, keepdims=True)
    source = (rows_of(meta.shape) // 2 * 4).astype(F32)
    spot = (lane.astype(F32) == source + own) & (valid > 0.5)
    return live, spot


def cross_body(rows_ref, table_ref, energy_ref, logits_ref, stats_ref, blocks_ref, acc_ref):
    total_rows = ROTATIONS * ROWS
    for b in range(ROTATIONS):
        blocks_ref[b * ROWS : (b + 1) * ROWS, :] = rows_ref[:, b * BLOCK : (b + 1) * BLOCK]
    for m in range(ROTATIONS // 4):
        g = lax.dot_general(
            blocks_ref[...],
            table_ref[m * BLOCK : (m + 1) * BLOCK, :],
            (((1,), (1,)), ((), ())),
            preferred_element_type=F32,
        )
        for h in range(2):
            tile = g[:, h * LANES : (h + 1) * LANES]
            shift = (2 * m + h) * 2 * ROWS
            if shift == 0:
                acc_ref[...] = tile
            else:
                acc_ref[0 : total_rows - shift, :] += tile[shift:, :]
                acc_ref[total_rows - shift :, :] += tile[:shift, :]
    meta = rows_ref[:, FEATURES : FEATURES + LANES].astype(F32)
    lane = lanes_of((ROWS, LANES))
    live, spot = row_facts(meta)
    quad = jnp.where(lane < HALF, meta, 0.0)
    norm = 0.5 * lax.dot_general(
        quad, energy_ref[...], (((1,), (1,)), ((), ())), precision=HIGH, preferred_element_type=F32
    )
    left = live & (lane < HALF)
    best = jnp.full((ROWS, LANES), NEGATIVE, F32)
    for r in range(ROTATIONS):
        nxt = (r + 1) % ROTATIONS
        mixed = jnp.where(
            lane < HALF,
            acc_ref[r * ROWS : (r + 1) * ROWS, :],
            acc_ref[nxt * ROWS : (nxt + 1) * ROWS, :],
        )
        value = mixed + pltpu.roll(mixed, HALF, 1) - norm
        logits_ref[r * ROWS : (r + 1) * ROWS, :] = value
        best = jnp.maximum(best, jnp.where(left, value, NEGATIVE))
    peak = jnp.max(best, axis=1, keepdims=True)
    total = jnp.zeros((ROWS, LANES), F32)
    for r in range(ROTATIONS):
        value = logits_ref[r * ROWS : (r + 1) * ROWS, :]
        total = total + jnp.where(left, jnp.exp(value - peak), 0.0)
    total = jnp.sum(total, axis=1, keepdims=True)
    stats_ref[0:1, :] = jnp.max(jnp.where(spot, peak, NEGATIVE), axis=0, keepdims=True)
    stats_ref[1:2, :] = jnp.sum(jnp.where(spot, total, 0.0), axis=0, keepdims=True)


def turn_body(blocks_ref, out_ref):
    out_ref[...] = blocks_ref[...].astype(F32).T.astype(BF16)


def sums_body(stats_ref, logits_ref, meta_ref, turned_ref, pay_ref, evid_ref, left_ref, right_ref):
    total_rows = ROTATIONS * ROWS
    peaks = stats_ref[:, 0, :]
    totals = stats_ref[:, 1, :]
    highest = jnp.max(peaks, axis=0, keepdims=True)
    total = jnp.sum(totals * jnp.exp(peaks - highest), axis=0, keepdims=True)
    evidence = highest + jnp.log(total)
    evid_ref[...] = evidence
    meta = meta_ref[...].astype(F32)
    live, spot = row_facts(meta)
    lane = lanes_of((ROWS, LANES))
    row_evidence = jnp.sum(jnp.where(spot, evidence, 0.0), axis=1, keepdims=True)
    weight = jnp.zeros((ROWS, LANES), F32)
    for r in range(ROTATIONS):
        value = logits_ref[r * ROWS : (r + 1) * ROWS, :]
        post = jnp.where(live, jnp.exp(value - row_evidence), 0.0).astype(BF16).astype(F32)
        weight = weight + post
        one = jnp.where(lane < HALF, post, 0.0).astype(BF16)
        two = jnp.where(lane < HALF, 0.0, post).astype(BF16)
        left_ref[r * ROWS : (r + 1) * ROWS, :] = one
        left_ref[total_rows + r * ROWS : total_rows + (r + 1) * ROWS, :] = one
        right_ref[r * ROWS : (r + 1) * ROWS, :] = two
        right_ref[total_rows + r * ROWS : total_rows + (r + 1) * ROWS, :] = two
    quad = jnp.where(lane < HALF, meta, 0.0)
    quad = quad + pltpu.roll(quad, HALF, 1)
    filters = jnp.dot(weight.T, quad, precision=HIGH, preferred_element_type=F32)
    pair = jnp.where(lanes_of((32, LANES)) < HALF, filters[0:32, :], filters[32:64, :]).astype(BF16)
    base = GROUPS // 2 * PAY_ROWS
    pay_ref[0, base : base + 32, :] = pair
    pay_ref[1, base : base + 32, :] = pair

    def turned_posterior(b):
        start = (ROTATIONS - b) * ROWS
        return (
            left_ref[start : start + total_rows, :]
            + right_ref[start - ROWS : start - ROWS + total_rows, :]
        )

    for m in range(ROTATIONS // 4):
        mixed = jnp.concatenate([turned_posterior(4 * m), turned_posterior(4 * m + 2)], axis=1)
        out = jnp.dot(turned_ref[...], mixed, preferred_element_type=F32).astype(BF16)
        for e in range(4):
            for i in range(16):
                q = (4 * m + e) * 16 + i
                group, j = q // CHUNKS, q % CHUNKS
                core, spot_at = group % 2, group // 2 * PAY_ROWS
                piece = out[i * 16 : (i + 1) * 16, e * HALF : (e + 1) * HALF]
                if j < CHUNKS - 1:
                    at = spot_at + j // 2 * 16
                    lo = j % 2 * HALF
                    pay_ref[core, at : at + 16, lo : lo + HALF] = piece
                else:
                    at = spot_at + PAY_ROWS - 8
                    pay_ref[core, at : at + 8, 0:HALF] = piece[0:8, :]
                    pay_ref[core, at : at + 8, HALF:LANES] = piece[8:16, :]


def combine_body(pay_ref, out_ref):
    half = GROUPS // 2
    base = half * PAY_ROWS
    weights = (pay_ref[0, base : base + 32, :].astype(F32) + pay_ref[1, base : base + 32, :].astype(F32)).astype(BF16)
    for g in range(half):
        at = g * PAY_ROWS
        out_ref[g, 0:PAY_ROWS, :] = (
            pay_ref[0, at : at + PAY_ROWS, :].astype(F32) + pay_ref[1, at : at + PAY_ROWS, :].astype(F32)
        ).astype(BF16)
        out_ref[g, PAY_ROWS : PAY_ROWS + 32, :] = weights


def final_body(parts_ref, sums_ref, weights_ref):
    count = weights_ref.shape[0]
    acc = parts_ref[0, :, :].astype(F32)
    for g in range(1, GROUPS // 2):
        acc = acc + parts_ref[g, :, :].astype(F32)
    pieces = []
    for j in range(CHUNKS - 1):
        lo = j % 2 * HALF
        pieces.append(acc[j // 2 * 16 : j // 2 * 16 + 16, lo : lo + HALF])
    pieces.append(acc[PAY_ROWS - 8 : PAY_ROWS, 0:HALF])
    pieces.append(acc[PAY_ROWS - 8 : PAY_ROWS, HALF:LANES])
    full = jnp.concatenate(pieces, axis=0)
    sums_ref[...] = full.T[0:count, :]
    weights_ref[0:32, :] = acc[PAY_ROWS : PAY_ROWS + 32, 0:HALF]
    weights_ref[32:count, :] = acc[PAY_ROWS : PAY_ROWS + count - 32, HALF:LANES]


def shards(images, ctf, inv_noise, classes, candidates):
    class_block = classes.shape[0]
    my_index = lax.axis_index("cls")
    total_rows = ROTATIONS * ROWS
    width = FEATURES + LANES
    shape = jax.ShapeDtypeStruct

    def swap(value, axes):
        return lax.all_to_all(value, axes, split_axis=0, concat_axis=0, tiled=True)

    def pack(*refs):
        pack_body(class_block, *refs)

    packed = call(
        pack, shape((ROWS, width), BF16), images, ctf, inv_noise.reshape(1, CYCLES), candidates.T
    )
    rows = swap(packed.reshape(8, 2, width), "cls").reshape(ROWS, width)
    table, energy = call(
        prep_body,
        (shape((ROTATIONS * HALF, BLOCK), BF16), shape((LANES, LANES), F32)),
        classes,
    )
    logits, stats, blocks = pl.pallas_call(
        cross_body,
        out_shape=(
            shape((total_rows, LANES), F32),
            shape((2, LANES), F32),
            shape((total_rows, BLOCK), BF16),
        ),
        scratch_shapes=[pltpu.VMEM((total_rows, LANES), F32)],
        compiler_params=pltpu.CompilerParams(vmem_limit_bytes=48 * 1024 * 1024),
    )(rows, table, energy)
    group_stats = swap(jnp.broadcast_to(stats[None], (8, 2, LANES)), "cls")
    turned = call(turn_body, shape((BLOCK, total_rows), BF16), blocks)
    meta = rows[:, FEATURES:]
    pay_total = GROUPS // 2 * PAY_ROWS + 32
    pay, evidence = pl.pallas_call(
        sums_body,
        out_shape=(shape((2, pay_total, LANES), BF16), shape((1, LANES), F32)),
        scratch_shapes=[
            pltpu.VMEM((2 * total_rows, LANES), BF16),
            pltpu.VMEM((2 * total_rows, LANES), BF16),
        ],
        compiler_params=pltpu.CompilerParams(vmem_limit_bytes=48 * 1024 * 1024),
    )(group_stats, logits, meta, turned)
    both = swap(pay, "core")
    merged = call(combine_body, shape((GROUPS // 2, PAY_ROWS + 32, LANES), BF16), both)
    parts = swap(merged, ("x", "z"))
    sums, weight_sums = call(
        final_body, (shape((class_block, SLICE), F32), shape((class_block, CYCLES), F32)), parts
    )
    own = lax.dynamic_slice(evidence.reshape(LANES), (my_index * 4,), (4,))
    return sums.T, weight_sums, own


def solution(mesh):
    fine = Mesh(mesh.devices.reshape(4, 8, 2, 8), ("x", "z", "core", "cls"))
    dom = ("x", "z", "core")
    every = dom + ("cls",)
    in_specs = (P(every, None), P(every, None), P(), P("cls", None), P(every, None))
    out_specs = (P(dom, "cls"), P("cls", None), P(every))
    return jax.shard_map(shards, mesh=fine, in_specs=in_specs, out_specs=out_specs, check_vma=False)
```

time: 1620 us -> 83.5 us (0.05)
  the two profiles are of different devices: /device:TPU:1 before, /device:TPU:64 now
where the time goes in v1:
time: 83.5 us; the launch traced here: 83.1 us
  waiting for transfers between devices  44 us (53%)
  starting transfers between devices  23 us (28%)
  Pallas kernels  5.62 us (7%)
  local copies, waits for them, and re-layouts  5.11 us (6%)
  blocking collectives  4.67 us (6%)
    all_to_all x3, waiting for transfers between devices, swap(): return lax.all_to_all(value, axes, split_axis=0, concat_axis=0, tiled=True)  44 us
    all_to_all x3, starting transfers between devices, swap(): return lax.all_to_all(value, axes, split_axis=0, concat_axis=0, tiled=True)  23 us
    all_to_all x1, blocking collectives, swap(): return lax.all_to_all(value, axes, split_axis=0, concat_axis=0, tiled=True)  4.67 us
    unnamed x10, local copies, waits for them, and re-layouts  2.98 us
    pallas_call x5, Pallas kernels, call(): pl.pallas_call(body, out_shape=outs, compiler_params=pltpu.CompilerParams...  2.77 us
  transfers between devices with their start and end apart: 3, of which 3 were waited for; matrix products, arithmetic and copies ran while one was open for 1% of the time, Pallas kernels for 1%

profile of v1, /device:TPU:64, one launch (start us, length us, event | category | flops | bytes accessed | tf_op | source)
XLA Modules:
  0.0 83.1 jit_solution(8866513346453055992)
XLA Ops:
  0.6 0.0 copy-start
  0.6 0.0 copy-start.1
  0.7 1.0 %copy-done.1 = bf16[4,9216]{1,0:T(4,128)(2,1)S(1)} copy-done((bf16[4,9216]{1,0:T(4,128)(2,1)S(1)}, bf16[4,9216]{1,0:T(4,128)(2,1)}, u32[]{:S(2)}) %copy-start.1) | copy-done | bytes 73752
  1.6 0.0 copy-start.2
  1.6 0.7 copy-done.2
  2.3 0.0 copy-start.3
  2.3 0.7 copy-done.3
  3.0 0.0 copy-start.4
  3.0 0.7 copy-done.4
  3.6 0.4 shard_map.76
  4.0 0.8 reshape.19
  4.8 7.1 %all-to-all-start = ((bf16[8,2,9344]{2,1,0:T(2,128)(2,1)}), bf16[8,2,9344]{2,1,0:T(2,128)(2,1)S(1)}, u32[]{:S(2)}, u32[]{:S(2)}) async-start(bf16[8,2,9344]{2,1,0:T(2,128)(2,1)} %reshape.19), calls=%async_computation | async-start | bytes 598016 | tf_op jit(solution)/shard_map/all_to_all | solution.py:265
  11.9 0.0 copy-done
  11.9 0.3 shard_map.77
  12.3 12.3 %all-to-all-done = bf16[8,2,9344]{2,1,0:T(2,128)(2,1)S(1)} async-done(((bf16[8,2,9344]{2,1,0:T(2,128)(2,1)}), bf16[8,2,9344]{2,1,0:T(2,128)(2,1)S(1)}, u32[]{:S(2)}, u32[]{:S(2)}) %all-to-all-start) | async-done | bytes 299040 | tf_op jit(solution)/shard_map/all_to_all | solution.py:265
  24.6 0.1 reshape.20.rows_ref
  24.7 1.3 %shard_map.78 = (f32[576,128]{1,0:T(8,128)S(1)}, f32[2,128]{1,0:T(2,128)S(1)}, bf16[576,256]{1,0:T(8,128)(2,1)S(1)}) custom-call(bf16[16,9344]{1,0:T(8,128)(2,1)S(1)} %reshape.20.rows_ref, bf16[2304,256]{1,0:T(8,128)(2,1)S(1)} %get-tuple-element.12.table_ref, f32[128,128]{1,0:T(8,128)S(1)} %get-tuple-element.13.energy_ref), custom_call_target="tpu_custom_call" | custom-call | tf_op jit(solution)/shard_map/pallas_call | solution.py:279
  26.0 0.6 broadcast_in_dim.2
  26.6 3.3 %all-to-all-start.1 = ((f32[8,2,128]{2,1,0:T(2,128)}), f32[8,2,128]{2,1,0:T(2,128)S(1)}, u32[]{:S(2)}, u32[]{:S(2)}) async-start(f32[8,2,128]{2,1,0:T(2,128)} %broadcast_in_dim.2), calls=%async_computation.1 | async-start | bytes 16384 | tf_op jit(solution)/shard_map/all_to_all | solution.py:265
  30.0 0.2 shard_map.79.turned_ref
  30.1 7.5 %all-to-all-done.1.stats_ref = f32[8,2,128]{2,1,0:T(2,128)S(1)} async-done(((f32[8,2,128]{2,1,0:T(2,128)}), f32[8,2,128]{2,1,0:T(2,128)S(1)}, u32[]{:S(2)}, u32[]{:S(2)}) %all-to-all-start.1) | async-done | bytes 8224 | tf_op jit(solution)/shard_map/all_to_all | solution.py:265
  37.6 1.5 %shard_map.80 = (bf16[2,2336,128]{2,1,0:T(8,128)(2,1)S(1)}, f32[1,128]{1,0:T(1,128)S(1)}) custom-call(f32[8,2,128]{2,1,0:T(2,128)S(1)} %all-to-all-done.1.stats_ref, f32[576,128]{1,0:T(8,128)S(1)} %get-tuple-element.15.logits_ref, bf16[16,128]{1,0:T(8,128)(2,1)S(1)} %slice.4.meta_ref, bf16[256,576]{1,0:T(8,128)(2,1)S(1)} %shard_map.79.turned_ref), custom_call_target="tpu_custom_call" | custom-call | tf_op jit(solution)/shard_map/pallas_call | solution.py:293
  39.2 4.7 %all_to_all.20.pay_ref = bf16[2,2336,128]{2,1,0:T(8,128)(2,1)S(1)} all-to-all(bf16[2,2336,128]{2,1,0:T(8,128)(2,1)S(1)} %get-tuple-element.17), channel_id=1, replica_groups=mesh['x'=4,'z'=8,'core'=2,'cls'=8] {'core'}, dimensions={0} | all-to-all | bytes 2392064 | tf_op jit(solution)/shard_map/all_to_all | solution.py:265
  43.8 1.1 %shard_map.81 = bf16[32,104,128]{2,1,0:T(8,128)(2,1)} custom-call(bf16[2,2336,128]{2,1,0:T(8,128)(2,1)S(1)} %all_to_all.20.pay_ref), custom_call_target="tpu_custom_call" | custom-call | tf_op jit(solution)/shard_map/pallas_call | solution.py:35
  44.9 12.6 %all-to-all-start.3 = ((bf16[32,104,128]{2,1,0:T(8,128)(2,1)}), bf16[32,104,128]{2,1,0:T(8,128)(2,1)S(1)}, u32[]{:S(2)}, u32[]{:S(2)}) async-start(bf16[32,104,128]{2,1,0:T(8,128)(2,1)} %shard_map.81), calls=%async_computation.3 | async-start | bytes 1703936 | tf_op jit(solution)/shard_map/all_to_all | solution.py:265
  57.5 0.6 dynamic-slice_bitcast_fusion
  58.1 24.2 %all-to-all-done.3.parts_ref = bf16[32,104,128]{2,1,0:T(8,128)(2,1)S(1)} async-done(((bf16[32,104,128]{2,1,0:T(8,128)(2,1)}), bf16[32,104,128]{2,1,0:T(8,128)(2,1)S(1)}, u32[]{:S(2)}, u32[]{:S(2)}) %all-to-all-start.3) | async-done | bytes 852000 | tf_op jit(solution)/shard_map/all_to_all | solution.py:265
  82.2 0.8 %shard_map.82 = (f32[50,144]{1,0:T(8,128)}, f32[50,64]{1,0:T(8,128)}) custom-call(bf16[32,104,128]{2,1,0:T(8,128)(2,1)S(1)} %all-to-all-done.3.parts_ref), custom_call_target="tpu_custom_call" | custom-call | tf_op jit(solution)/shard_map/pallas_call | solution.py:35
  (1 shorter events, 0.0 us)
Async XLA Ops:
  0.6 11.3 %copy-start = (bf16[50,9216]{1,0:T(8,128)(2,1)S(1)}, bf16[50,9216]{1,0:T(8,128)(2,1)}, u32[]{:S(2)}) copy-start(bf16[50,9216]{1,0:T(8,128)(2,1)} %classes_ref.1) | copy-start | bytes 2764804
  0.6 1.0 %copy-start.1 = (bf16[4,9216]{1,0:T(4,128)(2,1)S(1)}, bf16[4,9216]{1,0:T(4,128)(2,1)}, u32[]{:S(2)}) copy-start(bf16[4,9216]{1,0:T(4,128)(2,1)} %refs_0_.1) | copy-start | bytes 221188
  1.6 0.7 copy-start.2
  2.3 0.7 copy-start.3
  3.0 0.7 copy-start.4
  4.8 19.8 %all-to-all-start = ((bf16[8,2,9344]{2,1,0:T(2,128)(2,1)}), bf16[8,2,9344]{2,1,0:T(2,128)(2,1)S(1)}, u32[]{:S(2)}, u32[]{:S(2)}) async-start(bf16[8,2,9344]{2,1,0:T(2,128)(2,1)} %reshape.19), calls=%async_computation | async-start | bytes 598016 | tf_op jit(solution)/shard_map/all_to_all | solution.py:265
  26.6 11.0 %all-to-all-start.1 = ((f32[8,2,128]{2,1,0:T(2,128)}), f32[8,2,128]{2,1,0:T(2,128)S(1)}, u32[]{:S(2)}, u32[]{:S(2)}) async-start(f32[8,2,128]{2,1,0:T(2,128)} %broadcast_in_dim.2), calls=%async_computation.1 | async-start | bytes 16384 | tf_op jit(solution)/shard_map/all_to_all | solution.py:265
  44.9 37.3 %all-to-all-start.3 = ((bf16[32,104,128]{2,1,0:T(8,128)(2,1)}), bf16[32,104,128]{2,1,0:T(8,128)(2,1)S(1)}, u32[]{:S(2)}, u32[]{:S(2)}) async-start(bf16[32,104,128]{2,1,0:T(8,128)(2,1)} %shard_map.81), calls=%async_computation.3 | async-start | bytes 1703936 | tf_op jit(solution)/shard_map/all_to_all | solution.py:265

commit v2 on v1

v2 whole, which is shorter than its diff:
```python
import jax
import jax.numpy as jnp
from jax import lax
from jax.experimental import pallas as pl
from jax.experimental.pallas import tpu as pltpu
from jax.sharding import Mesh, PartitionSpec as P

CYCLES = 64
ROTATIONS = 36
BLOCK = 256
FEATURES = ROTATIONS * BLOCK
LANES = 128
HALF = 64
ROWS = 16
GROUPS = 64
CLASSES = 50
SLICE = FEATURES // GROUPS
CHUNKS = SLICE // 16
PAY_ROWS = SLICE // 2
NEGATIVE = -1e30
P_LANE = 120
F32 = jnp.float32
BF16 = jnp.bfloat16
HIGH = lax.Precision.HIGHEST


def lanes_of(shape):
    return lax.broadcasted_iota(jnp.int32, shape, len(shape) - 1)


def rows_of(shape):
    return lax.broadcasted_iota(jnp.int32, shape, len(shape) - 2)


def call(body, outs, *args, in_specs=None, scratch=(), micros=0):
    more = {} if in_specs is None else {"in_specs": in_specs}
    if micros:
        more["cost_estimate"] = pl.CostEstimate(
            flops=0, transcendentals=0, bytes_accessed=micros * 3_000_000
        )
    return pl.pallas_call(
        body,
        out_shape=outs,
        scratch_shapes=list(scratch),
        compiler_params=pltpu.CompilerParams(vmem_limit_bytes=48 * 1024 * 1024),
        **more,
    )(*args)


def pack_body(class_block, images_any, ctf_any, noise_any, cands_any, out_ref, images_ref, ctf_ref, noise_ref, cands_ref, sems):
    copies = [
        pltpu.make_async_copy(source, target, sems.at[i])
        for i, (source, target) in enumerate(
            (
                (cands_any, cands_ref),
                (ctf_any, ctf_ref),
                (noise_any, noise_ref),
                (images_any, images_ref),
            )
        )
    ]
    for copy in copies:
        copy.start()
    for copy in copies:
        copy.wait()
    part = images_ref.shape[0]
    ctf = ctf_ref[...]
    noise = noise_ref[...]
    ctf_noise = ctf * noise
    factor = jnp.concatenate([ctf_noise, ctf_noise], axis=1)
    quad = (ctf * ctf * noise).astype(BF16)
    quad = jnp.concatenate([quad, quad], axis=1)
    cands = cands_ref[...]
    first = jnp.broadcast_to(cands[0:1, :], (ROWS, part))
    second = jnp.broadcast_to(cands[1:2, :], (ROWS, part))
    row = rows_of((ROWS, part))
    low = (row // 2) * class_block
    hit = ((first >= low) & (first < low + class_block)) | (
        (second >= low) & (second < low + class_block)
    )
    hit = hit.astype(F32)
    taken = jnp.zeros((ROWS, 1), F32)
    columns = []
    slot = (rows_of((ROWS, 1)) % 2).astype(F32)
    for p in range(part):
        now = hit[:, p : p + 1]
        columns.append(now * (taken == slot).astype(F32))
        taken = taken + now
    packing = jnp.concatenate(columns, axis=1)
    valid = jnp.sum(packing, axis=1, keepdims=True)
    own = jnp.sum(packing * lanes_of((ROWS, part)).astype(F32), axis=1, keepdims=True)
    base = low[:, 0:1].astype(F32)
    id_a = jnp.sum(packing * first.astype(F32), axis=1, keepdims=True) - base
    id_b = jnp.sum(packing * second.astype(F32), axis=1, keepdims=True) - base
    lane = lanes_of((ROWS, LANES))
    klane = (lane - HALF).astype(F32)
    in_block = (lane >= HALF) & (lane < HALF + class_block)
    flags = (in_block & ((klane == id_a) | (klane == id_b))) | (
        (lane - P_LANE).astype(F32) == own
    )
    flags = flags.astype(F32) * (valid > 0.5).astype(F32)
    packing = packing.astype(BF16)

    def put(value, start, size):
        value = value.astype(BF16)
        for owner in range(ROWS // 2):
            out_ref[owner, :, start : start + size] = value[2 * owner : 2 * owner + 2, :]

    quad_rows = jnp.dot(packing, quad, preferred_element_type=F32)
    put(jnp.where(lane < HALF, quad_rows, flags), FEATURES, LANES)
    wide = jnp.concatenate([factor] * 4, axis=1)
    step = 4 * LANES
    for t in range(FEATURES // step):
        part_w = (images_ref[:, t * step : (t + 1) * step].astype(F32) * wide).astype(BF16)
        put(jnp.dot(packing, part_w, preferred_element_type=F32), t * step, step)


def prep_body(classes_ref, table_ref, energy_ref):
    count = classes_ref.shape[0]
    acc = jnp.zeros((count, LANES), F32)
    for b in range(ROTATIONS):
        block = classes_ref[:, b * BLOCK : (b + 1) * BLOCK]
        table_ref[b * HALF : b * HALF + count, :] = block
        table_ref[b * HALF + count : (b + 1) * HALF, :] = jnp.zeros((HALF - count, BLOCK), BF16)
        wide = block.astype(F32)
        square = wide * wide
        acc = acc + square[:, :LANES] + square[:, LANES:]
    acc = acc + pltpu.roll(acc, HALF, 1)
    energy_ref[...] = jnp.zeros((LANES, LANES), F32)
    energy_ref[0:count, :] = acc
    energy_ref[HALF : HALF + count, :] = acc


def row_facts(meta):
    lane = lanes_of(meta.shape)
    flags = jnp.where((lane >= HALF) & (lane < P_LANE), meta, 0.0)
    live = (flags + pltpu.roll(flags, HALF, 1)) > 0.5
    marks = jnp.where(lane >= P_LANE, meta, 0.0)
    valid = jnp.sum(marks, axis=1, keepdims=True)
    own = jnp.sum(marks * (lane - P_LANE).astype(F32), axis=1, keepdims=True)
    source = (rows_of(meta.shape) // 2 * 4).astype(F32)
    spot = (lane.astype(F32) == source + own) & (valid > 0.5)
    return live, spot


def cross_body(rows_ref, table_ref, energy_ref, logits_ref, stats_ref, blocks_ref, acc_ref):
    total_rows = ROTATIONS * ROWS
    for b in range(ROTATIONS):
        blocks_ref[b * ROWS : (b + 1) * ROWS, :] = rows_ref[:, b * BLOCK : (b + 1) * BLOCK]
    for m in range(ROTATIONS // 4):
        g = lax.dot_general(
            blocks_ref[0:total_rows, :],
            table_ref[m * BLOCK : (m + 1) * BLOCK, :],
            (((1,), (1,)), ((), ())),
            preferred_element_type=F32,
        )
        for h in range(2):
            tile = g[:, h * LANES : (h + 1) * LANES]
            shift = (2 * m + h) * 2 * ROWS
            if shift == 0:
                acc_ref[...] = tile
            else:
                acc_ref[0 : total_rows - shift, :] += tile[shift:, :]
                acc_ref[total_rows - shift :, :] += tile[:shift, :]
    raw = rows_ref[:, FEATURES : FEATURES + LANES]
    blocks_ref[total_rows:, 0:LANES] = raw
    blocks_ref[total_rows:, LANES:] = jnp.zeros((ROWS, LANES), BF16)
    meta = raw.astype(F32)
    lane = lanes_of((ROWS, LANES))
    live, spot = row_facts(meta)
    quad = jnp.where(lane < HALF, meta, 0.0)
    norm = 0.5 * lax.dot_general(
        quad, energy_ref[...], (((1,), (1,)), ((), ())), precision=HIGH, preferred_element_type=F32
    )
    left = live & (lane < HALF)
    best = jnp.full((ROWS, LANES), NEGATIVE, F32)
    for r in range(ROTATIONS):
        nxt = (r + 1) % ROTATIONS
        mixed = jnp.where(
            lane < HALF,
            acc_ref[r * ROWS : (r + 1) * ROWS, :],
            acc_ref[nxt * ROWS : (nxt + 1) * ROWS, :],
        )
        value = mixed + pltpu.roll(mixed, HALF, 1) - norm
        logits_ref[r * ROWS : (r + 1) * ROWS, :] = value
        best = jnp.maximum(best, jnp.where(left, value, NEGATIVE))
    peak = jnp.max(best, axis=1, keepdims=True)
    total = jnp.zeros((ROWS, LANES), F32)
    for r in range(ROTATIONS):
        value = logits_ref[r * ROWS : (r + 1) * ROWS, :]
        total = total + jnp.where(left, jnp.exp(value - peak), 0.0)
    total = jnp.sum(total, axis=1, keepdims=True)
    peak_row = jnp.max(jnp.where(spot, peak, NEGATIVE), axis=0, keepdims=True)
    total_row = jnp.sum(jnp.where(spot, total, 0.0), axis=0, keepdims=True)
    for d in range(stats_ref.shape[0]):
        stats_ref[d, 0:1, :] = peak_row
        stats_ref[d, 1:2, :] = total_row


def turn_body(core_ref, blocks_ref, logits_ref, mine_ref, theirs_ref, logits_out_ref):
    total_rows = ROTATIONS * ROWS
    second = core_ref[0] == 1
    value = blocks_ref[0:total_rows, :].astype(F32)
    rolled = pltpu.roll(value, BLOCK - SLICE, 1)
    after = jnp.concatenate([rolled[ROWS:, :], rolled[:ROWS, :]], axis=0)
    moved = jnp.where(lanes_of(value.shape) < BLOCK - SLICE, rolled, after)
    mine_ref[...] = jnp.where(second, moved, value).T.astype(BF16)
    theirs_ref[0:BLOCK, :] = jnp.where(second, value, moved).T.astype(BF16)
    theirs_ref[BLOCK:, 0:LANES] = blocks_ref[total_rows:, 0:LANES]
    theirs_ref[BLOCK:, LANES:] = jnp.zeros((ROWS, total_rows - LANES), BF16)
    logits_out_ref[...] = logits_ref[...]


def sums_body(
    core_ref,
    stats_ref,
    mine_logits_ref,
    sibling_logits_ref,
    mine_meta_ref,
    sibling_meta_ref,
    mine_turned_ref,
    sibling_turned_ref,
    pay_ref,
    evid_ref,
    *tables,
):
    total_rows = ROTATIONS * ROWS
    core = core_ref[0]
    lane = lanes_of((ROWS, LANES))
    weights, quads = [], []
    for g, (logits_ref, meta_ref) in enumerate(
        ((mine_logits_ref, mine_meta_ref), (sibling_logits_ref, sibling_meta_ref))
    ):
        left_ref, right_ref = tables[2 * g], tables[2 * g + 1]
        place = (core if g == 0 else 1 - core) * 8
        stats = stats_ref[pl.ds(place, 8), :, :]
        peaks = stats[:, 0, :]
        totals = stats[:, 1, :]
        highest = jnp.max(peaks, axis=0, keepdims=True)
        total = jnp.sum(totals * jnp.exp(peaks - highest), axis=0, keepdims=True)
        evidence = highest + jnp.log(total)
        if g == 0:
            evid_ref[...] = evidence
        meta = meta_ref[...].astype(F32)
        live, spot = row_facts(meta)
        row_evidence = jnp.sum(jnp.where(spot, evidence, 0.0), axis=1, keepdims=True)
        weight = jnp.zeros((ROWS, LANES), F32)
        for r in range(ROTATIONS):
            value = logits_ref[r * ROWS : (r + 1) * ROWS, :]
            post = jnp.where(live, jnp.exp(value - row_evidence), 0.0).astype(BF16).astype(F32)
            weight = weight + post
            one = jnp.where(lane < HALF, post, 0.0).astype(BF16)
            two = jnp.where(lane < HALF, 0.0, post).astype(BF16)
            left_ref[r * ROWS : (r + 1) * ROWS, :] = one
            left_ref[total_rows + r * ROWS : total_rows + (r + 1) * ROWS, :] = one
            right_ref[r * ROWS : (r + 1) * ROWS, :] = two
            right_ref[total_rows + r * ROWS : total_rows + (r + 1) * ROWS, :] = two
        quad = jnp.where(lane < HALF, meta, 0.0)
        quads.append(quad + pltpu.roll(quad, HALF, 1))
        weights.append(weight)
    weight = jnp.concatenate(weights, axis=0)
    quad = jnp.concatenate(quads, axis=0)
    by_class = jnp.dot(weight.T, quad, precision=HIGH, preferred_element_type=F32)
    by_shell = jnp.dot(quad.T, weight, precision=HIGH, preferred_element_type=F32)[0:HALF, :]
    tail = jnp.where(lane < HALF, by_class[0:16, :], by_class[16:32, :]).astype(BF16)
    wide = lanes_of((HALF, LANES))
    spare = jnp.where(
        (wide >= CLASSES) & (wide < HALF),
        pltpu.roll(by_shell, CLASSES - 32, 1),
        jnp.where(wide >= HALF + CLASSES, pltpu.roll(by_shell, CLASSES - 46, 1), 0.0),
    ).astype(BF16)
    for xz in range(GROUPS // 2):
        pay_ref[xz, 0:HALF, :] = spare
        pay_ref[xz, PAY_ROWS : PAY_ROWS + 16, :] = tail

    def turned_posterior(g, b, c):
        first = (ROTATIONS - b) * ROWS
        second = (ROTATIONS - c) * ROWS
        return (
            tables[2 * g][first : first + total_rows, :]
            + tables[2 * g + 1][second : second + total_rows, :]
        )

    for b in range(CHUNKS):
        kept = [i for i in range(16) if (16 * b + i) // CHUNKS % 2 == 0]
        bands = []
        for i in kept:
            if bands and bands[-1][1] == i:
                bands[-1][1] = i + 1
            else:
                bands.append([i, i + 1])
        out = jnp.zeros((16 * len(kept), BLOCK), F32)
        for g, turned_ref in enumerate((mine_turned_ref, sibling_turned_ref)):
            left = jnp.concatenate([turned_ref[16 * lo : 16 * hi, :] for lo, hi in bands], axis=0)
            mixed = jnp.concatenate(
                [turned_posterior(g, b, b + 9), turned_posterior(g, b + 18, b + 27)], axis=1
            )
            out = out + jnp.dot(left, mixed, preferred_element_type=F32)
        out = out.astype(BF16)
        for e in range(4):
            for n, i in enumerate(kept):
                q = (b + 9 * e) * 16 + i
                xz, j = q // CHUNKS // 2, q % CHUNKS
                piece = out[n * 16 : (n + 1) * 16, e * HALF : e * HALF + CLASSES]
                if j < CHUNKS - 1:
                    at = j // 2 * 16
                    lo = j % 2 * HALF
                    pay_ref[xz, at : at + 16, lo : lo + CLASSES] = piece
                else:
                    pay_ref[xz, PAY_ROWS - 8 : PAY_ROWS, 0:CLASSES] = piece[0:8, :]
                    pay_ref[xz, PAY_ROWS - 8 : PAY_ROWS, HALF : HALF + CLASSES] = piece[8:16, :]


def final_body(parts_ref, sums_ref, weights_ref):
    acc = parts_ref[0, :, :].astype(F32)
    for g in range(1, GROUPS // 2):
        acc = acc + parts_ref[g, :, :].astype(F32)
    pieces = []
    for j in range(CHUNKS - 1):
        lo = j % 2 * HALF
        pieces.append(acc[j // 2 * 16 : j // 2 * 16 + 16, lo : lo + HALF])
    pieces.append(acc[PAY_ROWS - 8 : PAY_ROWS, 0:HALF])
    pieces.append(acc[PAY_ROWS - 8 : PAY_ROWS, HALF:LANES])
    full = jnp.concatenate(pieces, axis=0)
    sums_ref[...] = full.T[0:CLASSES, :]
    weights_ref[0:16, :] = acc[PAY_ROWS : PAY_ROWS + 16, 0:HALF]
    weights_ref[16:32, :] = acc[PAY_ROWS : PAY_ROWS + 16, HALF:LANES]
    rest = acc[0:HALF, :].T
    weights_ref[32:46, :] = rest[CLASSES:HALF, :]
    weights_ref[46:CLASSES, :] = rest[HALF + CLASSES : HALF + CLASSES + 4, :]


def shards(images, ctf, inv_noise, classes, candidates):
    class_block = classes.shape[0]
    part = images.shape[0]
    my_index = lax.axis_index("cls")
    core = lax.axis_index("core").astype(jnp.int32).reshape(1)
    total_rows = ROTATIONS * ROWS
    width = FEATURES + LANES
    shape = jax.ShapeDtypeStruct
    vmem = pl.BlockSpec(memory_space=pltpu.VMEM)
    smem = pl.BlockSpec(memory_space=pltpu.SMEM)
    raw = pl.BlockSpec(memory_space=pltpu.HBM)

    def swap(value, axes):
        return lax.all_to_all(value, axes, split_axis=0, concat_axis=0, tiled=True)

    def cross_core(value):
        return lax.ppermute(value, "core", [(0, 1), (1, 0)])

    def pack(*refs):
        pack_body(class_block, *refs)

    hbm = [
        pltpu.with_memory_space_constraint(value, pltpu.HBM)
        for value in (images, ctf, inv_noise.reshape(1, CYCLES), candidates.T)
    ]
    packed = call(
        pack,
        shape((8, 2, width), BF16),
        *hbm,
        in_specs=[raw] * 4,
        scratch=[
            pltpu.VMEM((part, FEATURES), BF16),
            pltpu.VMEM((part, CYCLES), F32),
            pltpu.VMEM((1, CYCLES), F32),
            pltpu.VMEM((2, part), jnp.int32),
            pltpu.SemaphoreType.DMA((4,)),
        ],
    )
    rows = swap(packed, "cls").reshape(ROWS, width)
    table, energy = call(
        prep_body,
        (shape((ROTATIONS * HALF, BLOCK), BF16), shape((LANES, LANES), F32)),
        classes,
    )
    logits, stats, blocks = call(
        cross_body,
        (
            shape((total_rows, LANES), F32),
            shape((16, 2, LANES), F32),
            shape((total_rows + ROWS, BLOCK), BF16),
        ),
        rows,
        table,
        energy,
        scratch=[pltpu.VMEM((total_rows, LANES), F32)],
    )
    group_stats = swap(stats, ("core", "cls"))
    turned, turned_out, logits_out = call(
        turn_body,
        (
            shape((BLOCK, total_rows), BF16),
            shape((BLOCK + ROWS, total_rows), BF16),
            shape((total_rows, LANES), F32),
        ),
        core,
        blocks,
        logits,
        in_specs=[smem, vmem, vmem],
        micros=10,
    )
    other_turned = cross_core(turned_out)
    other_logits = cross_core(logits_out)
    pay, evidence = call(
        sums_body,
        (shape((GROUPS // 2, PAY_ROWS + 16, LANES), BF16), shape((1, LANES), F32)),
        core,
        group_stats,
        logits,
        other_logits,
        blocks[total_rows:, :LANES],
        other_turned[BLOCK:, :LANES],
        turned,
        other_turned,
        in_specs=[smem] + [vmem] * 7,
        scratch=[pltpu.VMEM((2 * total_rows, LANES), BF16)] * 4,
    )
    parts = swap(pay, ("x", "z"))
    sums, weight_sums = call(
        final_body, (shape((CLASSES, SLICE), F32), shape((CLASSES, CYCLES), F32)), parts
    )
    own = lax.dynamic_slice(evidence.reshape(LANES), (my_index * 4,), (4,))
    return sums.T, weight_sums, own


def solution(mesh):
    fine = Mesh(mesh.devices.reshape(4, 8, 2, 8), ("x", "z", "core", "cls"))
    dom = ("x", "z", "core")
    every = dom + ("cls",)
    in_specs = (P(every, None), P(every, None), P(), P("cls", None), P(every, None))
    out_specs = (P(dom, "cls"), P("cls", None), P(every))
    return jax.shard_map(shards, mesh=fine, in_specs=in_specs, out_specs=out_specs, check_vma=False)
```

time: 83.5 us -> 78.6 us (0.941)
  blocking collectives: 4.67 us -> 0 us
  starting transfers between devices: 23 us -> 27.5 us
  waiting for transfers between devices: 44 us -> 39.8 us
  local copies, waits for them, and re-layouts: 5.11 us -> 1.92 us
  Pallas kernels: 5.62 us -> 8.15 us
    all_to_all x1 -> x0, blocking collectives: 4.67 us -> none  [swap(): return lax.all_to_all(value, axes, split_axis=0, concat_axis=0, tiled=True)]
    ppermute x0 -> x2, starting transfers between devices: none -> 4.33 us  [cross_core(): return lax.ppermute(value, 'core', [(0, 1), (1, 0)])]
    all_to_all x3, waiting for transfers between devices: 44 us -> 39.8 us  [swap(): return lax.all_to_all(value, axes, split_axis=0, concat_axis=0, tiled=True)]
    pallas_call x7 -> x6, Pallas kernels: 5.62 us -> 8.15 us  [call(): pl.pallas_call(body, out_shape=outs, scratch_shapes=list(scratch), compil...]
    unnamed x10 -> x2, local copies, waits for them, and re-layouts: 2.98 us -> 1.22 us
  transfers between devices with their start and end apart: 3 -> 5, of which waited for: 3 -> 3; matrix products, arithmetic and copies ran while one was open for 1% -> 1% of each run, Pallas kernels for 1% -> 0%
where the time goes in v2:
time: 78.6 us; the launch traced here: 78.1 us
  waiting for transfers between devices  39.8 us (51%)
  starting transfers between devices  27.5 us (35%)
  Pallas kernels  8.15 us (10%)
  local copies, waits for them, and re-layouts  1.92 us (2%)
    all_to_all x3, waiting for transfers between devices, swap(): return lax.all_to_all(value, axes, split_axis=0, concat_axis=0, tiled=True)  39.8 us
    all_to_all x3, starting transfers between devices, swap(): return lax.all_to_all(value, axes, split_axis=0, concat_axis=0, tiled=True)  23.2 us
    pallas_call x6, Pallas kernels, call(): pl.pallas_call(body, out_shape=outs, scratch_shapes=list(scratch), compil...  8.15 us
    ppermute x2, starting transfers between devices, cross_core(): return lax.ppermute(value, 'core', [(0, 1), (1, 0)])  4.33 us
  transfers between devices with their start and end apart: 5, of which 3 were waited for; matrix products, arithmetic and copies ran while one was open for 1% of the time, Pallas kernels for 0%

profile of v2, /device:TPU:64, one launch (start us, length us, event | category | flops | bytes accessed | tf_op | source)
XLA Modules:
  0.0 78.1 jit_solution(12138181036032964469)
XLA Ops:
  0.6 2.1 %shard_map.76 = bf16[8,2,9344]{2,1,0:T(2,128)(2,1)} custom-call(bf16[4,9216]{1,0:T(4,128)(2,1)} %refs_0_.1, f32[4,64]{1,0:T(4,128)} %refs_1_.1, f32[1,64]{1,0:T(1,128)} %bitcast.7, s32[2,4]{1,0:T(2,128)} %bitcast.6), custom_call_target="tpu_custom_call" | custom-call | tf_op jit(solution)/shard_map/pallas_call | solution.py:41
  2.7 7.1 %all-to-all-start = ((bf16[8,2,9344]{2,1,0:T(2,128)(2,1)}), bf16[8,2,9344]{2,1,0:T(2,128)(2,1)S(1)}, u32[]{:S(2)}, u32[]{:S(2)}) async-start(bf16[8,2,9344]{2,1,0:T(2,128)(2,1)} %shard_map.76), calls=%async_computation | async-start | bytes 598016 | tf_op jit(solution)/shard_map/all_to_all | solution.py:346
  9.8 0.0 copy-start
  9.8 1.2 %copy-done = bf16[50,9216]{1,0:T(8,128)(2,1)S(1)} copy-done((bf16[50,9216]{1,0:T(8,128)(2,1)S(1)}, bf16[50,9216]{1,0:T(8,128)(2,1)}, u32[]{:S(2)}) %copy-start) | copy-done | bytes 921624
  11.0 0.3 shard_map.77
  11.4 11.1 %all-to-all-done = bf16[8,2,9344]{2,1,0:T(2,128)(2,1)S(1)} async-done(((bf16[8,2,9344]{2,1,0:T(2,128)(2,1)}), bf16[8,2,9344]{2,1,0:T(2,128)(2,1)S(1)}, u32[]{:S(2)}, u32[]{:S(2)}) %all-to-all-start) | async-done | bytes 299040 | tf_op jit(solution)/shard_map/all_to_all | solution.py:346
  22.5 0.1 reshape.19.rows_ref
  22.6 1.9 %shard_map.78 = (f32[576,128]{1,0:T(8,128)S(1)}, f32[16,2,128]{2,1,0:T(2,128)}, bf16[592,256]{1,0:T(8,128)(2,1)S(1)}) custom-call(bf16[16,9344]{1,0:T(8,128)(2,1)S(1)} %reshape.19.rows_ref, bf16[2304,256]{1,0:T(8,128)(2,1)S(1)} %get-tuple-element.15.table_ref, f32[128,128]{1,0:T(8,128)S(1)} %get-tuple-element.16.energy_ref), custom_call_target="tpu_custom_call" | custom-call | tf_op jit(solution)/shard_map/pallas_call | solution.py:41
  24.5 0.4 shard_map.79
  24.9 1.9 %collective-permute-start.1 = (bf16[272,576]{1,0:T(8,128)(2,1)S(1)}, bf16[272,576]{1,0:T(8,128)(2,1)S(1)}, u32[]{:S(2)}, u32[]{:S(2)}) collective-permute-start(bf16[272,576]{1,0:T(8,128)(2,1)S(1)} %get-tuple-element.21), channel_id=1, source_target_pairs={{0,8},{8,0},{1,9},{9,1},{2,10},{10,2},{3,11},{11,3},{4,12},{12,4},... | collective-permute-start | bytes 940040 | tf_op jit(solution)/shard_map/ppermute | solution.py:349
  26.8 2.4 %collective-permute-start = (f32[576,128]{1,0:T(8,128)S(1)}, f32[576,128]{1,0:T(8,128)S(1)}, u32[]{:S(2)}, u32[]{:S(2)}) collective-permute-start(f32[576,128]{1,0:T(8,128)S(1)} %get-tuple-element.20), channel_id=1, source_target_pairs={{0,8},{8,0},{1,9},{9,1},{2,10},{10,2},{3,11},{11,3},{4,12},{12,4},... | collective-permute-start | bytes 884744 | tf_op jit(solution)/shard_map/ppermute | solution.py:349
  29.2 3.5 %all-to-all-start.1 = ((f32[16,2,128]{2,1,0:T(2,128)}), f32[16,2,128]{2,1,0:T(2,128)S(1)}, u32[]{:S(2)}, u32[]{:S(2)}) async-start(f32[16,2,128]{2,1,0:T(2,128)} %get-tuple-element.17), calls=%async_computation.1 | async-start | bytes 32768 | tf_op jit(solution)/shard_map/all_to_all | solution.py:346
  32.8 0.0 collective-permute-done.1.sibling_turned_ref
  32.8 7.5 %all-to-all-done.1.stats_ref = f32[16,2,128]{2,1,0:T(2,128)S(1)} async-done(((f32[16,2,128]{2,1,0:T(2,128)}), f32[16,2,128]{2,1,0:T(2,128)S(1)}, u32[]{:S(2)}, u32[]{:S(2)}) %all-to-all-start.1) | async-done | bytes 16416 | tf_op jit(solution)/shard_map/all_to_all | solution.py:346
  40.3 0.0 collective-permute-done.sibling_logits_ref
  40.3 2.6 %shard_map.80 = (bf16[32,88,128]{2,1,0:T(8,128)(2,1)}, f32[1,128]{1,0:T(1,128)S(1)}) custom-call(s32[1]{0:T(128)} %bitcast.core_ref, f32[16,2,128]{2,1,0:T(2,128)S(1)} %all-to-all-done.1.stats_ref, f32[576,128]{1,0:T(8,128)S(1)} %get-tuple-element.18.logits_ref.mine_logits_ref, f32[576,128]{1,0:T(8,128)S(1)} %collective-permute-done.sibling_logits_ref, ...), custom_call_target="tpu_custom_call" | custom-call | tf_op jit(solution)/shard_map/pallas_call | solution.py:41
  42.9 12.6 %all-to-all-start.2 = ((bf16[32,88,128]{2,1,0:T(8,128)(2,1)}), bf16[32,88,128]{2,1,0:T(8,128)(2,1)S(1)}, u32[]{:S(2)}, u32[]{:S(2)}) async-start(bf16[32,88,128]{2,1,0:T(8,128)(2,1)} %get-tuple-element.23), calls=%async_computation.2 | async-start | bytes 1441792 | tf_op jit(solution)/shard_map/all_to_all | solution.py:346
  55.5 0.6 dynamic-slice_bitcast_fusion
  56.0 21.2 %all-to-all-done.2.parts_ref = bf16[32,88,128]{2,1,0:T(8,128)(2,1)S(1)} async-done(((bf16[32,88,128]{2,1,0:T(8,128)(2,1)}), bf16[32,88,128]{2,1,0:T(8,128)(2,1)S(1)}, u32[]{:S(2)}, u32[]{:S(2)}) %all-to-all-start.2) | async-done | bytes 720928 | tf_op jit(solution)/shard_map/all_to_all | solution.py:346
  77.2 0.9 %shard_map.81 = (f32[50,144]{1,0:T(8,128)}, f32[50,64]{1,0:T(8,128)}) custom-call(bf16[32,88,128]{2,1,0:T(8,128)(2,1)S(1)} %all-to-all-done.2.parts_ref), custom_call_target="tpu_custom_call" | custom-call | tf_op jit(solution)/shard_map/pallas_call | solution.py:41
  (2 shorter events, 0.0 us)
Async XLA Ops:
  2.7 19.8 %all-to-all-start = ((bf16[8,2,9344]{2,1,0:T(2,128)(2,1)}), bf16[8,2,9344]{2,1,0:T(2,128)(2,1)S(1)}, u32[]{:S(2)}, u32[]{:S(2)}) async-start(bf16[8,2,9344]{2,1,0:T(2,128)(2,1)} %shard_map.76), calls=%async_computation | async-start | bytes 598016 | tf_op jit(solution)/shard_map/all_to_all | solution.py:346
  9.8 1.2 %copy-start = (bf16[50,9216]{1,0:T(8,128)(2,1)S(1)}, bf16[50,9216]{1,0:T(8,128)(2,1)}, u32[]{:S(2)}) copy-start(bf16[50,9216]{1,0:T(8,128)(2,1)} %classes_ref.1) | copy-start | bytes 2764804
  24.9 7.9 %collective-permute-start.1 = (bf16[272,576]{1,0:T(8,128)(2,1)S(1)}, bf16[272,576]{1,0:T(8,128)(2,1)S(1)}, u32[]{:S(2)}, u32[]{:S(2)}) collective-permute-start(bf16[272,576]{1,0:T(8,128)(2,1)S(1)} %get-tuple-element.21), channel_id=1, source_target_pairs={{0,8},{8,0},{1,9},{9,1},{2,10},{10,2},{3,11},{11,3},{4,12},{12,4},... | collective-permute-start | bytes 940040 | tf_op jit(solution)/shard_map/ppermute | solution.py:349
  26.8 13.4 %collective-permute-start = (f32[576,128]{1,0:T(8,128)S(1)}, f32[576,128]{1,0:T(8,128)S(1)}, u32[]{:S(2)}, u32[]{:S(2)}) collective-permute-start(f32[576,128]{1,0:T(8,128)S(1)} %get-tuple-element.20), channel_id=1, source_target_pairs={{0,8},{8,0},{1,9},{9,1},{2,10},{10,2},{3,11},{11,3},{4,12},{12,4},... | collective-permute-start | bytes 884744 | tf_op jit(solution)/shard_map/ppermute | solution.py:349
  29.2 11.0 %all-to-all-start.1 = ((f32[16,2,128]{2,1,0:T(2,128)}), f32[16,2,128]{2,1,0:T(2,128)S(1)}, u32[]{:S(2)}, u32[]{:S(2)}) async-start(f32[16,2,128]{2,1,0:T(2,128)} %get-tuple-element.17), calls=%async_computation.1 | async-start | bytes 32768 | tf_op jit(solution)/shard_map/all_to_all | solution.py:346
  42.9 34.4 %all-to-all-start.2 = ((bf16[32,88,128]{2,1,0:T(8,128)(2,1)}), bf16[32,88,128]{2,1,0:T(8,128)(2,1)S(1)}, u32[]{:S(2)}, u32[]{:S(2)}) async-start(bf16[32,88,128]{2,1,0:T(8,128)(2,1)} %get-tuple-element.23), calls=%async_computation.2 | async-start | bytes 1441792 | tf_op jit(solution)/shard_map/all_to_all | solution.py:346

commit v3 on v2

--- a/solution.py
+++ b/solution.py
@@ -12,7 +12,9 @@
 LANES = 128
 HALF = 64
 ROWS = 16
+MICROS = 5
 GROUPS = 64
+TARGETS = GROUPS // 4
 CLASSES = 50
 SLICE = FEATURES // GROUPS
 CHUNKS = SLICE // 16
@@ -134,13 +136,22 @@
 def row_facts(meta):
     lane = lanes_of(meta.shape)
     flags = jnp.where((lane >= HALF) & (lane < P_LANE), meta, 0.0)
-    live = (flags + pltpu.roll(flags, HALF, 1)) > 0.5
+    flags = (flags + pltpu.roll(flags, HALF, 1)) > 0.5
     marks = jnp.where(lane >= P_LANE, meta, 0.0)
     valid = jnp.sum(marks, axis=1, keepdims=True)
     own = jnp.sum(marks * (lane - P_LANE).astype(F32), axis=1, keepdims=True)
     source = (rows_of(meta.shape) // 2 * 4).astype(F32)
     spot = (lane.astype(F32) == source + own) & (valid > 0.5)
-    return live, spot
+    return flags, spot
+
+
+def slots_of(live):
+    lane = lanes_of(live.shape)
+    ids = (lane % HALF).astype(F32)
+    low = jnp.min(jnp.where(live, ids, 1000.0), axis=1, keepdims=True)
+    high = jnp.max(jnp.where(live, ids, -1.0), axis=1, keepdims=True)
+    high = jnp.where(high > low, high, -1.0)
+    return ids == low, ids == high, low < 999.0, high > -0.5
 
 
 def cross_body(rows_ref, table_ref, energy_ref, logits_ref, stats_ref, blocks_ref, acc_ref):
@@ -149,7 +160,7 @@
         blocks_ref[b * ROWS : (b + 1) * ROWS, :] = rows_ref[:, b * BLOCK : (b + 1) * BLOCK]
     for m in range(ROTATIONS // 4):
         g = lax.dot_general(
-            blocks_ref[0:total_rows, :],
+            blocks_ref[...],
             table_ref[m * BLOCK : (m + 1) * BLOCK, :],
             (((1,), (1,)), ((), ())),
             preferred_element_type=F32,
@@ -162,10 +173,7 @@
             else:
                 acc_ref[0 : total_rows - shift, :] += tile[shift:, :]
                 acc_ref[total_rows - shift :, :] += tile[:shift, :]
-    raw = rows_ref[:, FEATURES : FEATURES + LANES]
-    blocks_ref[total_rows:, 0:LANES] = raw
-    blocks_ref[total_rows:, LANES:] = jnp.zeros((ROWS, LANES), BF16)
-    meta = raw.astype(F32)
+    meta = rows_ref[:, FEATURES : FEATURES + LANES].astype(F32)
     lane = lanes_of((ROWS, LANES))
     live, spot = row_facts(meta)
     quad = jnp.where(lane < HALF, meta, 0.0)
@@ -197,90 +205,117 @@
         stats_ref[d, 1:2, :] = total_row
 
 
-def turn_body(core_ref, blocks_ref, logits_ref, mine_ref, theirs_ref, logits_out_ref):
+def bundle_body(rows_ref, logits_ref, out_ref):
     total_rows = ROTATIONS * ROWS
-    second = core_ref[0] == 1
-    value = blocks_ref[0:total_rows, :].astype(F32)
-    rolled = pltpu.roll(value, BLOCK - SLICE, 1)
-    after = jnp.concatenate([rolled[ROWS:, :], rolled[:ROWS, :]], axis=0)
-    moved = jnp.where(lanes_of(value.shape) < BLOCK - SLICE, rolled, after)
-    mine_ref[...] = jnp.where(second, moved, value).T.astype(BF16)
-    theirs_ref[0:BLOCK, :] = jnp.where(second, value, moved).T.astype(BF16)
-    theirs_ref[BLOCK:, 0:LANES] = blocks_ref[total_rows:, 0:LANES]
-    theirs_ref[BLOCK:, LANES:] = jnp.zeros((ROWS, total_rows - LANES), BF16)
-    logits_out_ref[...] = logits_ref[...]
-
-
-def sums_body(
-    core_ref,
-    stats_ref,
-    mine_logits_ref,
-    sibling_logits_ref,
-    mine_meta_ref,
-    sibling_meta_ref,
-    mine_turned_ref,
-    sibling_turned_ref,
-    pay_ref,
-    evid_ref,
-    *tables,
-):
+    for b in range(ROTATIONS):
+        out_ref[b * ROWS : (b + 1) * ROWS, :] = rows_ref[:, b * BLOCK : (b + 1) * BLOCK]
+    raw = rows_ref[:, FEATURES : FEATURES + LANES]
+    live, _ = row_facts(raw.astype(F32))
+    lane = lanes_of((ROWS, LANES))
+    first, second, _, _ = slots_of(live & (lane < HALF))
+    first = first & (lane < HALF)
+    second = second & (lane < HALF)
+    compact = jnp.zeros((ROWS, LANES), F32)
+    for r in range(ROTATIONS):
+        value = logits_ref[r * ROWS : (r + 1) * ROWS, :]
+        one = jnp.sum(jnp.where(first, value, 0.0), axis=1, keepdims=True)
+        two = jnp.sum(jnp.where(second, value, 0.0), axis=1, keepdims=True)
+        compact = jnp.where(lane == r, one, jnp.where(lane == ROTATIONS + r, two, compact))
+    high = compact.astype(BF16)
+    rest = compact - high.astype(F32)
+    middle = rest.astype(BF16)
+    rest = rest - middle.astype(F32)
+    out_ref[total_rows : total_rows + ROWS, 0:LANES] = raw
+    out_ref[total_rows : total_rows + ROWS, LANES:] = high
+    out_ref[total_rows + ROWS :, 0:LANES] = middle
+    out_ref[total_rows + ROWS :, LANES:] = rest.astype(BF16)
+
+
+def turn_body(place_ref, one_ref, two_ref, out_ref):
     total_rows = ROTATIONS * ROWS
-    core = core_ref[0]
-    lane = lanes_of((ROWS, LANES))
-    weights, quads = [], []
-    for g, (logits_ref, meta_ref) in enumerate(
-        ((mine_logits_ref, mine_meta_ref), (sibling_logits_ref, sibling_meta_ref))
-    ):
-        left_ref, right_ref = tables[2 * g], tables[2 * g + 1]
-        place = (core if g == 0 else 1 - core) * 8
-        stats = stats_ref[pl.ds(place, 8), :, :]
+    second = place_ref[0] == 1
+    for g, blocks_ref in enumerate((one_ref, two_ref)):
+        value = blocks_ref[0:total_rows, :].astype(F32)
+        rolled = pltpu.roll(value, BLOCK - SLICE, 1)
+        after = jnp.concatenate([rolled[ROWS:, :], rolled[:ROWS, :]], axis=0)
+        moved = jnp.where(lanes_of(value.shape) < BLOCK - SLICE, rolled, after)
+        value = jnp.where(second, moved, value)
+        out_ref[:, g * total_rows : (g + 1) * total_rows] = value.T.astype(BF16)
+
+
+def evidence_body(place_ref, stats_ref, out_ref):
+    core, near = place_ref[0], place_ref[1]
+    for g in range(4):
+        at_core = core if g % 2 == 0 else 1 - core
+        at_near = near if g < 2 else 1 - near
+        stats = stats_ref[pl.ds((at_near * 2 + at_core) * 8, 8), :, :]
         peaks = stats[:, 0, :]
         totals = stats[:, 1, :]
         highest = jnp.max(peaks, axis=0, keepdims=True)
         total = jnp.sum(totals * jnp.exp(peaks - highest), axis=0, keepdims=True)
-        evidence = highest + jnp.log(total)
-        if g == 0:
-            evid_ref[...] = evidence
-        meta = meta_ref[...].astype(F32)
+        out_ref[g : g + 1, :] = highest + jnp.log(total)
+
+
+def sums_body(
+    place_ref, evid_ref, tail_a, tail_b, tail_c, tail_d, turned_a, turned_b, pay_ref, *tables
+):
+    total_rows = ROTATIONS * ROWS
+    near = place_ref[1]
+    lane = lanes_of((ROWS, LANES))
+    on_left = lane < HALF
+    weights, quads = [], []
+    for g, tail_ref in enumerate((tail_a, tail_b, tail_c, tail_d)):
+        table_ref = tables[g]
+        evidence = evid_ref[g : g + 1, :]
+        meta = tail_ref[0:ROWS, 0:LANES].astype(F32)
+        logits = tail_ref[0:ROWS, LANES:].astype(F32) + (
+            tail_ref[ROWS:, 0:LANES].astype(F32) + tail_ref[ROWS:, LANES:].astype(F32)
+        )
         live, spot = row_facts(meta)
+        first, second, has_first, has_second = slots_of(live)
         row_evidence = jnp.sum(jnp.where(spot, evidence, 0.0), axis=1, keepdims=True)
-        weight = jnp.zeros((ROWS, LANES), F32)
-        for r in range(ROTATIONS):
-            value = logits_ref[r * ROWS : (r + 1) * ROWS, :]
-            post = jnp.where(live, jnp.exp(value - row_evidence), 0.0).astype(BF16).astype(F32)
-            weight = weight + post
-            one = jnp.where(lane < HALF, post, 0.0).astype(BF16)
-            two = jnp.where(lane < HALF, 0.0, post).astype(BF16)
-            left_ref[r * ROWS : (r + 1) * ROWS, :] = one
-            left_ref[total_rows + r * ROWS : total_rows + (r + 1) * ROWS, :] = one
-            right_ref[r * ROWS : (r + 1) * ROWS, :] = two
-            right_ref[total_rows + r * ROWS : total_rows + (r + 1) * ROWS, :] = two
-        quad = jnp.where(lane < HALF, meta, 0.0)
+        known = ((lane < ROTATIONS) & has_first) | (
+            (lane >= ROTATIONS) & (lane < 2 * ROTATIONS) & has_second
+        )
+        post = jnp.where(known, jnp.exp(logits - row_evidence), 0.0).astype(BF16).astype(F32)
+        first = first.astype(F32)
+        second = second.astype(F32)
+        total_one = jnp.sum(jnp.where(lane < ROTATIONS, post, 0.0), axis=1, keepdims=True)
+        total_two = jnp.sum(jnp.where(lane < ROTATIONS, 0.0, post), axis=1, keepdims=True)
+        weights.append(total_one * first + total_two * second)
+        half = ROTATIONS // 2
+
+        def spread(r):
+            return (
+                post[:, r : r + 1] * first + post[:, ROTATIONS + r : ROTATIONS + r + 1] * second
+            )
+
+        for r in range(half):
+            here, there = spread(r), spread(r + half)
+            for row, value in (
+                (r, jnp.where(on_left, here, there)),
+                (r + half, jnp.where(on_left, there, here)),
+            ):
+                value = value.astype(BF16)
+                table_ref[row * ROWS : (row + 1) * ROWS, :] = value
+                table_ref[total_rows + row * ROWS : total_rows + (row + 1) * ROWS, :] = value
+        quad = jnp.where(on_left, meta, 0.0)
         quads.append(quad + pltpu.roll(quad, HALF, 1))
-        weights.append(weight)
     weight = jnp.concatenate(weights, axis=0)
     quad = jnp.concatenate(quads, axis=0)
     by_class = jnp.dot(weight.T, quad, precision=HIGH, preferred_element_type=F32)
     by_shell = jnp.dot(quad.T, weight, precision=HIGH, preferred_element_type=F32)[0:HALF, :]
-    tail = jnp.where(lane < HALF, by_class[0:16, :], by_class[16:32, :]).astype(BF16)
+    tail = jnp.where(on_left, by_class[0:16, :], by_class[16:32, :]).astype(BF16)
     wide = lanes_of((HALF, LANES))
     spare = jnp.where(
         (wide >= CLASSES) & (wide < HALF),
         pltpu.roll(by_shell, CLASSES - 32, 1),
         jnp.where(wide >= HALF + CLASSES, pltpu.roll(by_shell, CLASSES - 46, 1), 0.0),
     ).astype(BF16)
-    for xz in range(GROUPS // 2):
-        pay_ref[xz, 0:HALF, :] = spare
-        pay_ref[xz, PAY_ROWS : PAY_ROWS + 16, :] = tail
-
-    def turned_posterior(g, b, c):
-        first = (ROTATIONS - b) * ROWS
-        second = (ROTATIONS - c) * ROWS
-        return (
-            tables[2 * g][first : first + total_rows, :]
-            + tables[2 * g + 1][second : second + total_rows, :]
-        )
-
+    for d in range(TARGETS):
+        pay_ref[d, 0:HALF, :] = spare
+        pay_ref[d, PAY_ROWS : PAY_ROWS + 16, :] = tail
+    base = (ROTATIONS - CHUNKS * near) * ROWS
     for b in range(CHUNKS):
         kept = [i for i in range(16) if (16 * b + i) // CHUNKS % 2 == 0]
         bands = []
@@ -289,31 +324,36 @@
                 bands[-1][1] = i + 1
             else:
                 bands.append([i, i + 1])
-        out = jnp.zeros((16 * len(kept), BLOCK), F32)
-        for g, turned_ref in enumerate((mine_turned_ref, sibling_turned_ref)):
+        start = pl.multiple_of(base - b * ROWS, ROWS)
+        out = jnp.zeros((16 * len(kept), LANES), F32)
+        for g, turned_ref in enumerate((turned_a, turned_b)):
             left = jnp.concatenate([turned_ref[16 * lo : 16 * hi, :] for lo, hi in bands], axis=0)
-            mixed = jnp.concatenate(
-                [turned_posterior(g, b, b + 9), turned_posterior(g, b + 18, b + 27)], axis=1
+            right = jnp.concatenate(
+                [
+                    tables[2 * g][pl.ds(start, total_rows), :],
+                    tables[2 * g + 1][pl.ds(start, total_rows), :],
+                ],
+                axis=0,
             )
-            out = out + jnp.dot(left, mixed, preferred_element_type=F32)
+            out = out + jnp.dot(left, right, preferred_element_type=F32)
         out = out.astype(BF16)
-        for e in range(4):
+        for e in range(2):
             for n, i in enumerate(kept):
-                q = (b + 9 * e) * 16 + i
-                xz, j = q // CHUNKS // 2, q % CHUNKS
+                q = b * 16 + i
+                d, j = e * 8 + q // CHUNKS // 2, q % CHUNKS
                 piece = out[n * 16 : (n + 1) * 16, e * HALF : e * HALF + CLASSES]
                 if j < CHUNKS - 1:
                     at = j // 2 * 16
                     lo = j % 2 * HALF
-                    pay_ref[xz, at : at + 16, lo : lo + CLASSES] = piece
+                    pay_ref[d, at : at + 16, lo : lo + CLASSES] = piece
                 else:
-                    pay_ref[xz, PAY_ROWS - 8 : PAY_ROWS, 0:CLASSES] = piece[0:8, :]
-                    pay_ref[xz, PAY_ROWS - 8 : PAY_ROWS, HALF : HALF + CLASSES] = piece[8:16, :]
+                    pay_ref[d, PAY_ROWS - 8 : PAY_ROWS, 0:CLASSES] = piece[0:8, :]
+                    pay_ref[d, PAY_ROWS - 8 : PAY_ROWS, HALF : HALF + CLASSES] = piece[8:16, :]
 
 
 def final_body(parts_ref, sums_ref, weights_ref):
     acc = parts_ref[0, :, :].astype(F32)
-    for g in range(1, GROUPS // 2):
+    for g in range(1, TARGETS):
         acc = acc + parts_ref[g, :, :].astype(F32)
     pieces = []
     for j in range(CHUNKS - 1):
@@ -334,7 +374,7 @@
     class_block = classes.shape[0]
     part = images.shape[0]
     my_index = lax.axis_index("cls")
-    core = lax.axis_index("core").astype(jnp.int32).reshape(1)
+    place = jnp.stack([lax.axis_index("core"), lax.axis_index("xl")]).astype(jnp.int32)
     total_rows = ROTATIONS * ROWS
     width = FEATURES + LANES
     shape = jax.ShapeDtypeStruct
@@ -345,8 +385,8 @@
     def swap(value, axes):
         return lax.all_to_all(value, axes, split_axis=0, concat_axis=0, tiled=True)
 
-    def cross_core(value):
-        return lax.ppermute(value, "core", [(0, 1), (1, 0)])
+    def flip(value, axis):
+        return lax.ppermute(value, axis, [(0, 1), (1, 0)])
 
     def pack(*refs):
         pack_body(class_block, *refs)
@@ -374,59 +414,60 @@
         (shape((ROTATIONS * HALF, BLOCK), BF16), shape((LANES, LANES), F32)),
         classes,
     )
-    logits, stats, blocks = call(
+    logits, stats = call(
         cross_body,
-        (
-            shape((total_rows, LANES), F32),
-            shape((16, 2, LANES), F32),
-            shape((total_rows + ROWS, BLOCK), BF16),
-        ),
+        (shape((total_rows, LANES), F32), shape((32, 2, LANES), F32)),
         rows,
         table,
         energy,
-        scratch=[pltpu.VMEM((total_rows, LANES), F32)],
-    )
-    group_stats = swap(stats, ("core", "cls"))
-    turned, turned_out, logits_out = call(
-        turn_body,
-        (
-            shape((BLOCK, total_rows), BF16),
-            shape((BLOCK + ROWS, total_rows), BF16),
-            shape((total_rows, LANES), F32),
-        ),
-        core,
-        blocks,
-        logits,
-        in_specs=[smem, vmem, vmem],
-        micros=10,
-    )
-    other_turned = cross_core(turned_out)
-    other_logits = cross_core(logits_out)
-    pay, evidence = call(
+        scratch=[pltpu.VMEM((total_rows, BLOCK), BF16), pltpu.VMEM((total_rows, LANES), F32)],
+    )
+    group_stats = swap(stats, ("xl", "core", "cls"))
+    mine = call(bundle_body, shape((total_rows + 2 * ROWS, BLOCK), BF16), rows, logits)
+    beside = flip(mine, "xl")
+    sibling = flip(mine, "core")
+    across = lax.ppermute(mine, ("xl", "core"), [(0, 3), (1, 2), (2, 1), (3, 0)])
+
+    def turn(one, two):
+        return call(
+            turn_body,
+            shape((BLOCK, 2 * total_rows), BF16),
+            place,
+            one,
+            two,
+            in_specs=[smem, vmem, vmem],
+        )
+
+    evidence = call(
+        evidence_body,
+        shape((4, LANES), F32),
+        place,
+        group_stats,
+        in_specs=[smem, vmem],
+        micros=MICROS,
+    )
+    pay = call(
         sums_body,
-        (shape((GROUPS // 2, PAY_ROWS + 16, LANES), BF16), shape((1, LANES), F32)),
-        core,
-        group_stats,
-        logits,
-        other_logits,
-        blocks[total_rows:, :LANES],
-        other_turned[BLOCK:, :LANES],
-        turned,
-        other_turned,
+        shape((TARGETS, PAY_ROWS + 16, LANES), BF16),
+        place,
+        evidence,
+        *(value[total_rows:, :] for value in (mine, sibling, beside, across)),
+        turn(mine, sibling),
+        turn(beside, across),
         in_specs=[smem] + [vmem] * 7,
         scratch=[pltpu.VMEM((2 * total_rows, LANES), BF16)] * 4,
     )
-    parts = swap(pay, ("x", "z"))
+    parts = swap(pay, ("xh", "z"))
     sums, weight_sums = call(
         final_body, (shape((CLASSES, SLICE), F32), shape((CLASSES, CYCLES), F32)), parts
     )
-    own = lax.dynamic_slice(evidence.reshape(LANES), (my_index * 4,), (4,))
+    own = lax.dynamic_slice(evidence, (0, my_index * 4), (1, 4)).reshape(4)
     return sums.T, weight_sums, own
 
 
 def solution(mesh):
-    fine = Mesh(mesh.devices.reshape(4, 8, 2, 8), ("x", "z", "core", "cls"))
-    dom = ("x", "z", "core")
+    dom = ("xh", "xl", "z", "core")
+    fine = Mesh(mesh.devices.reshape(2, 2, 8, 2, 8), dom + ("cls",))
     every = dom + ("cls",)
     in_specs = (P(every, None), P(every, None), P(), P("cls", None), P(every, None))
     out_specs = (P(dom, "cls"), P("cls", None), P(every))

time: 78.6 us -> 79.4 us (1.010)
  the two profiles are of different devices: /device:TPU:64 before, /device:TPU:1 now
where the time goes in v3:
time: 79.4 us; the launch traced here: 78.4 us
  starting transfers between devices  35.1 us (44%)
  waiting for transfers between devices  27.9 us (35%)
  Pallas kernels  12.6 us (16%)
  local copies, waits for them, and re-layouts  1.92 us (2%)
    all_to_all x3, waiting for transfers between devices, swap(): return lax.all_to_all(value, axes, split_axis=0, concat_axis=0, tiled=True)  27.9 us
    all_to_all x3, starting transfers between devices, swap(): return lax.all_to_all(value, axes, split_axis=0, concat_axis=0, tiled=True)  24.2 us
    pallas_call x9, Pallas kernels, call(): pl.pallas_call(body, out_shape=outs, scratch_shapes=list(scratch), compil...  12.6 us
    ppermute x1, starting transfers between devices, shards(): lax.ppermute(mine, ('xl', 'core'), [(0, 3), (1, 2), (2, 1), (3, 0)])  6.67 us
    ppermute x2, starting transfers between devices, flip(): return lax.ppermute(value, axis, [(0, 1), (1, 0)])  4.22 us
  transfers between devices with their start and end apart: 6, of which 3 were waited for; matrix products, arithmetic and copies ran while one was open for 1% of the time, Pallas kernels for 3%

profile of v3, /device:TPU:1, one launch (start us, length us, event | category | flops | bytes accessed | tf_op | source)
XLA Modules:
  0.0 78.4 jit_solution(2516606286455076166)
XLA Ops:
  0.6 2.1 %shard_map.76 = bf16[8,2,9344]{2,1,0:T(2,128)(2,1)} custom-call(bf16[4,9216]{1,0:T(4,128)(2,1)} %refs_0_.1, f32[4,64]{1,0:T(4,128)} %refs_1_.1, f32[1,64]{1,0:T(1,128)} %bitcast.8, s32[2,4]{1,0:T(2,128)} %bitcast.7), custom_call_target="tpu_custom_call" | custom-call | tf_op jit(solution)/shard_map/pallas_call | solution.py:43
  2.7 7.7 %all-to-all-start = ((bf16[8,2,9344]{2,1,0:T(2,128)(2,1)}), bf16[8,2,9344]{2,1,0:T(2,128)(2,1)S(1)}, u32[]{:S(2)}, u32[]{:S(2)}) async-start(bf16[8,2,9344]{2,1,0:T(2,128)(2,1)} %shard_map.76), calls=%async_computation | async-start | bytes 598016 | tf_op jit(solution)/shard_map/all_to_all | solution.py:386
  10.4 0.0 copy-start
  10.4 1.2 %copy-done = bf16[50,9216]{1,0:T(8,128)(2,1)S(1)} copy-done((bf16[50,9216]{1,0:T(8,128)(2,1)S(1)}, bf16[50,9216]{1,0:T(8,128)(2,1)}, u32[]{:S(2)}) %copy-start) | copy-done | bytes 921624
  11.6 0.3 shard_map.77
  11.9 8.4 %all-to-all-done = bf16[8,2,9344]{2,1,0:T(2,128)(2,1)S(1)} async-done(((bf16[8,2,9344]{2,1,0:T(2,128)(2,1)}), bf16[8,2,9344]{2,1,0:T(2,128)(2,1)S(1)}, u32[]{:S(2)}, u32[]{:S(2)}) %all-to-all-start) | async-done | bytes 299040 | tf_op jit(solution)/shard_map/all_to_all | solution.py:386
  20.3 0.1 reshape.16.rows_ref
  20.4 1.9 %shard_map.78 = (f32[576,128]{1,0:T(8,128)S(1)}, f32[32,2,128]{2,1,0:T(2,128)}) custom-call(bf16[16,9344]{1,0:T(8,128)(2,1)S(1)} %reshape.16.rows_ref, bf16[2304,256]{1,0:T(8,128)(2,1)S(1)} %get-tuple-element.9.table_ref, f32[128,128]{1,0:T(8,128)S(1)} %get-tuple-element.10.energy_ref), custom_call_target="tpu_custom_call" | custom-call | tf_op jit(solution)/shard_map/pallas_call | solution.py:43
  22.4 0.4 shard_map.80.one_ref
  22.8 6.7 %collective-permute-start.2 = (bf16[608,256]{1,0:T(8,128)(2,1)S(1)}, bf16[608,256]{1,0:T(8,128)(2,1)S(1)}, u32[]{:S(2)}, u32[]{:S(2)}) collective-permute-start(bf16[608,256]{1,0:T(8,128)(2,1)S(1)} %shard_map.80.one_ref), channel_id=1, source_target_pairs={{0,136},{8,128},{128,8},{136,0},{1,137},{9,129},{129,9},{137,1},{2... | collective-permute-start | bytes 933896 | tf_op jit(solution)/shard_map/ppermute | solution.py:429
  29.4 2.2 %collective-permute-start.1 = (bf16[608,256]{1,0:T(8,128)(2,1)S(1)}, bf16[608,256]{1,0:T(8,128)(2,1)S(1)}, u32[]{:S(2)}, u32[]{:S(2)}) collective-permute-start(bf16[608,256]{1,0:T(8,128)(2,1)S(1)} %shard_map.80.one_ref), channel_id=1, source_target_pairs={{0,128},{128,0},{1,129},{129,1},{2,130},{130,2},{3,131},{131,3},{4... | collective-permute-start | bytes 933896 | tf_op jit(solution)/shard_map/ppermute | solution.py:389
  31.6 2.1 %collective-permute-start = (bf16[608,256]{1,0:T(8,128)(2,1)S(1)}, bf16[608,256]{1,0:T(8,128)(2,1)S(1)}, u32[]{:S(2)}, u32[]{:S(2)}) collective-permute-start(bf16[608,256]{1,0:T(8,128)(2,1)S(1)} %shard_map.80.one_ref), channel_id=1, source_target_pairs={{0,8},{8,0},{1,9},{9,1},{2,10},{10,2},{3,11},{11,3},{4,12},{12,4},... | collective-permute-start | bytes 933896 | tf_op jit(solution)/shard_map/ppermute | solution.py:389
  33.7 3.9 %all-to-all-start.1 = ((f32[32,2,128]{2,1,0:T(2,128)}), f32[32,2,128]{2,1,0:T(2,128)S(1)}, u32[]{:S(2)}, u32[]{:S(2)}) async-start(f32[32,2,128]{2,1,0:T(2,128)} %get-tuple-element.11), calls=%async_computation.1 | async-start | bytes 65536 | tf_op jit(solution)/shard_map/all_to_all | solution.py:386
  37.6 0.1 pad_add_fusion.place_ref
  37.7 8.2 %all-to-all-done.1.stats_ref = f32[32,2,128]{2,1,0:T(2,128)S(1)} async-done(((f32[32,2,128]{2,1,0:T(2,128)}), f32[32,2,128]{2,1,0:T(2,128)S(1)}, u32[]{:S(2)}, u32[]{:S(2)}) %all-to-all-start.1) | async-done | bytes 32800 | tf_op jit(solution)/shard_map/all_to_all | solution.py:386
  45.9 0.6 shard_map.79.evid_ref
  46.5 0.0 collective-permute-done.2.two_ref
  46.5 0.0 collective-permute-done.1.one_ref
  46.5 1.3 %shard_map.82.turned_b = bf16[256,1152]{1,0:T(8,128)(2,1)S(1)} custom-call(s32[2]{0:T(128)S(1)} %pad_add_fusion.place_ref, bf16[608,256]{1,0:T(8,128)(2,1)S(1)} %collective-permute-done.1.one_ref, bf16[608,256]{1,0:T(8,128)(2,1)S(1)} %collective-permute-done.2.two_ref), custom_call_target="tpu_custom_call" | custom-call | tf_op jit(solution)/shard_map/pallas_call | solution.py:43
  47.8 0.0 collective-permute-done.two_ref
  47.9 1.3 %shard_map.81.turned_a = bf16[256,1152]{1,0:T(8,128)(2,1)S(1)} custom-call(s32[2]{0:T(128)S(1)} %pad_add_fusion.place_ref, bf16[608,256]{1,0:T(8,128)(2,1)S(1)} %shard_map.80.one_ref, bf16[608,256]{1,0:T(8,128)(2,1)S(1)} %collective-permute-done.two_ref), custom_call_target="tpu_custom_call" | custom-call | tf_op jit(solution)/shard_map/pallas_call | solution.py:43
  49.2 3.9 %shard_map.83 = bf16[16,88,128]{2,1,0:T(8,128)(2,1)} custom-call(s32[2]{0:T(128)S(1)} %pad_add_fusion.place_ref, f32[4,128]{1,0:T(4,128)S(1)} %shard_map.79.evid_ref, bf16[32,256]{1,0:T(8,128)(2,1)S(1)} %slice.16.tail_a, bf16[32,256]{1,0:T(8,128)(2,1)S(1)} %slice.17.tail_b, bf16[32,256]{1,0:T(8,128)(2,1)S(1)} %slice.18.tail_c, ...), custom_call_target="tpu_custom_call" | custom-call | tf_op jit(solution)/shard_map/pallas_call | solution.py:43
  53.1 12.6 %all-to-all-start.2 = ((bf16[16,88,128]{2,1,0:T(8,128)(2,1)}), bf16[16,88,128]{2,1,0:T(8,128)(2,1)S(1)}, u32[]{:S(2)}, u32[]{:S(2)}) async-start(bf16[16,88,128]{2,1,0:T(8,128)(2,1)} %shard_map.83), calls=%async_computation.2 | async-start | bytes 720896 | tf_op jit(solution)/shard_map/all_to_all | solution.py:386
  65.7 0.6 dynamic-slice_bitcast_fusion
  66.3 11.3 %all-to-all-done.2.parts_ref = bf16[16,88,128]{2,1,0:T(8,128)(2,1)S(1)} async-done(((bf16[16,88,128]{2,1,0:T(8,128)(2,1)}), bf16[16,88,128]{2,1,0:T(8,128)(2,1)S(1)}, u32[]{:S(2)}, u32[]{:S(2)}) %all-to-all-start.2) | async-done | bytes 360480 | tf_op jit(solution)/shard_map/all_to_all | solution.py:386
  77.6 0.8 %shard_map.84 = (f32[50,144]{1,0:T(8,128)}, f32[50,64]{1,0:T(8,128)}) custom-call(bf16[16,88,128]{2,1,0:T(8,128)(2,1)S(1)} %all-to-all-done.2.parts_ref), custom_call_target="tpu_custom_call" | custom-call | tf_op jit(solution)/shard_map/pallas_call | solution.py:43
  (4 shorter events, 0.0 us)
Async XLA Ops:
  2.7 17.6 %all-to-all-start = ((bf16[8,2,9344]{2,1,0:T(2,128)(2,1)}), bf16[8,2,9344]{2,1,0:T(2,128)(2,1)S(1)}, u32[]{:S(2)}, u32[]{:S(2)}) async-start(bf16[8,2,9344]{2,1,0:T(2,128)(2,1)} %shard_map.76), calls=%async_computation | async-start | bytes 598016 | tf_op jit(solution)/shard_map/all_to_all | solution.py:386
  10.4 1.2 %copy-start = (bf16[50,9216]{1,0:T(8,128)(2,1)S(1)}, bf16[50,9216]{1,0:T(8,128)(2,1)}, u32[]{:S(2)}) copy-start(bf16[50,9216]{1,0:T(8,128)(2,1)} %classes_ref.1) | copy-start | bytes 2764804
  22.8 23.7 %collective-permute-start.2 = (bf16[608,256]{1,0:T(8,128)(2,1)S(1)}, bf16[608,256]{1,0:T(8,128)(2,1)S(1)}, u32[]{:S(2)}, u32[]{:S(2)}) collective-permute-start(bf16[608,256]{1,0:T(8,128)(2,1)S(1)} %shard_map.80.one_ref), channel_id=1, source_target_pairs={{0,136},{8,128},{128,8},{136,0},{1,137},{9,129},{129,9},{137,1},{2... | collective-permute-start | bytes 933896 | tf_op jit(solution)/shard_map/ppermute | solution.py:429
  29.4 17.1 %collective-permute-start.1 = (bf16[608,256]{1,0:T(8,128)(2,1)S(1)}, bf16[608,256]{1,0:T(8,128)(2,1)S(1)}, u32[]{:S(2)}, u32[]{:S(2)}) collective-permute-start(bf16[608,256]{1,0:T(8,128)(2,1)S(1)} %shard_map.80.one_ref), channel_id=1, source_target_pairs={{0,128},{128,0},{1,129},{129,1},{2,130},{130,2},{3,131},{131,3},{4... | collective-permute-start | bytes 933896 | tf_op jit(solution)/shard_map/ppermute | solution.py:389
  31.6 16.2 %collective-permute-start = (bf16[608,256]{1,0:T(8,128)(2,1)S(1)}, bf16[608,256]{1,0:T(8,128)(2,1)S(1)}, u32[]{:S(2)}, u32[]{:S(2)}) collective-permute-start(bf16[608,256]{1,0:T(8,128)(2,1)S(1)} %shard_map.80.one_ref), channel_id=1, source_target_pairs={{0,8},{8,0},{1,9},{9,1},{2,10},{10,2},{3,11},{11,3},{4,12},{12,4},... | collective-permute-start | bytes 933896 | tf_op jit(solution)/shard_map/ppermute | solution.py:389
  33.7 12.2 %all-to-all-start.1 = ((f32[32,2,128]{2,1,0:T(2,128)}), f32[32,2,128]{2,1,0:T(2,128)S(1)}, u32[]{:S(2)}, u32[]{:S(2)}) async-start(f32[32,2,128]{2,1,0:T(2,128)} %get-tuple-element.11), calls=%async_computation.1 | async-start | bytes 65536 | tf_op jit(solution)/shard_map/all_to_all | solution.py:386
  53.1 24.5 %all-to-all-start.2 = ((bf16[16,88,128]{2,1,0:T(8,128)(2,1)}), bf16[16,88,128]{2,1,0:T(8,128)(2,1)S(1)}, u32[]{:S(2)}, u32[]{:S(2)}) async-start(bf16[16,88,128]{2,1,0:T(8,128)(2,1)} %shard_map.83), calls=%async_computation.2 | async-start | bytes 720896 | tf_op jit(solution)/shard_map/all_to_all | solution.py:386

commit v4 on v3

--- a/solution.py
+++ b/solution.py
@@ -12,9 +12,9 @@
 LANES = 128
 HALF = 64
 ROWS = 16
-MICROS = 5
 GROUPS = 64
 TARGETS = GROUPS // 4
+DEPTH = 640
 CLASSES = 50
 SLICE = FEATURES // GROUPS
 CHUNKS = SLICE // 16
@@ -34,12 +34,10 @@
     return lax.broadcasted_iota(jnp.int32, shape, len(shape) - 2)
 
 
-def call(body, outs, *args, in_specs=None, scratch=(), micros=0):
+def call(body, outs, *args, in_specs=None, out_specs=None, scratch=()):
     more = {} if in_specs is None else {"in_specs": in_specs}
-    if micros:
-        more["cost_estimate"] = pl.CostEstimate(
-            flops=0, transcendentals=0, bytes_accessed=micros * 3_000_000
-        )
+    if out_specs is not None:
+        more["out_specs"] = out_specs
     return pl.pallas_call(
         body,
         out_shape=outs,
@@ -231,21 +229,62 @@
     out_ref[total_rows + ROWS :, LANES:] = rest.astype(BF16)
 
 
-def turn_body(place_ref, one_ref, two_ref, out_ref):
+def turn_body(place_ref, blocks_ref, turned_ref, facts_ref):
     total_rows = ROTATIONS * ROWS
     second = place_ref[0] == 1
-    for g, blocks_ref in enumerate((one_ref, two_ref)):
-        value = blocks_ref[0:total_rows, :].astype(F32)
-        rolled = pltpu.roll(value, BLOCK - SLICE, 1)
-        after = jnp.concatenate([rolled[ROWS:, :], rolled[:ROWS, :]], axis=0)
-        moved = jnp.where(lanes_of(value.shape) < BLOCK - SLICE, rolled, after)
-        value = jnp.where(second, moved, value)
-        out_ref[:, g * total_rows : (g + 1) * total_rows] = value.T.astype(BF16)
-
-
-def evidence_body(place_ref, stats_ref, out_ref):
+    value = blocks_ref[0:total_rows, :].astype(F32)
+    rolled = pltpu.roll(value, BLOCK - SLICE, 1)
+    after = jnp.concatenate([rolled[ROWS:, :], rolled[:ROWS, :]], axis=0)
+    moved = jnp.where(lanes_of(value.shape) < BLOCK - SLICE, rolled, after)
+    value = jnp.where(second, moved, value)
+    turned_ref[:, 0:total_rows] = value.T.astype(BF16)
+    turned_ref[:, total_rows:] = jnp.zeros((BLOCK, DEPTH - total_rows), BF16)
+    lane = lanes_of((ROWS, LANES))
+    meta = blocks_ref[total_rows : total_rows + ROWS, 0:LANES].astype(F32)
+    logits = blocks_ref[total_rows : total_rows + ROWS, LANES:].astype(F32) + (
+        blocks_ref[total_rows + ROWS :, 0:LANES].astype(F32)
+        + blocks_ref[total_rows + ROWS :, LANES:].astype(F32)
+    )
+    live, spot = row_facts(meta)
+    first, second, has_first, has_second = slots_of(live)
+    known = ((lane < ROTATIONS) & has_first) | (
+        (lane >= ROTATIONS) & (lane < 2 * ROTATIONS) & has_second
+    )
+    quad = jnp.where(lane < HALF, meta, 0.0)
+    quad = quad + pltpu.roll(quad, HALF, 1)
+    for i, fact in enumerate((first, second, spot, known, logits, quad)):
+        facts_ref[i, :, :] = fact.astype(F32)
+
+
+def sums_body(
+    place_ref,
+    stats_ref,
+    facts_a,
+    facts_b,
+    facts_c,
+    facts_d,
+    turned_a,
+    turned_b,
+    turned_c,
+    turned_d,
+    out_any,
+    evid_ref,
+    pay_ref,
+    table_a,
+    table_b,
+    table_c,
+    table_d,
+    sems,
+):
+    total_rows = ROTATIONS * ROWS
     core, near = place_ref[0], place_ref[1]
-    for g in range(4):
+    all_facts = (facts_a, facts_b, facts_c, facts_d)
+    all_turned = (turned_a, turned_b, turned_c, turned_d)
+    tables = (table_a, table_b, table_c, table_d)
+    lane = lanes_of((ROWS, LANES))
+    on_left = lane < HALF
+    weights, quads = [], []
+    for g, (facts_ref, table_ref) in enumerate(zip(all_facts, tables)):
         at_core = core if g % 2 == 0 else 1 - core
         at_near = near if g < 2 else 1 - near
         stats = stats_ref[pl.ds((at_near * 2 + at_core) * 8, 8), :, :]
@@ -253,36 +292,21 @@
         totals = stats[:, 1, :]
         highest = jnp.max(peaks, axis=0, keepdims=True)
         total = jnp.sum(totals * jnp.exp(peaks - highest), axis=0, keepdims=True)
-        out_ref[g : g + 1, :] = highest + jnp.log(total)
-
-
-def sums_body(
-    place_ref, evid_ref, tail_a, tail_b, tail_c, tail_d, turned_a, turned_b, pay_ref, *tables
-):
-    total_rows = ROTATIONS * ROWS
-    near = place_ref[1]
-    lane = lanes_of((ROWS, LANES))
-    on_left = lane < HALF
-    weights, quads = [], []
-    for g, tail_ref in enumerate((tail_a, tail_b, tail_c, tail_d)):
-        table_ref = tables[g]
-        evidence = evid_ref[g : g + 1, :]
-        meta = tail_ref[0:ROWS, 0:LANES].astype(F32)
-        logits = tail_ref[0:ROWS, LANES:].astype(F32) + (
-            tail_ref[ROWS:, 0:LANES].astype(F32) + tail_ref[ROWS:, LANES:].astype(F32)
-        )
-        live, spot = row_facts(meta)
-        first, second, has_first, has_second = slots_of(live)
-        row_evidence = jnp.sum(jnp.where(spot, evidence, 0.0), axis=1, keepdims=True)
-        known = ((lane < ROTATIONS) & has_first) | (
-            (lane >= ROTATIONS) & (lane < 2 * ROTATIONS) & has_second
-        )
-        post = jnp.where(known, jnp.exp(logits - row_evidence), 0.0).astype(BF16).astype(F32)
-        first = first.astype(F32)
-        second = second.astype(F32)
+        evidence = highest + jnp.log(total)
+        if g == 0:
+            evid_ref[...] = evidence
+        first, second = facts_ref[0, :, :], facts_ref[1, :, :]
+        row_evidence = jnp.sum(
+            jnp.where(facts_ref[2, :, :] > 0.5, evidence, 0.0), axis=1, keepdims=True
+        )
+        post = jnp.where(
+            facts_ref[3, :, :] > 0.5, jnp.exp(facts_ref[4, :, :] - row_evidence), 0.0
+        )
+        post = post.astype(BF16).astype(F32)
         total_one = jnp.sum(jnp.where(lane < ROTATIONS, post, 0.0), axis=1, keepdims=True)
         total_two = jnp.sum(jnp.where(lane < ROTATIONS, 0.0, post), axis=1, keepdims=True)
         weights.append(total_one * first + total_two * second)
+        quads.append(facts_ref[5, :, :])
         half = ROTATIONS // 2
 
         def spread(r):
@@ -297,10 +321,10 @@
                 (r + half, jnp.where(on_left, there, here)),
             ):
                 value = value.astype(BF16)
-                table_ref[row * ROWS : (row + 1) * ROWS, :] = value
-                table_ref[total_rows + row * ROWS : total_rows + (row + 1) * ROWS, :] = value
-        quad = jnp.where(on_left, meta, 0.0)
-        quads.append(quad + pltpu.roll(quad, HALF, 1))
+                for turn in range(3):
+                    at = (turn * ROTATIONS + row) * ROWS
+                    if at + ROWS <= total_rows + DEPTH:
+                        table_ref[at : at + ROWS, :] = value
     weight = jnp.concatenate(weights, axis=0)
     quad = jnp.concatenate(quads, axis=0)
     by_class = jnp.dot(weight.T, quad, precision=HIGH, preferred_element_type=F32)
@@ -315,6 +339,10 @@
     for d in range(TARGETS):
         pay_ref[d, 0:HALF, :] = spare
         pay_ref[d, PAY_ROWS : PAY_ROWS + 16, :] = tail
+    copies = [
+        pltpu.make_async_copy(pay_ref.at[d], out_any.at[d], sems.at[d]) for d in range(TARGETS)
+    ]
+    started = 0
     base = (ROTATIONS - CHUNKS * near) * ROWS
     for b in range(CHUNKS):
         kept = [i for i in range(16) if (16 * b + i) // CHUNKS % 2 == 0]
@@ -325,18 +353,15 @@
             else:
                 bands.append([i, i + 1])
         start = pl.multiple_of(base - b * ROWS, ROWS)
-        out = jnp.zeros((16 * len(kept), LANES), F32)
-        for g, turned_ref in enumerate((turned_a, turned_b)):
-            left = jnp.concatenate([turned_ref[16 * lo : 16 * hi, :] for lo, hi in bands], axis=0)
-            right = jnp.concatenate(
-                [
-                    tables[2 * g][pl.ds(start, total_rows), :],
-                    tables[2 * g + 1][pl.ds(start, total_rows), :],
-                ],
-                axis=0,
-            )
-            out = out + jnp.dot(left, right, preferred_element_type=F32)
-        out = out.astype(BF16)
+        left = jnp.concatenate(
+            [
+                jnp.concatenate([ref[16 * lo : 16 * hi, :] for lo, hi in bands], axis=0)
+                for ref in all_turned
+            ],
+            axis=1,
+        )
+        right = jnp.concatenate([ref[pl.ds(start, DEPTH), :] for ref in tables], axis=0)
+        out = jnp.dot(left, right, preferred_element_type=F32).astype(BF16)
         for e in range(2):
             for n, i in enumerate(kept):
                 q = b * 16 + i
@@ -349,6 +374,13 @@
                 else:
                     pay_ref[d, PAY_ROWS - 8 : PAY_ROWS, 0:CLASSES] = piece[0:8, :]
                     pay_ref[d, PAY_ROWS - 8 : PAY_ROWS, HALF : HALF + CLASSES] = piece[8:16, :]
+        finished = (16 * b + 16 + CHUNKS) // (2 * CHUNKS)
+        for z in range(started, finished):
+            copies[z].start()
+            copies[8 + z].start()
+        started = finished
+    for copy in copies:
+        copy.wait()
 
 
 def final_body(parts_ref, sums_ref, weights_ref):
@@ -424,38 +456,38 @@
     )
     group_stats = swap(stats, ("xl", "core", "cls"))
     mine = call(bundle_body, shape((total_rows + 2 * ROWS, BLOCK), BF16), rows, logits)
-    beside = flip(mine, "xl")
-    sibling = flip(mine, "core")
-    across = lax.ppermute(mine, ("xl", "core"), [(0, 3), (1, 2), (2, 1), (3, 0)])
-
-    def turn(one, two):
+
+    def turn(value):
         return call(
             turn_body,
-            shape((BLOCK, 2 * total_rows), BF16),
+            (shape((BLOCK, DEPTH), BF16), shape((6, ROWS, LANES), F32)),
             place,
-            one,
-            two,
-            in_specs=[smem, vmem, vmem],
-        )
-
-    evidence = call(
-        evidence_body,
-        shape((4, LANES), F32),
+            value,
+            in_specs=[smem, vmem],
+        )
+
+    def trade(value):
+        beside = flip(value, "xl")
+        sibling = flip(value, "core")
+        across = flip(beside, "core")
+        return turn(value), turn(sibling), turn(beside), turn(across)
+
+    def alone(value):
+        return (turn(value),) * 4
+
+    turned, facts = zip(*lax.cond(place[0] < 2, trade, alone, mine))
+    pay, evidence = call(
+        sums_body,
+        (shape((TARGETS, PAY_ROWS + 16, LANES), BF16), shape((1, LANES), F32)),
         place,
         group_stats,
-        in_specs=[smem, vmem],
-        micros=MICROS,
-    )
-    pay = call(
-        sums_body,
-        shape((TARGETS, PAY_ROWS + 16, LANES), BF16),
-        place,
-        evidence,
-        *(value[total_rows:, :] for value in (mine, sibling, beside, across)),
-        turn(mine, sibling),
-        turn(beside, across),
-        in_specs=[smem] + [vmem] * 7,
-        scratch=[pltpu.VMEM((2 * total_rows, LANES), BF16)] * 4,
+        *facts,
+        *turned,
+        in_specs=[smem] + [vmem] * 9,
+        out_specs=(raw, vmem),
+        scratch=[pltpu.VMEM((TARGETS, PAY_ROWS + 16, LANES), BF16)]
+        + [pltpu.VMEM((total_rows + DEPTH, LANES), BF16)] * 4
+        + [pltpu.SemaphoreType.DMA((TARGETS,))],
     )
     parts = swap(pay, ("xh", "z"))
     sums, weight_sums = call(

time: 79.4 us -> 78.9 us (level)
  waiting for transfers between devices: 27.9 us -> 25.5 us
  starting transfers between devices: 35.1 us -> 36.3 us
  Pallas kernels: 12.6 us -> 13.4 us
    all_to_all x3, waiting for transfers between devices: 27.9 us -> 20.5 us  [swap(): return lax.all_to_all(value, axes, split_axis=0, concat_axis=0, tiled=True)]
    ppermute x1 -> x0, starting transfers between devices: 6.67 us -> none  [shards(): lax.ppermute(mine, ('xl', 'core'), [(0, 3), (1, 2), (2, 1), (3, 0)])]
    ppermute x2 -> x3, waiting for transfers between devices: 0.01 us -> 4.94 us  [flip(): return lax.ppermute(value, axis, [(0, 1), (1, 0)])]
    ppermute x2 -> x3, starting transfers between devices: 4.22 us -> 8.84 us  [flip(): return lax.ppermute(value, axis, [(0, 1), (1, 0)])]
    all_to_all x3, starting transfers between devices: 24.2 us -> 27.5 us  [swap(): return lax.all_to_all(value, axes, split_axis=0, concat_axis=0, tiled=True)]
    pallas_call x9 -> x10, Pallas kernels: 12.6 us -> 13.4 us  [call(): pl.pallas_call(body, out_shape=outs, scratch_shapes=list(scratch), compil...]
  transfers between devices with their start and end apart: 6 -> 6, of which waited for: 3 -> 3; matrix products, arithmetic and copies ran while one was open for 1% -> 1% of each run, Pallas kernels for 3% -> 6%
where the time goes in v4:
time: 78.9 us; the launch traced here: 77.9 us
  starting transfers between devices  36.3 us (46%)
  waiting for transfers between devices  25.5 us (32%)
  Pallas kernels  13.4 us (17%)
  local copies, waits for them, and re-layouts  1.91 us (2%)
    all_to_all x3, starting transfers between devices, swap(): return lax.all_to_all(value, axes, split_axis=0, concat_axis=0, tiled=True)  27.5 us
    all_to_all x3, waiting for transfers between devices, swap(): return lax.all_to_all(value, axes, split_axis=0, concat_axis=0, tiled=True)  20.5 us
    pallas_call x10, Pallas kernels, call(): pl.pallas_call(body, out_shape=outs, scratch_shapes=list(scratch), compil...  13.4 us
    ppermute x3, starting transfers between devices, flip(): return lax.ppermute(value, axis, [(0, 1), (1, 0)])  8.84 us
    ppermute x3, waiting for transfers between devices, flip(): return lax.ppermute(value, axis, [(0, 1), (1, 0)])  4.94 us
  transfers between devices with their start and end apart: 6, of which 3 were waited for; matrix products, arithmetic and copies ran while one was open for 1% of the time, Pallas kernels for 6%

profile of v4, /device:TPU:1, one launch (start us, length us, event | category | flops | bytes accessed | tf_op | source)
XLA Modules:
  0.0 77.9 jit_solution(15033938809174947653)
XLA Ops:
  0.6 2.0 %shard_map.76 = bf16[8,2,9344]{2,1,0:T(2,128)(2,1)} custom-call(bf16[4,9216]{1,0:T(4,128)(2,1)} %refs_0_.1, f32[4,64]{1,0:T(4,128)} %refs_1_.1, f32[1,64]{1,0:T(1,128)} %bitcast.8, s32[2,4]{1,0:T(2,128)} %bitcast.7), custom_call_target="tpu_custom_call" | custom-call | tf_op jit(solution)/shard_map/pallas_call | solution.py:41
  2.7 7.7 %all-to-all-start = ((bf16[8,2,9344]{2,1,0:T(2,128)(2,1)}), bf16[8,2,9344]{2,1,0:T(2,128)(2,1)S(1)}, u32[]{:S(2)}, u32[]{:S(2)}) async-start(bf16[8,2,9344]{2,1,0:T(2,128)(2,1)} %shard_map.76), calls=%async_computation | async-start | bytes 598016 | tf_op jit(solution)/shard_map/all_to_all | solution.py:418
  10.3 0.0 copy-start
  10.4 1.2 %copy-done = bf16[50,9216]{1,0:T(8,128)(2,1)S(1)} copy-done((bf16[50,9216]{1,0:T(8,128)(2,1)S(1)}, bf16[50,9216]{1,0:T(8,128)(2,1)}, u32[]{:S(2)}) %copy-start) | copy-done | bytes 921624
  11.6 0.3 shard_map.77
  11.9 8.4 %all-to-all-done = bf16[8,2,9344]{2,1,0:T(2,128)(2,1)S(1)} async-done(((bf16[8,2,9344]{2,1,0:T(2,128)(2,1)}), bf16[8,2,9344]{2,1,0:T(2,128)(2,1)S(1)}, u32[]{:S(2)}, u32[]{:S(2)}) %all-to-all-start) | async-done | bytes 299040 | tf_op jit(solution)/shard_map/all_to_all | solution.py:418
  20.3 0.1 reshape.16.rows_ref
  20.4 1.9 %shard_map.78 = (f32[576,128]{1,0:T(8,128)S(1)}, f32[32,2,128]{2,1,0:T(2,128)}) custom-call(bf16[16,9344]{1,0:T(8,128)(2,1)S(1)} %reshape.16.rows_ref, bf16[2304,256]{1,0:T(8,128)(2,1)S(1)} %get-tuple-element.41.table_ref, f32[128,128]{1,0:T(8,128)S(1)} %get-tuple-element.42.energy_ref), custom_call_target="tpu_custom_call" | custom-call | tf_op jit(solution)/shard_map/pallas_call | solution.py:41
  22.4 7.2 %all-to-all-start.1 = ((f32[32,2,128]{2,1,0:T(2,128)}), f32[32,2,128]{2,1,0:T(2,128)S(1)}, u32[]{:S(2)}, u32[]{:S(2)}) async-start(f32[32,2,128]{2,1,0:T(2,128)} %get-tuple-element.43), calls=%async_computation.1 | async-start | bytes 65536 | tf_op jit(solution)/shard_map/all_to_all | solution.py:418
  29.6 0.1 pad_add_fusion.place_ref
  29.7 0.4 shard_map.79
  30.1 17.8 %conditional.1 = (bf16[256,640]{1,0:T(8,128)(2,1)S(1)}, f32[6,16,128]{2,1,0:T(8,128)S(1)}, bf16[256,640]{1,0:T(8,128)(2,1)S(1)}, f32[6,16,128]{2,1,0:T(8,128)S(1...) conditional(s32[]{:T(128)} %convert_element_type.3, ...), branch_computations={%region_0.0_spmd, %region_1.0_spmd} | conditional | bytes 3735736 | solution.py:478
  30.1 3.4 %collective-permute-start.1 = (bf16[608,256]{1,0:T(8,128)(2,1)S(1)}, bf16[608,256]{1,0:T(8,128)(2,1)S(1)}, u32[]{:S(2)}, u32[]{:S(2)}) collective-permute-start(bf16[608,256]{1,0:T(8,128)(2,1)S(1)} %get-tuple-element.13.blocks_ref), channel_id=1, source_target_pairs={{0,128},{128,0},{1,129},{129,1},{2,130},{130,2},{3,131},{131,3},{4... | collective-permute-start | bytes 933896 | tf_op jit(solution)/shard_map/cond/branch_1_fun/ppermute | solution.py:421
  33.4 2.5 %collective-permute-start = (bf16[608,256]{1,0:T(8,128)(2,1)S(1)}, bf16[608,256]{1,0:T(8,128)(2,1)S(1)}, u32[]{:S(2)}, u32[]{:S(2)}) collective-permute-start(bf16[608,256]{1,0:T(8,128)(2,1)S(1)} %get-tuple-element.13.blocks_ref), channel_id=1, source_target_pairs={{0,8},{8,0},{1,9},{9,1},{2,10},{10,2},{3,11},{11,3},{4,12},{12,4},... | collective-permute-start | bytes 933896 | tf_op jit(solution)/shard_map/cond/branch_1_fun/ppermute | solution.py:421
  36.0 4.9 %collective-permute-done.1.blocks_ref = bf16[608,256]{1,0:T(8,128)(2,1)S(1)} collective-permute-done((bf16[608,256]{1,0:T(8,128)(2,1)S(1)}, bf16[608,256]{1,0:T(8,128)(2,1)S(1)}, u32[]{:S(2)}, u32[]{:S(2)}) %collective-permute-start.1) | collective-permute-done | bytes 311328 | tf_op jit(solution)/shard_map/cond/branch_1_fun/ppermute | solution.py:421
  40.9 2.9 %collective-permute-start.2 = (bf16[608,256]{1,0:T(8,128)(2,1)S(1)}, bf16[608,256]{1,0:T(8,128)(2,1)S(1)}, u32[]{:S(2)}, u32[]{:S(2)}) collective-permute-start(bf16[608,256]{1,0:T(8,128)(2,1)S(1)} %collective-permute-done.1.blocks_ref), channel_id=1, source_target_pairs={{0,8},{8,0},{1,9},{9,1},{2,10},{10,2},{3,11},{11,3},{4,12},{12,4},... | collective-permute-start | bytes 933896 | tf_op jit(solution)/shard_map/cond/branch_1_fun/ppermute | solution.py:421
  43.9 1.0 %branch_1_fun.4 = (bf16[256,640]{1,0:T(8,128)(2,1)S(1)}, f32[6,16,128]{2,1,0:T(8,128)S(1)}) custom-call(s32[2]{0:T(128)S(1)} %get-tuple-element.12.place_ref, bf16[608,256]{1,0:T(8,128)(2,1)S(1)} %get-tuple-element.13.blocks_ref), custom_call_target="tpu_custom_call" | custom-call | tf_op jit(solution)/shard_map/cond/branch_1_fun/pallas_call | solution.py:41
  44.9 1.0 %branch_1_fun.6 = (bf16[256,640]{1,0:T(8,128)(2,1)S(1)}, f32[6,16,128]{2,1,0:T(8,128)S(1)}) custom-call(s32[2]{0:T(128)S(1)} %get-tuple-element.12.place_ref, bf16[608,256]{1,0:T(8,128)(2,1)S(1)} %collective-permute-done.1.blocks_ref), custom_call_target="tpu_custom_call" | custom-call | tf_op jit(solution)/shard_map/cond/branch_1_fun/pallas_call | solution.py:41
  45.9 0.0 collective-permute-done.blocks_ref
  45.9 1.0 %branch_1_fun.5 = (bf16[256,640]{1,0:T(8,128)(2,1)S(1)}, f32[6,16,128]{2,1,0:T(8,128)S(1)}) custom-call(s32[2]{0:T(128)S(1)} %get-tuple-element.12.place_ref, bf16[608,256]{1,0:T(8,128)(2,1)S(1)} %collective-permute-done.blocks_ref), custom_call_target="tpu_custom_call" | custom-call | tf_op jit(solution)/shard_map/cond/branch_1_fun/pallas_call | solution.py:41
  46.9 0.0 collective-permute-done.2.blocks_ref
  46.9 1.0 %branch_1_fun.7 = (bf16[256,640]{1,0:T(8,128)(2,1)S(1)}, f32[6,16,128]{2,1,0:T(8,128)S(1)}) custom-call(s32[2]{0:T(128)S(1)} %get-tuple-element.12.place_ref, bf16[608,256]{1,0:T(8,128)(2,1)S(1)} %collective-permute-done.2.blocks_ref), custom_call_target="tpu_custom_call" | custom-call | tf_op jit(solution)/shard_map/cond/branch_1_fun/pallas_call | solution.py:41
  47.9 0.0 all-to-all-done.1.stats_ref
  47.9 3.9 %shard_map.80 = (bf16[16,88,128]{2,1,0:T(8,128)(2,1)}, f32[1,128]{1,0:T(1,128)S(1)}) custom-call(s32[2]{0:T(128)S(1)} %pad_add_fusion.place_ref, f32[32,2,128]{2,1,0:T(2,128)S(1)} %all-to-all-done.1.stats_ref, f32[6,16,128]{2,1,0:T(8,128)S(1)} %get-tuple-element.45.facts_a, f32[6,16,128]{2,1,0:T(8,128)S(1)} %get-tuple-element.46.facts_b, ...), custom_call_target="tpu_custom_call" | custom-call | tf_op jit(solution)/shard_map/pallas_call | solution.py:41
  51.8 12.6 %all-to-all-start.2 = ((bf16[16,88,128]{2,1,0:T(8,128)(2,1)}), bf16[16,88,128]{2,1,0:T(8,128)(2,1)S(1)}, u32[]{:S(2)}, u32[]{:S(2)}) async-start(bf16[16,88,128]{2,1,0:T(8,128)(2,1)} %get-tuple-element.53), calls=%async_computation.2 | async-start | bytes 720896 | tf_op jit(solution)/shard_map/all_to_all | solution.py:418
  64.4 0.6 dynamic-slice_bitcast_fusion
  65.0 12.1 %all-to-all-done.2.parts_ref = bf16[16,88,128]{2,1,0:T(8,128)(2,1)S(1)} async-done(((bf16[16,88,128]{2,1,0:T(8,128)(2,1)}), bf16[16,88,128]{2,1,0:T(8,128)(2,1)S(1)}, u32[]{:S(2)}, u32[]{:S(2)}) %all-to-all-start.2) | async-done | bytes 360480 | tf_op jit(solution)/shard_map/all_to_all | solution.py:418
  77.1 0.8 %shard_map.81 = (f32[50,144]{1,0:T(8,128)}, f32[50,64]{1,0:T(8,128)}) custom-call(bf16[16,88,128]{2,1,0:T(8,128)(2,1)S(1)} %all-to-all-done.2.parts_ref), custom_call_target="tpu_custom_call" | custom-call | tf_op jit(solution)/shard_map/pallas_call | solution.py:41
Async XLA Ops:
  2.7 17.6 %all-to-all-start = ((bf16[8,2,9344]{2,1,0:T(2,128)(2,1)}), bf16[8,2,9344]{2,1,0:T(2,128)(2,1)S(1)}, u32[]{:S(2)}, u32[]{:S(2)}) async-start(bf16[8,2,9344]{2,1,0:T(2,128)(2,1)} %shard_map.76), calls=%async_computation | async-start | bytes 598016 | tf_op jit(solution)/shard_map/all_to_all | solution.py:418
  10.3 1.2 %copy-start = (bf16[50,9216]{1,0:T(8,128)(2,1)S(1)}, bf16[50,9216]{1,0:T(8,128)(2,1)}, u32[]{:S(2)}) copy-start(bf16[50,9216]{1,0:T(8,128)(2,1)} %classes_ref.1) | copy-start | bytes 2764804
  22.4 25.5 %all-to-all-start.1 = ((f32[32,2,128]{2,1,0:T(2,128)}), f32[32,2,128]{2,1,0:T(2,128)S(1)}, u32[]{:S(2)}, u32[]{:S(2)}) async-start(f32[32,2,128]{2,1,0:T(2,128)} %get-tuple-element.43), calls=%async_computation.1 | async-start | bytes 65536 | tf_op jit(solution)/shard_map/all_to_all | solution.py:418
  30.1 10.8 %collective-permute-start.1 = (bf16[608,256]{1,0:T(8,128)(2,1)S(1)}, bf16[608,256]{1,0:T(8,128)(2,1)S(1)}, u32[]{:S(2)}, u32[]{:S(2)}) collective-permute-start(bf16[608,256]{1,0:T(8,128)(2,1)S(1)} %get-tuple-element.13.blocks_ref), channel_id=1, source_target_pairs={{0,128},{128,0},{1,129},{129,1},{2,130},{130,2},{3,131},{131,3},{4... | collective-permute-start | bytes 933896 | tf_op jit(solution)/shard_map/cond/branch_1_fun/ppermute | solution.py:421
  33.4 12.4 %collective-permute-start = (bf16[608,256]{1,0:T(8,128)(2,1)S(1)}, bf16[608,256]{1,0:T(8,128)(2,1)S(1)}, u32[]{:S(2)}, u32[]{:S(2)}) collective-permute-start(bf16[608,256]{1,0:T(8,128)(2,1)S(1)} %get-tuple-element.13.blocks_ref), channel_id=1, source_target_pairs={{0,8},{8,0},{1,9},{9,1},{2,10},{10,2},{3,11},{11,3},{4,12},{12,4},... | collective-permute-start | bytes 933896 | tf_op jit(solution)/shard_map/cond/branch_1_fun/ppermute | solution.py:421
  40.9 6.0 %collective-permute-start.2 = (bf16[608,256]{1,0:T(8,128)(2,1)S(1)}, bf16[608,256]{1,0:T(8,128)(2,1)S(1)}, u32[]{:S(2)}, u32[]{:S(2)}) collective-permute-start(bf16[608,256]{1,0:T(8,128)(2,1)S(1)} %collective-permute-done.1.blocks_ref), channel_id=1, source_target_pairs={{0,8},{8,0},{1,9},{9,1},{2,10},{10,2},{3,11},{11,3},{4,12},{12,4},... | collective-permute-start | bytes 933896 | tf_op jit(solution)/shard_map/cond/branch_1_fun/ppermute | solution.py:421
  51.8 25.4 %all-to-all-start.2 = ((bf16[16,88,128]{2,1,0:T(8,128)(2,1)}), bf16[16,88,128]{2,1,0:T(8,128)(2,1)S(1)}, u32[]{:S(2)}, u32[]{:S(2)}) async-start(bf16[16,88,128]{2,1,0:T(8,128)(2,1)} %get-tuple-element.53), calls=%async_computation.2 | async-start | bytes 720896 | tf_op jit(solution)/shard_map/all_to_all | solution.py:418

commit v5 on v4

--- a/solution.py
+++ b/solution.py
@@ -14,7 +14,7 @@
 ROWS = 16
 GROUPS = 64
 TARGETS = GROUPS // 4
-DEPTH = 640
+DEPTH = 2 * ROTATIONS * ROWS
 CLASSES = 50
 SLICE = FEATURES // GROUPS
 CHUNKS = SLICE // 16
@@ -138,7 +138,7 @@
     marks = jnp.where(lane >= P_LANE, meta, 0.0)
     valid = jnp.sum(marks, axis=1, keepdims=True)
     own = jnp.sum(marks * (lane - P_LANE).astype(F32), axis=1, keepdims=True)
-    source = (rows_of(meta.shape) // 2 * 4).astype(F32)
+    source = (rows_of(meta.shape) % ROWS // 2 * 4).astype(F32)
     spot = (lane.astype(F32) == source + own) & (valid > 0.5)
     return flags, spot
 
@@ -152,7 +152,7 @@
     return ids == low, ids == high, low < 999.0, high > -0.5
 
 
-def cross_body(rows_ref, table_ref, energy_ref, logits_ref, stats_ref, blocks_ref, acc_ref):
+def correlate(rows_ref, table_ref, energy_ref, logits_ref, blocks_ref, acc_ref):
     total_rows = ROTATIONS * ROWS
     for b in range(ROTATIONS):
         blocks_ref[b * ROWS : (b + 1) * ROWS, :] = rows_ref[:, b * BLOCK : (b + 1) * BLOCK]
@@ -173,13 +173,10 @@
                 acc_ref[total_rows - shift :, :] += tile[:shift, :]
     meta = rows_ref[:, FEATURES : FEATURES + LANES].astype(F32)
     lane = lanes_of((ROWS, LANES))
-    live, spot = row_facts(meta)
     quad = jnp.where(lane < HALF, meta, 0.0)
     norm = 0.5 * lax.dot_general(
         quad, energy_ref[...], (((1,), (1,)), ((), ())), precision=HIGH, preferred_element_type=F32
     )
-    left = live & (lane < HALF)
-    best = jnp.full((ROWS, LANES), NEGATIVE, F32)
     for r in range(ROTATIONS):
         nxt = (r + 1) % ROTATIONS
         mixed = jnp.where(
@@ -187,8 +184,18 @@
             acc_ref[r * ROWS : (r + 1) * ROWS, :],
             acc_ref[nxt * ROWS : (nxt + 1) * ROWS, :],
         )
-        value = mixed + pltpu.roll(mixed, HALF, 1) - norm
-        logits_ref[r * ROWS : (r + 1) * ROWS, :] = value
+        logits_ref[r * ROWS : (r + 1) * ROWS, :] = mixed + pltpu.roll(mixed, HALF, 1) - norm
+
+
+def cross_body(rows_ref, table_ref, energy_ref, logits_ref, stats_ref, blocks_ref, acc_ref):
+    correlate(rows_ref, table_ref, energy_ref, logits_ref, blocks_ref, acc_ref)
+    meta = rows_ref[:, FEATURES : FEATURES + LANES].astype(F32)
+    lane = lanes_of((ROWS, LANES))
+    live, spot = row_facts(meta)
+    left = live & (lane < HALF)
+    best = jnp.full((ROWS, LANES), NEGATIVE, F32)
+    for r in range(ROTATIONS):
+        value = logits_ref[r * ROWS : (r + 1) * ROWS, :]
         best = jnp.maximum(best, jnp.where(left, value, NEGATIVE))
     peak = jnp.max(best, axis=1, keepdims=True)
     total = jnp.zeros((ROWS, LANES), F32)
@@ -203,90 +210,76 @@
         stats_ref[d, 1:2, :] = total_row
 
 
-def bundle_body(rows_ref, logits_ref, out_ref):
-    total_rows = ROTATIONS * ROWS
+def share_body(place_ref, one_ref, two_ref, one_logits_ref, two_logits_ref, mine_ref, theirs_ref):
+    second = place_ref[0] == 1
+    pieces = []
     for b in range(ROTATIONS):
-        out_ref[b * ROWS : (b + 1) * ROWS, :] = rows_ref[:, b * BLOCK : (b + 1) * BLOCK]
-    raw = rows_ref[:, FEATURES : FEATURES + LANES]
-    live, _ = row_facts(raw.astype(F32))
-    lane = lanes_of((ROWS, LANES))
-    first, second, _, _ = slots_of(live & (lane < HALF))
-    first = first & (lane < HALF)
-    second = second & (lane < HALF)
-    compact = jnp.zeros((ROWS, LANES), F32)
+        for ref in (one_ref, two_ref):
+            pieces.append(ref[:, b * BLOCK : (b + 1) * BLOCK])
+    value = jnp.concatenate(pieces, axis=0).astype(F32)
+    rolled = pltpu.roll(value, BLOCK - SLICE, 1)
+    after = jnp.concatenate([rolled[2 * ROWS :, :], rolled[: 2 * ROWS, :]], axis=0)
+    moved = jnp.where(lanes_of(value.shape) < BLOCK - SLICE, rolled, after)
+    mine_ref[0:BLOCK, :] = jnp.where(second, moved, value).T.astype(BF16)
+    theirs_ref[0:BLOCK, :] = jnp.where(second, value, moved).T.astype(BF16)
+    columns = slice(FEATURES, FEATURES + LANES)
+    meta = jnp.concatenate([one_ref[:, columns], two_ref[:, columns]], axis=0).astype(F32)
+    lane = lanes_of(meta.shape)
+    live, spot = row_facts(meta)
+    first, other, has_first, has_other = slots_of(live)
+    known = ((lane < ROTATIONS) & has_first) | (
+        (lane >= ROTATIONS) & (lane < 2 * ROTATIONS) & has_other
+    )
+    quad = jnp.where(lane < HALF, meta, 0.0)
+    quad = quad + pltpu.roll(quad, HALF, 1)
+    one_mask = first & (lane < HALF)
+    two_mask = other & (lane < HALF)
+    compact = jnp.zeros(meta.shape, F32)
     for r in range(ROTATIONS):
-        value = logits_ref[r * ROWS : (r + 1) * ROWS, :]
-        one = jnp.sum(jnp.where(first, value, 0.0), axis=1, keepdims=True)
-        two = jnp.sum(jnp.where(second, value, 0.0), axis=1, keepdims=True)
+        own = slice(r * ROWS, (r + 1) * ROWS)
+        level = jnp.concatenate([one_logits_ref[own, :], two_logits_ref[own, :]], axis=0)
+        one = jnp.sum(jnp.where(one_mask, level, 0.0), axis=1, keepdims=True)
+        two = jnp.sum(jnp.where(two_mask, level, 0.0), axis=1, keepdims=True)
         compact = jnp.where(lane == r, one, jnp.where(lane == ROTATIONS + r, two, compact))
     high = compact.astype(BF16)
-    rest = compact - high.astype(F32)
-    middle = rest.astype(BF16)
-    rest = rest - middle.astype(F32)
-    out_ref[total_rows : total_rows + ROWS, 0:LANES] = raw
-    out_ref[total_rows : total_rows + ROWS, LANES:] = high
-    out_ref[total_rows + ROWS :, 0:LANES] = middle
-    out_ref[total_rows + ROWS :, LANES:] = rest.astype(BF16)
-
-
-def turn_body(place_ref, blocks_ref, turned_ref, facts_ref):
-    total_rows = ROTATIONS * ROWS
-    second = place_ref[0] == 1
-    value = blocks_ref[0:total_rows, :].astype(F32)
-    rolled = pltpu.roll(value, BLOCK - SLICE, 1)
-    after = jnp.concatenate([rolled[ROWS:, :], rolled[:ROWS, :]], axis=0)
-    moved = jnp.where(lanes_of(value.shape) < BLOCK - SLICE, rolled, after)
-    value = jnp.where(second, moved, value)
-    turned_ref[:, 0:total_rows] = value.T.astype(BF16)
-    turned_ref[:, total_rows:] = jnp.zeros((BLOCK, DEPTH - total_rows), BF16)
-    lane = lanes_of((ROWS, LANES))
-    meta = blocks_ref[total_rows : total_rows + ROWS, 0:LANES].astype(F32)
-    logits = blocks_ref[total_rows : total_rows + ROWS, LANES:].astype(F32) + (
-        blocks_ref[total_rows + ROWS :, 0:LANES].astype(F32)
-        + blocks_ref[total_rows + ROWS :, LANES:].astype(F32)
-    )
-    live, spot = row_facts(meta)
-    first, second, has_first, has_second = slots_of(live)
-    known = ((lane < ROTATIONS) & has_first) | (
-        (lane >= ROTATIONS) & (lane < 2 * ROTATIONS) & has_second
-    )
-    quad = jnp.where(lane < HALF, meta, 0.0)
-    quad = quad + pltpu.roll(quad, HALF, 1)
-    for i, fact in enumerate((first, second, spot, known, logits, quad)):
-        facts_ref[i, :, :] = fact.astype(F32)
+    left = compact - high.astype(F32)
+    middle = left.astype(BF16)
+    left = left - middle.astype(F32)
+    for i, fact in enumerate((first, other, spot, known, quad, high, middle, left)):
+        fact = fact.astype(F32).astype(BF16)
+        for ref in (mine_ref, theirs_ref):
+            ref[BLOCK:, i * LANES : (i + 1) * LANES] = fact
+    for ref in (mine_ref, theirs_ref):
+        ref[BLOCK:, 8 * LANES :] = jnp.zeros((2 * ROWS, DEPTH - 8 * LANES), BF16)
 
 
 def sums_body(
-    place_ref,
-    stats_ref,
-    facts_a,
-    facts_b,
-    facts_c,
-    facts_d,
-    turned_a,
-    turned_b,
-    turned_c,
-    turned_d,
-    out_any,
-    evid_ref,
-    pay_ref,
-    table_a,
-    table_b,
-    table_c,
-    table_d,
-    sems,
+    place_ref, stats_ref, mine_ref, other_any, out_any, evid_ref, pay_ref, other_ref, table_a, table_b, sems
 ):
-    total_rows = ROTATIONS * ROWS
+    fetch_facts = pltpu.make_async_copy(
+        other_any.at[pl.ds(BLOCK, 2 * ROWS), :], other_ref.at[pl.ds(BLOCK, 2 * ROWS), :], sems.at[TARGETS]
+    )
+    fetch_turned = pltpu.make_async_copy(
+        other_any.at[pl.ds(0, BLOCK), :], other_ref.at[pl.ds(0, BLOCK), :], sems.at[TARGETS + 1]
+    )
+    fetch_facts.start()
+    fetch_turned.start()
     core, near = place_ref[0], place_ref[1]
-    all_facts = (facts_a, facts_b, facts_c, facts_d)
-    all_turned = (turned_a, turned_b, turned_c, turned_d)
-    tables = (table_a, table_b, table_c, table_d)
+    tables = (table_a, table_b)
     lane = lanes_of((ROWS, LANES))
     on_left = lane < HALF
     weights, quads = [], []
-    for g, (facts_ref, table_ref) in enumerate(zip(all_facts, tables)):
-        at_core = core if g % 2 == 0 else 1 - core
-        at_near = near if g < 2 else 1 - near
+    for g in range(4):
+        if g == 2:
+            fetch_facts.wait()
+        facts_ref, table_ref = (mine_ref, other_ref)[g // 2], tables[g // 2]
+
+        def fact(i):
+            at = BLOCK + g % 2 * ROWS
+            return facts_ref[at : at + ROWS, i * LANES : (i + 1) * LANES].astype(F32)
+
+        at_core = core if g < 2 else 1 - core
+        at_near = near if g % 2 == 0 else 1 - near
         stats = stats_ref[pl.ds((at_near * 2 + at_core) * 8, 8), :, :]
         peaks = stats[:, 0, :]
         totals = stats[:, 1, :]
@@ -295,18 +288,17 @@
         evidence = highest + jnp.log(total)
         if g == 0:
             evid_ref[...] = evidence
-        first, second = facts_ref[0, :, :], facts_ref[1, :, :]
+        first, second = fact(0), fact(1)
         row_evidence = jnp.sum(
-            jnp.where(facts_ref[2, :, :] > 0.5, evidence, 0.0), axis=1, keepdims=True
-        )
-        post = jnp.where(
-            facts_ref[3, :, :] > 0.5, jnp.exp(facts_ref[4, :, :] - row_evidence), 0.0
-        )
+            jnp.where(fact(2) > 0.5, evidence, 0.0), axis=1, keepdims=True
+        )
+        logits = fact(5) + (fact(6) + fact(7))
+        post = jnp.where(fact(3) > 0.5, jnp.exp(logits - row_evidence), 0.0)
         post = post.astype(BF16).astype(F32)
         total_one = jnp.sum(jnp.where(lane < ROTATIONS, post, 0.0), axis=1, keepdims=True)
         total_two = jnp.sum(jnp.where(lane < ROTATIONS, 0.0, post), axis=1, keepdims=True)
         weights.append(total_one * first + total_two * second)
-        quads.append(facts_ref[5, :, :])
+        quads.append(fact(4))
         half = ROTATIONS // 2
 
         def spread(r):
@@ -321,10 +313,9 @@
                 (r + half, jnp.where(on_left, there, here)),
             ):
                 value = value.astype(BF16)
-                for turn in range(3):
-                    at = (turn * ROTATIONS + row) * ROWS
-                    if at + ROWS <= total_rows + DEPTH:
-                        table_ref[at : at + ROWS, :] = value
+                for turn in range(2):
+                    at = ((turn * ROTATIONS + row) * 2 + g % 2) * ROWS
+                    table_ref[at : at + ROWS, :] = value
     weight = jnp.concatenate(weights, axis=0)
     quad = jnp.concatenate(quads, axis=0)
     by_class = jnp.dot(weight.T, quad, precision=HIGH, preferred_element_type=F32)
@@ -343,38 +334,46 @@
         pltpu.make_async_copy(pay_ref.at[d], out_any.at[d], sems.at[d]) for d in range(TARGETS)
     ]
     started = 0
-    base = (ROTATIONS - CHUNKS * near) * ROWS
-    for b in range(CHUNKS):
-        kept = [i for i in range(16) if (16 * b + i) // CHUNKS % 2 == 0]
+    fetch_turned.wait()
+    base = (ROTATIONS - CHUNKS * near) * 2 * ROWS
+    for group in ((0, 1), (2, 3), (4, 5), (6, 7), (8,)):
+        kept = {b: [i for i in range(16) if (16 * b + i) // CHUNKS % 2 == 0] for b in group}
+        used = sorted(set(i for b in group for i in kept[b]))
         bands = []
-        for i in kept:
+        for i in used:
             if bands and bands[-1][1] == i:
                 bands[-1][1] = i + 1
             else:
                 bands.append([i, i + 1])
-        start = pl.multiple_of(base - b * ROWS, ROWS)
         left = jnp.concatenate(
             [
                 jnp.concatenate([ref[16 * lo : 16 * hi, :] for lo, hi in bands], axis=0)
-                for ref in all_turned
+                for ref in (mine_ref, other_ref)
             ],
             axis=1,
         )
-        right = jnp.concatenate([ref[pl.ds(start, DEPTH), :] for ref in tables], axis=0)
+        columns = []
+        for b in group:
+            start = pl.multiple_of(base - b * 2 * ROWS, 2 * ROWS)
+            columns.append(jnp.concatenate([ref[pl.ds(start, DEPTH), :] for ref in tables], axis=0))
+        right = jnp.concatenate(columns, axis=1)
         out = jnp.dot(left, right, preferred_element_type=F32).astype(BF16)
-        for e in range(2):
-            for n, i in enumerate(kept):
-                q = b * 16 + i
-                d, j = e * 8 + q // CHUNKS // 2, q % CHUNKS
-                piece = out[n * 16 : (n + 1) * 16, e * HALF : e * HALF + CLASSES]
-                if j < CHUNKS - 1:
-                    at = j // 2 * 16
-                    lo = j % 2 * HALF
-                    pay_ref[d, at : at + 16, lo : lo + CLASSES] = piece
-                else:
-                    pay_ref[d, PAY_ROWS - 8 : PAY_ROWS, 0:CLASSES] = piece[0:8, :]
-                    pay_ref[d, PAY_ROWS - 8 : PAY_ROWS, HALF : HALF + CLASSES] = piece[8:16, :]
-        finished = (16 * b + 16 + CHUNKS) // (2 * CHUNKS)
+        for c, b in enumerate(group):
+            for i in kept[b]:
+                n = used.index(i)
+                for e in range(2):
+                    q = b * 16 + i
+                    d, j = e * 8 + q // CHUNKS // 2, q % CHUNKS
+                    from_lane = c * LANES + e * HALF
+                    piece = out[n * 16 : (n + 1) * 16, from_lane : from_lane + CLASSES]
+                    if j < CHUNKS - 1:
+                        at = j // 2 * 16
+                        lo = j % 2 * HALF
+                        pay_ref[d, at : at + 16, lo : lo + CLASSES] = piece
+                    else:
+                        pay_ref[d, PAY_ROWS - 8 : PAY_ROWS, 0:CLASSES] = piece[0:8, :]
+                        pay_ref[d, PAY_ROWS - 8 : PAY_ROWS, HALF : HALF + CLASSES] = piece[8:16, :]
+        finished = (16 * group[-1] + 16 + CHUNKS) // (2 * CHUNKS)
         for z in range(started, finished):
             copies[z].start()
             copies[8 + z].start()
@@ -446,6 +445,8 @@
         (shape((ROTATIONS * HALF, BLOCK), BF16), shape((LANES, LANES), F32)),
         classes,
     )
+    rows, table, energy = lax.optimization_barrier((rows, table, energy))
+    beside = flip(rows, "xl")
     logits, stats = call(
         cross_body,
         (shape((total_rows, LANES), F32), shape((32, 2, LANES), F32)),
@@ -455,39 +456,51 @@
         scratch=[pltpu.VMEM((total_rows, BLOCK), BF16), pltpu.VMEM((total_rows, LANES), F32)],
     )
     group_stats = swap(stats, ("xl", "core", "cls"))
-    mine = call(bundle_body, shape((total_rows + 2 * ROWS, BLOCK), BF16), rows, logits)
-
-    def turn(value):
-        return call(
-            turn_body,
-            (shape((BLOCK, DEPTH), BF16), shape((6, ROWS, LANES), F32)),
+
+    shared = shape((BLOCK + 2 * ROWS, DEPTH), BF16)
+
+    def trade(one, two, one_logits):
+        two_logits = call(
+            correlate,
+            shape((total_rows, LANES), F32),
+            two,
+            table,
+            energy,
+            scratch=[pltpu.VMEM((total_rows, BLOCK), BF16), pltpu.VMEM((total_rows, LANES), F32)],
+        )
+        own, theirs = call(
+            share_body,
+            (shared, shared),
             place,
-            value,
-            in_specs=[smem, vmem],
-        )
-
-    def trade(value):
-        beside = flip(value, "xl")
-        sibling = flip(value, "core")
-        across = flip(beside, "core")
-        return turn(value), turn(sibling), turn(beside), turn(across)
-
-    def alone(value):
-        return (turn(value),) * 4
-
-    turned, facts = zip(*lax.cond(place[0] < 2, trade, alone, mine))
+            one,
+            two,
+            one_logits,
+            two_logits,
+            in_specs=[smem] + [vmem] * 4,
+        )
+        return own, flip(theirs, "core")
+
+    def alone(one, two, one_logits):
+        nothing = jnp.zeros(shared.shape, BF16)
+        return nothing, nothing
+
+    own_share, other_share = lax.cond(place[0] < 2, trade, alone, rows, beside, logits)
     pay, evidence = call(
         sums_body,
         (shape((TARGETS, PAY_ROWS + 16, LANES), BF16), shape((1, LANES), F32)),
         place,
         group_stats,
-        *facts,
-        *turned,
-        in_specs=[smem] + [vmem] * 9,
+        own_share,
+        pltpu.with_memory_space_constraint(other_share, pltpu.HBM),
+        in_specs=[smem, vmem, vmem, raw],
         out_specs=(raw, vmem),
-        scratch=[pltpu.VMEM((TARGETS, PAY_ROWS + 16, LANES), BF16)]
-        + [pltpu.VMEM((total_rows + DEPTH, LANES), BF16)] * 4
-        + [pltpu.SemaphoreType.DMA((TARGETS,))],
+        scratch=[
+            pltpu.VMEM((TARGETS, PAY_ROWS + 16, LANES), BF16),
+            pltpu.VMEM(shared.shape, BF16),
+            pltpu.VMEM((2 * DEPTH, LANES), BF16),
+            pltpu.VMEM((2 * DEPTH, LANES), BF16),
+            pltpu.SemaphoreType.DMA((TARGETS + 2,)),
+        ],
     )
     parts = swap(pay, ("xh", "z"))
     sums, weight_sums = call(

time: 78.9 us -> 71.6 us (0.907)
  starting transfers between devices: 36.3 us -> 32.8 us
  waiting for transfers between devices: 25.5 us -> 23 us
  Pallas kernels: 13.4 us -> 12.1 us
    ppermute x3 -> x2, waiting for transfers between devices: 4.94 us -> 1.92 us  [flip(): return lax.ppermute(value, axis, [(0, 1), (1, 0)])]
    ppermute x3 -> x2, starting transfers between devices: 8.84 us -> 6.63 us  [flip(): return lax.ppermute(value, axis, [(0, 1), (1, 0)])]
    all_to_all x3, starting transfers between devices: 27.5 us -> 26.2 us  [swap(): return lax.all_to_all(value, axes, split_axis=0, concat_axis=0, tiled=True)]
    pallas_call x10 -> x7, Pallas kernels: 13.4 us -> 12.1 us  [call(): pl.pallas_call(body, out_shape=outs, scratch_shapes=list(scratch), compil...]
  transfers between devices with their start and end apart: 6 -> 5, of which waited for: 3 -> 4; matrix products, arithmetic and copies ran while one was open for 1% -> 1% of each run, Pallas kernels for 6% -> 7%
where the time goes in v5:
time: 71.6 us; the launch traced here: 70.6 us
  starting transfers between devices  32.8 us (46%)
  waiting for transfers between devices  23 us (32%)
  Pallas kernels  12.1 us (17%)
  local copies, waits for them, and re-layouts  1.91 us (3%)
    all_to_all x3, starting transfers between devices, swap(): return lax.all_to_all(value, axes, split_axis=0, concat_axis=0, tiled=True)  26.2 us
    all_to_all x3, waiting for transfers between devices, swap(): return lax.all_to_all(value, axes, split_axis=0, concat_axis=0, tiled=True)  21.1 us
    pallas_call x7, Pallas kernels, call(): pl.pallas_call(body, out_shape=outs, scratch_shapes=list(scratch), compil...  12.1 us
    ppermute x2, starting transfers between devices, flip(): return lax.ppermute(value, axis, [(0, 1), (1, 0)])  6.63 us
    ppermute x2, waiting for transfers between devices, flip(): return lax.ppermute(value, axis, [(0, 1), (1, 0)])  1.92 us
  transfers between devices with their start and end apart: 5, of which 4 were waited for; matrix products, arithmetic and copies ran while one was open for 1% of the time, Pallas kernels for 7%

profile of v5, /device:TPU:1, one launch (start us, length us, event | category | flops | bytes accessed | tf_op | source)
XLA Modules:
  0.0 70.6 jit_solution(6988955431860214918)
XLA Ops:
  0.6 2.0 %shard_map.76 = bf16[8,2,9344]{2,1,0:T(2,128)(2,1)} custom-call(bf16[4,9216]{1,0:T(4,128)(2,1)} %refs_0_.1, f32[4,64]{1,0:T(4,128)} %refs_1_.1, f32[1,64]{1,0:T(1,128)} %bitcast.8, s32[2,4]{1,0:T(2,128)} %bitcast.7), custom_call_target="tpu_custom_call" | custom-call | tf_op jit(solution)/shard_map/pallas_call | solution.py:41
  2.7 7.7 %all-to-all-start = ((bf16[8,2,9344]{2,1,0:T(2,128)(2,1)}), bf16[8,2,9344]{2,1,0:T(2,128)(2,1)S(1)}, u32[]{:S(2)}, u32[]{:S(2)}) async-start(bf16[8,2,9344]{2,1,0:T(2,128)(2,1)} %shard_map.76), calls=%async_computation | async-start | bytes 598016 | tf_op jit(solution)/shard_map/all_to_all | solution.py:417
  10.3 0.0 copy-start
  10.3 1.2 %copy-done = bf16[50,9216]{1,0:T(8,128)(2,1)S(1)} copy-done((bf16[50,9216]{1,0:T(8,128)(2,1)S(1)}, bf16[50,9216]{1,0:T(8,128)(2,1)}, u32[]{:S(2)}) %copy-start) | copy-done | bytes 921624
  11.6 0.3 shard_map.77
  11.9 8.4 %all-to-all-done = bf16[8,2,9344]{2,1,0:T(2,128)(2,1)S(1)} async-done(((bf16[8,2,9344]{2,1,0:T(2,128)(2,1)}), bf16[8,2,9344]{2,1,0:T(2,128)(2,1)S(1)}, u32[]{:S(2)}, u32[]{:S(2)}) %all-to-all-start) | async-done | bytes 299040 | tf_op jit(solution)/shard_map/all_to_all | solution.py:417
  20.3 0.1 reshape.16.rows_ref
  20.4 4.4 %collective-permute-start.1 = (bf16[16,9344]{1,0:T(8,128)(2,1)S(1)}, bf16[16,9344]{1,0:T(8,128)(2,1)S(1)}, u32[]{:S(2)}, u32[]{:S(2)}) collective-permute-start(bf16[16,9344]{1,0:T(8,128)(2,1)S(1)} %reshape.16.rows_ref), channel_id=1, source_target_pairs={{0,128},{128,0},{1,129},{129,1},{2,130},{130,2},{3,131},{131,3},{4... | collective-permute-start | bytes 897032 | tf_op jit(solution)/shard_map/ppermute | solution.py:420
  24.9 1.9 %shard_map.78 = (f32[576,128]{1,0:T(8,128)S(1)}, f32[32,2,128]{2,1,0:T(2,128)}) custom-call(bf16[16,9344]{1,0:T(8,128)(2,1)S(1)} %reshape.16.rows_ref, bf16[2304,256]{1,0:T(8,128)(2,1)S(1)} %get-tuple-element.39.table_ref, f32[128,128]{1,0:T(8,128)S(1)} %get-tuple-element.40.energy_ref), custom_call_target="tpu_custom_call" | custom-call | tf_op jit(solution)/shard_map/pallas_call | solution.py:41
  26.8 6.2 %all-to-all-start.1 = ((f32[32,2,128]{2,1,0:T(2,128)}), f32[32,2,128]{2,1,0:T(2,128)S(1)}, u32[]{:S(2)}, u32[]{:S(2)}) async-start(f32[32,2,128]{2,1,0:T(2,128)} %get-tuple-element.41), calls=%async_computation.1 | async-start | bytes 65536 | tf_op jit(solution)/shard_map/all_to_all | solution.py:417
  33.0 0.1 pad_add_fusion.place_ref
  33.1 0.0 collective-permute-done.1
  33.1 6.9 %conditional.1 = (bf16[288,1152]{1,0:T(8,128)(2,1)S(1)}, bf16[288,1152]{1,0:T(8,128)(2,1)}) conditional(s32[]{:T(128)} %convert_element_type.3, () %tuple.18, (bf16[16,9344]{1,0:T(8,128)(2,1)S(1)}, bf16[2304,256]{1,0:T(8,128)(2,1)S(1)}, f32[128,128]{1,0:T(8,128)S(1)}, s32[2]{0:T(128)S(1)}, bf16[16,9344]{1,0:T(8,128)(2,1)S(1)}, ...), branch_computations={%region_0.0_spmd, %region_1.0_spmd} | conditional | bytes 2654264 | solution.py:487
  33.1 1.1 %branch_1_fun.2.two_logits_ref = f32[576,128]{1,0:T(8,128)S(1)} custom-call(bf16[16,9344]{1,0:T(8,128)(2,1)S(1)} %get-tuple-element.14.rows_ref.two_ref, bf16[2304,256]{1,0:T(8,128)(2,1)S(1)} %get-tuple-element.16.table_ref, f32[128,128]{1,0:T(8,128)S(1)} %get-tuple-element.17.energy_ref), custom_call_target="tpu_custom_call" | custom-call | tf_op jit(solution)/shard_map/cond/branch_1_fun/pallas_call | solution.py:41
  34.1 1.6 %branch_1_fun.3 = (bf16[288,1152]{1,0:T(8,128)(2,1)S(1)}, bf16[288,1152]{1,0:T(8,128)(2,1)S(1)}) custom-call(s32[2]{0:T(128)S(1)} %get-tuple-element.12.place_ref, bf16[16,9344]{1,0:T(8,128)(2,1)S(1)} %get-tuple-element.13.one_ref, bf16[16,9344]{1,0:T(8,128)(2,1)S(1)} %get-tuple-element.14.rows_ref.two_ref, f32[576,128]{1,0:T(8,128)S(1)} %get-tuple-element.15.one_logits_ref, ...), custom_call_target="tpu_custom_call" | custom-call | tf_op jit(solution)/shard_map/cond/branch_1_fun/pallas_call | solution.py:41
  35.8 2.2 %collective-permute-start = (bf16[288,1152]{1,0:T(8,128)(2,1)S(1)}, bf16[288,1152]{1,0:T(8,128)(2,1)}, u32[]{:S(2)}, u32[]{:S(2)}) collective-permute-start(bf16[288,1152]{1,0:T(8,128)(2,1)S(1)} %get-tuple-element.19), channel_id=1, source_target_pairs={{0,8},{8,0},{1,9},{9,1},{2,10},{10,2},{3,11},{11,3},{4,12},{12,4},... | collective-permute-start | bytes 1990664 | tf_op jit(solution)/shard_map/cond/branch_1_fun/ppermute | solution.py:420
  38.0 1.9 %collective-permute-done = bf16[288,1152]{1,0:T(8,128)(2,1)} collective-permute-done((bf16[288,1152]{1,0:T(8,128)(2,1)S(1)}, bf16[288,1152]{1,0:T(8,128)(2,1)}, u32[]{:S(2)}, u32[]{:S(2)}) %collective-permute-start) | collective-permute-done | bytes 663584 | tf_op jit(solution)/shard_map/cond/branch_1_fun/ppermute | solution.py:420
  39.9 1.4 %all-to-all-done.1.stats_ref = f32[32,2,128]{2,1,0:T(2,128)S(1)} async-done(((f32[32,2,128]{2,1,0:T(2,128)}), f32[32,2,128]{2,1,0:T(2,128)S(1)}, u32[]{:S(2)}, u32[]{:S(2)}) %all-to-all-start.1) | async-done | bytes 32800 | tf_op jit(solution)/shard_map/all_to_all | solution.py:417
  41.3 4.3 %shard_map.79 = (bf16[16,88,128]{2,1,0:T(8,128)(2,1)}, f32[1,128]{1,0:T(1,128)S(1)}) custom-call(s32[2]{0:T(128)S(1)} %pad_add_fusion.place_ref, f32[32,2,128]{2,1,0:T(2,128)S(1)} %all-to-all-done.1.stats_ref, bf16[288,1152]{1,0:T(8,128)(2,1)S(1)} %get-tuple-element.43.mine_ref, bf16[288,1152]{1,0:T(8,128)(2,1)} %get-tuple-element.44.other_any), custom_call_target="tpu_custom_call" | custom-call | tf_op jit(solution)/shard_map/pallas_call | solution.py:41
  45.6 12.3 %all-to-all-start.2 = ((bf16[16,88,128]{2,1,0:T(8,128)(2,1)}), bf16[16,88,128]{2,1,0:T(8,128)(2,1)S(1)}, u32[]{:S(2)}, u32[]{:S(2)}) async-start(bf16[16,88,128]{2,1,0:T(8,128)(2,1)} %get-tuple-element.45), calls=%async_computation.2 | async-start | bytes 720896 | tf_op jit(solution)/shard_map/all_to_all | solution.py:417
  57.9 0.6 dynamic-slice_bitcast_fusion
  58.5 11.3 %all-to-all-done.2.parts_ref = bf16[16,88,128]{2,1,0:T(8,128)(2,1)S(1)} async-done(((bf16[16,88,128]{2,1,0:T(8,128)(2,1)}), bf16[16,88,128]{2,1,0:T(8,128)(2,1)S(1)}, u32[]{:S(2)}, u32[]{:S(2)}) %all-to-all-start.2) | async-done | bytes 360480 | tf_op jit(solution)/shard_map/all_to_all | solution.py:417
  69.8 0.8 %shard_map.80 = (f32[50,144]{1,0:T(8,128)}, f32[50,64]{1,0:T(8,128)}) custom-call(bf16[16,88,128]{2,1,0:T(8,128)(2,1)S(1)} %all-to-all-done.2.parts_ref), custom_call_target="tpu_custom_call" | custom-call | tf_op jit(solution)/shard_map/pallas_call | solution.py:41
Async XLA Ops:
  2.7 17.6 %all-to-all-start = ((bf16[8,2,9344]{2,1,0:T(2,128)(2,1)}), bf16[8,2,9344]{2,1,0:T(2,128)(2,1)S(1)}, u32[]{:S(2)}, u32[]{:S(2)}) async-start(bf16[8,2,9344]{2,1,0:T(2,128)(2,1)} %shard_map.76), calls=%async_computation | async-start | bytes 598016 | tf_op jit(solution)/shard_map/all_to_all | solution.py:417
  10.3 1.2 %copy-start = (bf16[50,9216]{1,0:T(8,128)(2,1)S(1)}, bf16[50,9216]{1,0:T(8,128)(2,1)}, u32[]{:S(2)}) copy-start(bf16[50,9216]{1,0:T(8,128)(2,1)} %classes_ref.1) | copy-start | bytes 2764804
  20.4 12.6 %collective-permute-start.1 = (bf16[16,9344]{1,0:T(8,128)(2,1)S(1)}, bf16[16,9344]{1,0:T(8,128)(2,1)S(1)}, u32[]{:S(2)}, u32[]{:S(2)}) collective-permute-start(bf16[16,9344]{1,0:T(8,128)(2,1)S(1)} %reshape.16.rows_ref), channel_id=1, source_target_pairs={{0,128},{128,0},{1,129},{129,1},{2,130},{130,2},{3,131},{131,3},{4... | collective-permute-start | bytes 897032 | tf_op jit(solution)/shard_map/ppermute | solution.py:420
  26.8 14.5 %all-to-all-start.1 = ((f32[32,2,128]{2,1,0:T(2,128)}), f32[32,2,128]{2,1,0:T(2,128)S(1)}, u32[]{:S(2)}, u32[]{:S(2)}) async-start(f32[32,2,128]{2,1,0:T(2,128)} %get-tuple-element.41), calls=%async_computation.1 | async-start | bytes 65536 | tf_op jit(solution)/shard_map/all_to_all | solution.py:417
  35.8 4.1 %collective-permute-start = (bf16[288,1152]{1,0:T(8,128)(2,1)S(1)}, bf16[288,1152]{1,0:T(8,128)(2,1)}, u32[]{:S(2)}, u32[]{:S(2)}) collective-permute-start(bf16[288,1152]{1,0:T(8,128)(2,1)S(1)} %get-tuple-element.19), channel_id=1, source_target_pairs={{0,8},{8,0},{1,9},{9,1},{2,10},{10,2},{3,11},{11,3},{4,12},{12,4},... | collective-permute-start | bytes 1990664 | tf_op jit(solution)/shard_map/cond/branch_1_fun/ppermute | solution.py:420
  45.6 24.3 %all-to-all-start.2 = ((bf16[16,88,128]{2,1,0:T(8,128)(2,1)}), bf16[16,88,128]{2,1,0:T(8,128)(2,1)S(1)}, u32[]{:S(2)}, u32[]{:S(2)}) async-start(bf16[16,88,128]{2,1,0:T(8,128)(2,1)} %get-tuple-element.45), calls=%async_computation.2 | async-start | bytes 720896 | tf_op jit(solution)/shard_map/all_to_all | solution.py:417

commit v6 on v5

--- a/solution.py
+++ b/solution.py
@@ -12,6 +12,7 @@
 LANES = 128
 HALF = 64
 ROWS = 16
+TURNS = 2 * ROTATIONS - 4
 GROUPS = 64
 TARGETS = GROUPS // 4
 DEPTH = 2 * ROTATIONS * ROWS
@@ -47,7 +48,7 @@
     )(*args)
 
 
-def pack_body(class_block, images_any, ctf_any, noise_any, cands_any, out_ref, images_ref, ctf_ref, noise_ref, cands_ref, sems):
+def pack_body(class_block, images_any, ctf_any, noise_any, cands_any, out_any, images_ref, ctf_ref, noise_ref, cands_ref, out_ref, sems):
     copies = [
         pltpu.make_async_copy(source, target, sems.at[i])
         for i, (source, target) in enumerate(
@@ -61,7 +62,7 @@
     ]
     for copy in copies:
         copy.start()
-    for copy in copies:
+    for copy in copies[:3]:
         copy.wait()
     part = images_ref.shape[0]
     ctf = ctf_ref[...]
@@ -110,9 +111,25 @@
     put(jnp.where(lane < HALF, quad_rows, flags), FEATURES, LANES)
     wide = jnp.concatenate([factor] * 4, axis=1)
     step = 4 * LANES
+    copies[3].wait()
+    sent = []
+
+    def leave(start, size):
+        piece = pl.ds(start, size)
+        copy = pltpu.make_async_copy(
+            out_ref.at[:, :, piece], out_any.at[:, :, piece], sems.at[4 + len(sent)]
+        )
+        copy.start()
+        sent.append(copy)
+
+    leave(FEATURES, LANES)
     for t in range(FEATURES // step):
         part_w = (images_ref[:, t * step : (t + 1) * step].astype(F32) * wide).astype(BF16)
         put(jnp.dot(packing, part_w, preferred_element_type=F32), t * step, step)
+        if t % 6 == 5:
+            leave((t - 5) * step, 6 * step)
+    for copy in sent:
+        copy.wait()
 
 
 def prep_body(classes_ref, table_ref, energy_ref):
@@ -120,11 +137,15 @@
     acc = jnp.zeros((count, LANES), F32)
     for b in range(ROTATIONS):
         block = classes_ref[:, b * BLOCK : (b + 1) * BLOCK]
-        table_ref[b * HALF : b * HALF + count, :] = block
-        table_ref[b * HALF + count : (b + 1) * HALF, :] = jnp.zeros((HALF - count, BLOCK), BF16)
+        m, c = b // 4, b % 4
+        table_ref[c * HALF : c * HALF + count, m * BLOCK : (m + 1) * BLOCK] = block
         wide = block.astype(F32)
         square = wide * wide
         acc = acc + square[:, :LANES] + square[:, LANES:]
+    for c in range(4):
+        table_ref[c * HALF + count : (c + 1) * HALF, :] = jnp.zeros(
+            (HALF - count, ROTATIONS // 4 * BLOCK), BF16
+        )
     acc = acc + pltpu.roll(acc, HALF, 1)
     energy_ref[...] = jnp.zeros((LANES, LANES), F32)
     energy_ref[0:count, :] = acc
@@ -154,35 +175,33 @@
 
 def correlate(rows_ref, table_ref, energy_ref, logits_ref, blocks_ref, acc_ref):
     total_rows = ROTATIONS * ROWS
-    for b in range(ROTATIONS):
-        blocks_ref[b * ROWS : (b + 1) * ROWS, :] = rows_ref[:, b * BLOCK : (b + 1) * BLOCK]
-    for m in range(ROTATIONS // 4):
-        g = lax.dot_general(
-            blocks_ref[...],
-            table_ref[m * BLOCK : (m + 1) * BLOCK, :],
-            (((1,), (1,)), ((), ())),
-            preferred_element_type=F32,
-        )
-        for h in range(2):
-            tile = g[:, h * LANES : (h + 1) * LANES]
-            shift = (2 * m + h) * 2 * ROWS
-            if shift == 0:
-                acc_ref[...] = tile
-            else:
-                acc_ref[0 : total_rows - shift, :] += tile[shift:, :]
-                acc_ref[total_rows - shift :, :] += tile[:shift, :]
+    for b in range(TURNS):
+        at = b % ROTATIONS * BLOCK
+        blocks_ref[b * ROWS : (b + 1) * ROWS, :] = rows_ref[:, at : at + BLOCK]
+    left = jnp.concatenate(
+        [
+            blocks_ref[4 * m * ROWS : 4 * m * ROWS + total_rows, :]
+            for m in range(ROTATIONS // 4)
+        ],
+        axis=1,
+    )
+    acc_ref[...] = lax.dot_general(
+        left, table_ref[...], (((1,), (1,)), ((), ())), preferred_element_type=F32
+    )
     meta = rows_ref[:, FEATURES : FEATURES + LANES].astype(F32)
     lane = lanes_of((ROWS, LANES))
     quad = jnp.where(lane < HALF, meta, 0.0)
     norm = 0.5 * lax.dot_general(
         quad, energy_ref[...], (((1,), (1,)), ((), ())), precision=HIGH, preferred_element_type=F32
     )
+
+    def tile(r, half):
+        r = r % ROTATIONS
+        return acc_ref[r * ROWS : (r + 1) * ROWS, half * LANES : (half + 1) * LANES]
+
     for r in range(ROTATIONS):
-        nxt = (r + 1) % ROTATIONS
-        mixed = jnp.where(
-            lane < HALF,
-            acc_ref[r * ROWS : (r + 1) * ROWS, :],
-            acc_ref[nxt * ROWS : (nxt + 1) * ROWS, :],
+        mixed = jnp.where(lane < HALF, tile(r, 0), tile(r + 1, 0)) + jnp.where(
+            lane < HALF, tile(r + 2, 1), tile(r + 3, 1)
         )
         logits_ref[r * ROWS : (r + 1) * ROWS, :] = mixed + pltpu.roll(mixed, HALF, 1) - norm
 
@@ -318,8 +337,11 @@
                     table_ref[at : at + ROWS, :] = value
     weight = jnp.concatenate(weights, axis=0)
     quad = jnp.concatenate(quads, axis=0)
-    by_class = jnp.dot(weight.T, quad, precision=HIGH, preferred_element_type=F32)
-    by_shell = jnp.dot(quad.T, weight, precision=HIGH, preferred_element_type=F32)[0:HALF, :]
+    upper = weight.astype(BF16).astype(F32)
+    parts = jnp.concatenate([upper, weight - upper], axis=0).T.astype(BF16)
+    quad = jnp.concatenate([quad, quad], axis=0).astype(BF16)
+    by_class = jnp.dot(parts, quad, preferred_element_type=F32)
+    by_shell = by_class.T[0:HALF, :]
     tail = jnp.where(on_left, by_class[0:16, :], by_class[16:32, :]).astype(BF16)
     wide = lanes_of((HALF, LANES))
     spare = jnp.where(
@@ -431,18 +453,20 @@
         shape((8, 2, width), BF16),
         *hbm,
         in_specs=[raw] * 4,
+        out_specs=raw,
         scratch=[
             pltpu.VMEM((part, FEATURES), BF16),
             pltpu.VMEM((part, CYCLES), F32),
             pltpu.VMEM((1, CYCLES), F32),
             pltpu.VMEM((2, part), jnp.int32),
-            pltpu.SemaphoreType.DMA((4,)),
+            pltpu.VMEM((8, 2, width), BF16),
+            pltpu.SemaphoreType.DMA((8,)),
         ],
     )
     rows = swap(packed, "cls").reshape(ROWS, width)
     table, energy = call(
         prep_body,
-        (shape((ROTATIONS * HALF, BLOCK), BF16), shape((LANES, LANES), F32)),
+        (shape((BLOCK, ROTATIONS // 4 * BLOCK), BF16), shape((LANES, LANES), F32)),
         classes,
     )
     rows, table, energy = lax.optimization_barrier((rows, table, energy))
@@ -453,7 +477,7 @@
         rows,
         table,
         energy,
-        scratch=[pltpu.VMEM((total_rows, BLOCK), BF16), pltpu.VMEM((total_rows, LANES), F32)],
+        scratch=[pltpu.VMEM((TURNS * ROWS, BLOCK), BF16), pltpu.VMEM((total_rows, BLOCK), F32)],
     )
     group_stats = swap(stats, ("xl", "core", "cls"))
 
@@ -466,7 +490,7 @@
             two,
             table,
             energy,
-            scratch=[pltpu.VMEM((total_rows, BLOCK), BF16), pltpu.VMEM((total_rows, LANES), F32)],
+            scratch=[pltpu.VMEM((TURNS * ROWS, BLOCK), BF16), pltpu.VMEM((total_rows, BLOCK), F32)],
         )
         own, theirs = call(
             share_body,

time: 71.6 us -> 71.4 us (level)
  no operation moved by 1% of the time
where the time goes in v6:
time: 71.4 us; the launch traced here: 70.4 us
  starting transfers between devices  32.8 us (46%)
  waiting for transfers between devices  23 us (32%)
  Pallas kernels  11.9 us (17%)
  local copies, waits for them, and re-layouts  1.91 us (3%)
    all_to_all x3, starting transfers between devices, swap(): return lax.all_to_all(value, axes, split_axis=0, concat_axis=0, tiled=True)  26.2 us
    all_to_all x3, waiting for transfers between devices, swap(): return lax.all_to_all(value, axes, split_axis=0, concat_axis=0, tiled=True)  21 us
    pallas_call x7, Pallas kernels, call(): pl.pallas_call(body, out_shape=outs, scratch_shapes=list(scratch), compil...  11.9 us
    ppermute x2, starting transfers between devices, flip(): return lax.ppermute(value, axis, [(0, 1), (1, 0)])  6.63 us
    ppermute x2, waiting for transfers between devices, flip(): return lax.ppermute(value, axis, [(0, 1), (1, 0)])  1.92 us
  transfers between devices with their start and end apart: 5, of which 4 were waited for; matrix products, arithmetic and copies ran while one was open for 1% of the time, Pallas kernels for 7%

profile of v6, /device:TPU:1, one launch (start us, length us, event | category | flops | bytes accessed | tf_op | source)
XLA Modules:
  0.0 70.4 jit_solution(6807326072779194238)
XLA Ops:
  0.6 1.9 %shard_map.76 = bf16[8,2,9344]{2,1,0:T(2,128)(2,1)} custom-call(bf16[4,9216]{1,0:T(4,128)(2,1)} %refs_0_.1, f32[4,64]{1,0:T(4,128)} %refs_1_.1, f32[1,64]{1,0:T(1,128)} %bitcast.8, s32[2,4]{1,0:T(2,128)} %bitcast.7), custom_call_target="tpu_custom_call" | custom-call | tf_op jit(solution)/shard_map/pallas_call | solution.py:42
  2.6 7.7 %all-to-all-start = ((bf16[8,2,9344]{2,1,0:T(2,128)(2,1)}), bf16[8,2,9344]{2,1,0:T(2,128)(2,1)S(1)}, u32[]{:S(2)}, u32[]{:S(2)}) async-start(bf16[8,2,9344]{2,1,0:T(2,128)(2,1)} %shard_map.76), calls=%async_computation | async-start | bytes 598016 | tf_op jit(solution)/shard_map/all_to_all | solution.py:439
  10.2 0.0 copy-start
  10.2 1.2 %copy-done = bf16[50,9216]{1,0:T(8,128)(2,1)S(1)} copy-done((bf16[50,9216]{1,0:T(8,128)(2,1)S(1)}, bf16[50,9216]{1,0:T(8,128)(2,1)}, u32[]{:S(2)}) %copy-start) | copy-done | bytes 921624
  11.4 0.3 shard_map.77
  11.8 8.4 %all-to-all-done = bf16[8,2,9344]{2,1,0:T(2,128)(2,1)S(1)} async-done(((bf16[8,2,9344]{2,1,0:T(2,128)(2,1)}), bf16[8,2,9344]{2,1,0:T(2,128)(2,1)S(1)}, u32[]{:S(2)}, u32[]{:S(2)}) %all-to-all-start) | async-done | bytes 299040 | tf_op jit(solution)/shard_map/all_to_all | solution.py:439
  20.2 0.1 reshape.16.rows_ref
  20.3 4.4 %collective-permute-start.1 = (bf16[16,9344]{1,0:T(8,128)(2,1)S(1)}, bf16[16,9344]{1,0:T(8,128)(2,1)S(1)}, u32[]{:S(2)}, u32[]{:S(2)}) collective-permute-start(bf16[16,9344]{1,0:T(8,128)(2,1)S(1)} %reshape.16.rows_ref), channel_id=1, source_target_pairs={{0,128},{128,0},{1,129},{129,1},{2,130},{130,2},{3,131},{131,3},{4... | collective-permute-start | bytes 897032 | tf_op jit(solution)/shard_map/ppermute | solution.py:442
  24.7 1.9 %shard_map.78 = (f32[576,128]{1,0:T(8,128)S(1)}, f32[32,2,128]{2,1,0:T(2,128)}) custom-call(bf16[16,9344]{1,0:T(8,128)(2,1)S(1)} %reshape.16.rows_ref, bf16[256,2304]{1,0:T(8,128)(2,1)S(1)} %get-tuple-element.39.table_ref, f32[128,128]{1,0:T(8,128)S(1)} %get-tuple-element.40.energy_ref), custom_call_target="tpu_custom_call" | custom-call | tf_op jit(solution)/shard_map/pallas_call | solution.py:42
  26.7 6.2 %all-to-all-start.1 = ((f32[32,2,128]{2,1,0:T(2,128)}), f32[32,2,128]{2,1,0:T(2,128)S(1)}, u32[]{:S(2)}, u32[]{:S(2)}) async-start(f32[32,2,128]{2,1,0:T(2,128)} %get-tuple-element.41), calls=%async_computation.1 | async-start | bytes 65536 | tf_op jit(solution)/shard_map/all_to_all | solution.py:439
  32.9 0.1 pad_add_fusion.place_ref
  32.9 0.0 collective-permute-done.1
  32.9 6.9 %conditional.1 = (bf16[288,1152]{1,0:T(8,128)(2,1)S(1)}, bf16[288,1152]{1,0:T(8,128)(2,1)}) conditional(s32[]{:T(128)} %convert_element_type.3, () %tuple.18, (bf16[16,9344]{1,0:T(8,128)(2,1)S(1)}, bf16[256,2304]{1,0:T(8,128)(2,1)S(1)}, f32[128,128]{1,0:T(8,128)S(1)}, s32[2]{0:T(128)S(1)}, bf16[16,9344]{1,0:T(8,128)(2,1)S(1)}, ...), branch_computations={%region_0.0_spmd, %region_1.0_spmd} | conditional | bytes 2654264 | solution.py:511
  32.9 1.1 %branch_1_fun.2.two_logits_ref = f32[576,128]{1,0:T(8,128)S(1)} custom-call(bf16[16,9344]{1,0:T(8,128)(2,1)S(1)} %get-tuple-element.14.rows_ref.two_ref, bf16[256,2304]{1,0:T(8,128)(2,1)S(1)} %get-tuple-element.16.table_ref, f32[128,128]{1,0:T(8,128)S(1)} %get-tuple-element.17.energy_ref), custom_call_target="tpu_custom_call" | custom-call | tf_op jit(solution)/shard_map/cond/branch_1_fun/pallas_call | solution.py:42
  34.0 1.6 %branch_1_fun.3 = (bf16[288,1152]{1,0:T(8,128)(2,1)S(1)}, bf16[288,1152]{1,0:T(8,128)(2,1)S(1)}) custom-call(s32[2]{0:T(128)S(1)} %get-tuple-element.12.place_ref, bf16[16,9344]{1,0:T(8,128)(2,1)S(1)} %get-tuple-element.13.one_ref, bf16[16,9344]{1,0:T(8,128)(2,1)S(1)} %get-tuple-element.14.rows_ref.two_ref, f32[576,128]{1,0:T(8,128)S(1)} %get-tuple-element.15.one_logits_ref, ...), custom_call_target="tpu_custom_call" | custom-call | tf_op jit(solution)/shard_map/cond/branch_1_fun/pallas_call | solution.py:42
  35.7 2.2 %collective-permute-start = (bf16[288,1152]{1,0:T(8,128)(2,1)S(1)}, bf16[288,1152]{1,0:T(8,128)(2,1)}, u32[]{:S(2)}, u32[]{:S(2)}) collective-permute-start(bf16[288,1152]{1,0:T(8,128)(2,1)S(1)} %get-tuple-element.19), channel_id=1, source_target_pairs={{0,8},{8,0},{1,9},{9,1},{2,10},{10,2},{3,11},{11,3},{4,12},{12,4},... | collective-permute-start | bytes 1990664 | tf_op jit(solution)/shard_map/cond/branch_1_fun/ppermute | solution.py:442
  37.9 1.9 %collective-permute-done = bf16[288,1152]{1,0:T(8,128)(2,1)} collective-permute-done((bf16[288,1152]{1,0:T(8,128)(2,1)S(1)}, bf16[288,1152]{1,0:T(8,128)(2,1)}, u32[]{:S(2)}, u32[]{:S(2)}) %collective-permute-start) | collective-permute-done | bytes 663584 | tf_op jit(solution)/shard_map/cond/branch_1_fun/ppermute | solution.py:442
  39.8 1.4 %all-to-all-done.1.stats_ref = f32[32,2,128]{2,1,0:T(2,128)S(1)} async-done(((f32[32,2,128]{2,1,0:T(2,128)}), f32[32,2,128]{2,1,0:T(2,128)S(1)}, u32[]{:S(2)}, u32[]{:S(2)}) %all-to-all-start.1) | async-done | bytes 32800 | tf_op jit(solution)/shard_map/all_to_all | solution.py:439
  41.1 4.2 %shard_map.79 = (bf16[16,88,128]{2,1,0:T(8,128)(2,1)}, f32[1,128]{1,0:T(1,128)S(1)}) custom-call(s32[2]{0:T(128)S(1)} %pad_add_fusion.place_ref, f32[32,2,128]{2,1,0:T(2,128)S(1)} %all-to-all-done.1.stats_ref, bf16[288,1152]{1,0:T(8,128)(2,1)S(1)} %get-tuple-element.43.mine_ref, bf16[288,1152]{1,0:T(8,128)(2,1)} %get-tuple-element.44.other_any), custom_call_target="tpu_custom_call" | custom-call | tf_op jit(solution)/shard_map/pallas_call | solution.py:42
  45.4 12.3 %all-to-all-start.2 = ((bf16[16,88,128]{2,1,0:T(8,128)(2,1)}), bf16[16,88,128]{2,1,0:T(8,128)(2,1)S(1)}, u32[]{:S(2)}, u32[]{:S(2)}) async-start(bf16[16,88,128]{2,1,0:T(8,128)(2,1)} %get-tuple-element.45), calls=%async_computation.2 | async-start | bytes 720896 | tf_op jit(solution)/shard_map/all_to_all | solution.py:439
  57.7 0.6 dynamic-slice_bitcast_fusion
  58.3 11.3 %all-to-all-done.2.parts_ref = bf16[16,88,128]{2,1,0:T(8,128)(2,1)S(1)} async-done(((bf16[16,88,128]{2,1,0:T(8,128)(2,1)}), bf16[16,88,128]{2,1,0:T(8,128)(2,1)S(1)}, u32[]{:S(2)}, u32[]{:S(2)}) %all-to-all-start.2) | async-done | bytes 360480 | tf_op jit(solution)/shard_map/all_to_all | solution.py:439
  69.6 0.8 %shard_map.80 = (f32[50,144]{1,0:T(8,128)}, f32[50,64]{1,0:T(8,128)}) custom-call(bf16[16,88,128]{2,1,0:T(8,128)(2,1)S(1)} %all-to-all-done.2.parts_ref), custom_call_target="tpu_custom_call" | custom-call | tf_op jit(solution)/shard_map/pallas_call | solution.py:42
Async XLA Ops:
  2.6 17.6 %all-to-all-start = ((bf16[8,2,9344]{2,1,0:T(2,128)(2,1)}), bf16[8,2,9344]{2,1,0:T(2,128)(2,1)S(1)}, u32[]{:S(2)}, u32[]{:S(2)}) async-start(bf16[8,2,9344]{2,1,0:T(2,128)(2,1)} %shard_map.76), calls=%async_computation | async-start | bytes 598016 | tf_op jit(solution)/shard_map/all_to_all | solution.py:439
  10.2 1.2 %copy-start = (bf16[50,9216]{1,0:T(8,128)(2,1)S(1)}, bf16[50,9216]{1,0:T(8,128)(2,1)}, u32[]{:S(2)}) copy-start(bf16[50,9216]{1,0:T(8,128)(2,1)} %classes_ref.1) | copy-start | bytes 2764804
  20.3 12.7 %collective-permute-start.1 = (bf16[16,9344]{1,0:T(8,128)(2,1)S(1)}, bf16[16,9344]{1,0:T(8,128)(2,1)S(1)}, u32[]{:S(2)}, u32[]{:S(2)}) collective-permute-start(bf16[16,9344]{1,0:T(8,128)(2,1)S(1)} %reshape.16.rows_ref), channel_id=1, source_target_pairs={{0,128},{128,0},{1,129},{129,1},{2,130},{130,2},{3,131},{131,3},{4... | collective-permute-start | bytes 897032 | tf_op jit(solution)/shard_map/ppermute | solution.py:442
  26.7 14.5 %all-to-all-start.1 = ((f32[32,2,128]{2,1,0:T(2,128)}), f32[32,2,128]{2,1,0:T(2,128)S(1)}, u32[]{:S(2)}, u32[]{:S(2)}) async-start(f32[32,2,128]{2,1,0:T(2,128)} %get-tuple-element.41), calls=%async_computation.1 | async-start | bytes 65536 | tf_op jit(solution)/shard_map/all_to_all | solution.py:439
  35.7 4.1 %collective-permute-start = (bf16[288,1152]{1,0:T(8,128)(2,1)S(1)}, bf16[288,1152]{1,0:T(8,128)(2,1)}, u32[]{:S(2)}, u32[]{:S(2)}) collective-permute-start(bf16[288,1152]{1,0:T(8,128)(2,1)S(1)} %get-tuple-element.19), channel_id=1, source_target_pairs={{0,8},{8,0},{1,9},{9,1},{2,10},{10,2},{3,11},{11,3},{4,12},{12,4},... | collective-permute-start | bytes 1990664 | tf_op jit(solution)/shard_map/cond/branch_1_fun/ppermute | solution.py:442
  45.4 24.2 %all-to-all-start.2 = ((bf16[16,88,128]{2,1,0:T(8,128)(2,1)}), bf16[16,88,128]{2,1,0:T(8,128)(2,1)S(1)}, u32[]{:S(2)}, u32[]{:S(2)}) async-start(bf16[16,88,128]{2,1,0:T(8,128)(2,1)} %get-tuple-element.45), calls=%async_computation.2 | async-start | bytes 720896 | tf_op jit(solution)/shard_map/all_to_all | solution.py:439

commit v7 on v6

--- a/solution.py
+++ b/solution.py
@@ -229,8 +229,8 @@
         stats_ref[d, 1:2, :] = total_row
 
 
-def share_body(place_ref, one_ref, two_ref, one_logits_ref, two_logits_ref, mine_ref, theirs_ref):
-    second = place_ref[0] == 1
+def share_body(one_ref, two_ref, one_logits_ref, two_logits_ref, mine_ref, theirs_ref):
+    second = lax.axis_index("core") == 1
     pieces = []
     for b in range(ROTATIONS):
         for ref in (one_ref, two_ref):
@@ -272,25 +272,19 @@
         ref[BLOCK:, 8 * LANES :] = jnp.zeros((2 * ROWS, DEPTH - 8 * LANES), BF16)
 
 
+def settle_body(value_ref, out_ref):
+    out_ref[...] = value_ref[...]
+
+
 def sums_body(
-    place_ref, stats_ref, mine_ref, other_any, out_any, evid_ref, pay_ref, other_ref, table_a, table_b, sems
+    stats_ref, mine_ref, other_ref, out_any, evid_ref, pay_ref, table_a, table_b, sems
 ):
-    fetch_facts = pltpu.make_async_copy(
-        other_any.at[pl.ds(BLOCK, 2 * ROWS), :], other_ref.at[pl.ds(BLOCK, 2 * ROWS), :], sems.at[TARGETS]
-    )
-    fetch_turned = pltpu.make_async_copy(
-        other_any.at[pl.ds(0, BLOCK), :], other_ref.at[pl.ds(0, BLOCK), :], sems.at[TARGETS + 1]
-    )
-    fetch_facts.start()
-    fetch_turned.start()
-    core, near = place_ref[0], place_ref[1]
+    core, near = lax.axis_index("core"), lax.axis_index("xl")
     tables = (table_a, table_b)
     lane = lanes_of((ROWS, LANES))
     on_left = lane < HALF
     weights, quads = [], []
     for g in range(4):
-        if g == 2:
-            fetch_facts.wait()
         facts_ref, table_ref = (mine_ref, other_ref)[g // 2], tables[g // 2]
 
         def fact(i):
@@ -356,7 +350,6 @@
         pltpu.make_async_copy(pay_ref.at[d], out_any.at[d], sems.at[d]) for d in range(TARGETS)
     ]
     started = 0
-    fetch_turned.wait()
     base = (ROTATIONS - CHUNKS * near) * 2 * ROWS
     for group in ((0, 1), (2, 3), (4, 5), (6, 7), (8,)):
         kept = {b: [i for i in range(16) if (16 * b + i) // CHUNKS % 2 == 0] for b in group}
@@ -427,12 +420,10 @@
     class_block = classes.shape[0]
     part = images.shape[0]
     my_index = lax.axis_index("cls")
-    place = jnp.stack([lax.axis_index("core"), lax.axis_index("xl")]).astype(jnp.int32)
     total_rows = ROTATIONS * ROWS
     width = FEATURES + LANES
     shape = jax.ShapeDtypeStruct
     vmem = pl.BlockSpec(memory_space=pltpu.VMEM)
-    smem = pl.BlockSpec(memory_space=pltpu.SMEM)
     raw = pl.BlockSpec(memory_space=pltpu.HBM)
 
     def swap(value, axes):
@@ -492,38 +483,26 @@
             energy,
             scratch=[pltpu.VMEM((TURNS * ROWS, BLOCK), BF16), pltpu.VMEM((total_rows, BLOCK), F32)],
         )
-        own, theirs = call(
-            share_body,
-            (shared, shared),
-            place,
-            one,
-            two,
-            one_logits,
-            two_logits,
-            in_specs=[smem] + [vmem] * 4,
-        )
-        return own, flip(theirs, "core")
+        own, theirs = call(share_body, (shared, shared), one, two, one_logits, two_logits)
+        return own, call(settle_body, shared, flip(theirs, "core"))
 
     def alone(one, two, one_logits):
         nothing = jnp.zeros(shared.shape, BF16)
         return nothing, nothing
 
-    own_share, other_share = lax.cond(place[0] < 2, trade, alone, rows, beside, logits)
+    own_share, other_share = lax.cond(lax.axis_index("core") < 2, trade, alone, rows, beside, logits)
     pay, evidence = call(
         sums_body,
         (shape((TARGETS, PAY_ROWS + 16, LANES), BF16), shape((1, LANES), F32)),
-        place,
         group_stats,
         own_share,
-        pltpu.with_memory_space_constraint(other_share, pltpu.HBM),
-        in_specs=[smem, vmem, vmem, raw],
+        other_share,
         out_specs=(raw, vmem),
         scratch=[
             pltpu.VMEM((TARGETS, PAY_ROWS + 16, LANES), BF16),
-            pltpu.VMEM(shared.shape, BF16),
             pltpu.VMEM((2 * DEPTH, LANES), BF16),
             pltpu.VMEM((2 * DEPTH, LANES), BF16),
-            pltpu.SemaphoreType.DMA((TARGETS + 2,)),
+            pltpu.SemaphoreType.DMA((TARGETS,)),
         ],
     )
     parts = swap(pay, ("xh", "z"))

time: 71.4 us -> 69.8 us (0.978)
  Pallas kernels: 11.9 us -> 9.87 us
    pallas_call x7 -> x8, Pallas kernels: 11.9 us -> 9.87 us  [call(): pl.pallas_call(body, out_shape=outs, scratch_shapes=list(scratch), compil...]
    all_to_all x3, waiting for transfers between devices: 21 us -> 21.8 us  [swap(): return lax.all_to_all(value, axes, split_axis=0, concat_axis=0, tiled=True)]
  transfers between devices with their start and end apart: 5 -> 5, of which waited for: 4 -> 4; matrix products, arithmetic and copies ran while one was open for 1% -> 1% of each run, Pallas kernels for 7% -> 6%
where the time goes in v7:
time: 69.8 us; the launch traced here: 68.9 us
  starting transfers between devices  32.8 us (47%)
  waiting for transfers between devices  23.6 us (34%)
  Pallas kernels  9.87 us (14%)
  local copies, waits for them, and re-layouts  1.91 us (3%)
  between operations  0.7 us (1%)
    all_to_all x3, starting transfers between devices, swap(): return lax.all_to_all(value, axes, split_axis=0, concat_axis=0, tiled=True)  26.2 us
    all_to_all x3, waiting for transfers between devices, swap(): return lax.all_to_all(value, axes, split_axis=0, concat_axis=0, tiled=True)  21.8 us
    pallas_call x8, Pallas kernels, call(): pl.pallas_call(body, out_shape=outs, scratch_shapes=list(scratch), compil...  9.87 us
    ppermute x2, starting transfers between devices, flip(): return lax.ppermute(value, axis, [(0, 1), (1, 0)])  6.63 us
    ppermute x2, waiting for transfers between devices, flip(): return lax.ppermute(value, axis, [(0, 1), (1, 0)])  1.79 us
  transfers between devices with their start and end apart: 5, of which 4 were waited for; matrix products, arithmetic and copies ran while one was open for 1% of the time, Pallas kernels for 6%

profile of v7, /device:TPU:1, one launch (start us, length us, event | category | flops | bytes accessed | tf_op | source)
XLA Modules:
  0.0 68.9 jit_solution(8192092346889924913)
XLA Ops:
  0.6 1.9 %shard_map.76 = bf16[8,2,9344]{2,1,0:T(2,128)(2,1)} custom-call(bf16[4,9216]{1,0:T(4,128)(2,1)} %refs_0_.1, f32[4,64]{1,0:T(4,128)} %refs_1_.1, f32[1,64]{1,0:T(1,128)} %bitcast.6, s32[2,4]{1,0:T(2,128)} %bitcast.5), custom_call_target="tpu_custom_call" | custom-call | tf_op jit(solution)/shard_map/pallas_call | solution.py:42
  2.6 7.7 %all-to-all-start = ((bf16[8,2,9344]{2,1,0:T(2,128)(2,1)}), bf16[8,2,9344]{2,1,0:T(2,128)(2,1)S(1)}, u32[]{:S(2)}, u32[]{:S(2)}) async-start(bf16[8,2,9344]{2,1,0:T(2,128)(2,1)} %shard_map.76), calls=%async_computation | async-start | bytes 598016 | tf_op jit(solution)/shard_map/all_to_all | solution.py:430
  10.2 0.0 copy-start
  10.2 1.2 %copy-done = bf16[50,9216]{1,0:T(8,128)(2,1)S(1)} copy-done((bf16[50,9216]{1,0:T(8,128)(2,1)S(1)}, bf16[50,9216]{1,0:T(8,128)(2,1)}, u32[]{:S(2)}) %copy-start) | copy-done | bytes 921624
  11.4 0.3 shard_map.77
  11.8 8.4 %all-to-all-done = bf16[8,2,9344]{2,1,0:T(2,128)(2,1)S(1)} async-done(((bf16[8,2,9344]{2,1,0:T(2,128)(2,1)}), bf16[8,2,9344]{2,1,0:T(2,128)(2,1)S(1)}, u32[]{:S(2)}, u32[]{:S(2)}) %all-to-all-start) | async-done | bytes 299040 | tf_op jit(solution)/shard_map/all_to_all | solution.py:430
  20.2 0.1 reshape.16.rows_ref
  20.3 4.4 %collective-permute-start.1 = (bf16[16,9344]{1,0:T(8,128)(2,1)S(1)}, bf16[16,9344]{1,0:T(8,128)(2,1)S(1)}, u32[]{:S(2)}, u32[]{:S(2)}) collective-permute-start(bf16[16,9344]{1,0:T(8,128)(2,1)S(1)} %reshape.16.rows_ref), channel_id=1, source_target_pairs={{0,128},{128,0},{1,129},{129,1},{2,130},{130,2},{3,131},{131,3},{4... | collective-permute-start | bytes 897032 | tf_op jit(solution)/shard_map/ppermute | solution.py:433
  24.7 1.9 %shard_map.78 = (f32[576,128]{1,0:T(8,128)S(1)}, f32[32,2,128]{2,1,0:T(2,128)}) custom-call(bf16[16,9344]{1,0:T(8,128)(2,1)S(1)} %reshape.16.rows_ref, bf16[256,2304]{1,0:T(8,128)(2,1)S(1)} %get-tuple-element.36.table_ref, f32[128,128]{1,0:T(8,128)S(1)} %get-tuple-element.37.energy_ref), custom_call_target="tpu_custom_call" | custom-call | tf_op jit(solution)/shard_map/pallas_call | solution.py:42
  26.7 6.2 %all-to-all-start.1 = ((f32[32,2,128]{2,1,0:T(2,128)}), f32[32,2,128]{2,1,0:T(2,128)S(1)}, u32[]{:S(2)}, u32[]{:S(2)}) async-start(f32[32,2,128]{2,1,0:T(2,128)} %get-tuple-element.38), calls=%async_computation.1 | async-start | bytes 65536 | tf_op jit(solution)/shard_map/all_to_all | solution.py:430
  32.9 0.0 collective-permute-done.1
  32.9 6.2 %conditional.1 = (bf16[288,1152]{1,0:T(8,128)(2,1)S(1)}, bf16[288,1152]{1,0:T(8,128)(2,1)S(1)}) conditional(s32[]{:T(128)} %convert_element_type.3, () %tuple.18, (bf16[16,9344]{1,0:T(8,128)(2,1)S(1)}, bf16[256,2304]{1,0:T(8,128)(2,1)S(1)}, f32[128,128]{1,0:T(8,128)S(1)}, bf16[16,9344]{1,0:T(8,128)(2,1)S(1)}, f32[576,128]{1,0:T(8,128)S(1)}) %tuple.19), branch_computations={%region_0.0_spmd, %region_1.0_spmd} | conditional | bytes 2654264 | solution.py:493
  32.9 1.1 %branch_1_fun.3.two_logits_ref = f32[576,128]{1,0:T(8,128)S(1)} custom-call(bf16[16,9344]{1,0:T(8,128)(2,1)S(1)} %get-tuple-element.11.rows_ref.two_ref, bf16[256,2304]{1,0:T(8,128)(2,1)S(1)} %get-tuple-element.13.table_ref, f32[128,128]{1,0:T(8,128)S(1)} %get-tuple-element.14.energy_ref), custom_call_target="tpu_custom_call" | custom-call | tf_op jit(solution)/shard_map/cond/branch_1_fun/pallas_call | solution.py:42
  33.9 1.1 %branch_1_fun.4 = (bf16[288,1152]{1,0:T(8,128)(2,1)S(1)}, bf16[288,1152]{1,0:T(8,128)(2,1)S(1)}) custom-call(bf16[16,9344]{1,0:T(8,128)(2,1)S(1)} %get-tuple-element.10.one_ref, bf16[16,9344]{1,0:T(8,128)(2,1)S(1)} %get-tuple-element.11.rows_ref.two_ref, f32[576,128]{1,0:T(8,128)S(1)} %get-tuple-element.12.one_logits_ref, ...), custom_call_target="tpu_custom_call" | custom-call | tf_op jit(solution)/shard_map/cond/branch_1_fun/pallas_call | solution.py:42
  35.0 2.2 %collective-permute-start = (bf16[288,1152]{1,0:T(8,128)(2,1)S(1)}, bf16[288,1152]{1,0:T(8,128)(2,1)S(1)}, u32[]{:S(2)}, u32[]{:S(2)}) collective-permute-start(bf16[288,1152]{1,0:T(8,128)(2,1)S(1)} %get-tuple-element.16), channel_id=1, source_target_pairs={{0,8},{8,0},{1,9},{9,1},{2,10},{10,2},{3,11},{11,3},{4,12},{12,4},... | collective-permute-start | bytes 1990664 | tf_op jit(solution)/shard_map/cond/branch_1_fun/ppermute | solution.py:433
  37.3 1.8 %collective-permute-done.value_ref = bf16[288,1152]{1,0:T(8,128)(2,1)S(1)} collective-permute-done((bf16[288,1152]{1,0:T(8,128)(2,1)S(1)}, bf16[288,1152]{1,0:T(8,128)(2,1)S(1)}, u32[]{:S(2)}, u32[]{:S(2)}) %collective-permute-start) | collective-permute-done | bytes 663584 | tf_op jit(solution)/shard_map/cond/branch_1_fun/ppermute | solution.py:433
  39.1 2.0 %all-to-all-done.1.stats_ref = f32[32,2,128]{2,1,0:T(2,128)S(1)} async-done(((f32[32,2,128]{2,1,0:T(2,128)}), f32[32,2,128]{2,1,0:T(2,128)S(1)}, u32[]{:S(2)}, u32[]{:S(2)}) %all-to-all-start.1) | async-done | bytes 32800 | tf_op jit(solution)/shard_map/all_to_all | solution.py:430
  41.1 2.7 %shard_map.79 = (bf16[16,88,128]{2,1,0:T(8,128)(2,1)}, f32[1,128]{1,0:T(1,128)S(1)}) custom-call(f32[32,2,128]{2,1,0:T(2,128)S(1)} %all-to-all-done.1.stats_ref, bf16[288,1152]{1,0:T(8,128)(2,1)S(1)} %get-tuple-element.40.mine_ref, bf16[288,1152]{1,0:T(8,128)(2,1)S(1)} %get-tuple-element.41.other_ref), custom_call_target="tpu_custom_call" | custom-call | tf_op jit(solution)/shard_map/pallas_call | solution.py:42
  43.8 12.3 %all-to-all-start.2 = ((bf16[16,88,128]{2,1,0:T(8,128)(2,1)}), bf16[16,88,128]{2,1,0:T(8,128)(2,1)S(1)}, u32[]{:S(2)}, u32[]{:S(2)}) async-start(bf16[16,88,128]{2,1,0:T(8,128)(2,1)} %get-tuple-element.42), calls=%async_computation.2 | async-start | bytes 720896 | tf_op jit(solution)/shard_map/all_to_all | solution.py:430
  56.2 0.6 dynamic-slice_bitcast_fusion
  56.7 11.3 %all-to-all-done.2.parts_ref = bf16[16,88,128]{2,1,0:T(8,128)(2,1)S(1)} async-done(((bf16[16,88,128]{2,1,0:T(8,128)(2,1)}), bf16[16,88,128]{2,1,0:T(8,128)(2,1)S(1)}, u32[]{:S(2)}, u32[]{:S(2)}) %all-to-all-start.2) | async-done | bytes 360480 | tf_op jit(solution)/shard_map/all_to_all | solution.py:430
  68.1 0.8 %shard_map.80 = (f32[50,144]{1,0:T(8,128)}, f32[50,64]{1,0:T(8,128)}) custom-call(bf16[16,88,128]{2,1,0:T(8,128)(2,1)S(1)} %all-to-all-done.2.parts_ref), custom_call_target="tpu_custom_call" | custom-call | tf_op jit(solution)/shard_map/pallas_call | solution.py:42
  (1 shorter events, 0.0 us)
Async XLA Ops:
  2.6 17.6 %all-to-all-start = ((bf16[8,2,9344]{2,1,0:T(2,128)(2,1)}), bf16[8,2,9344]{2,1,0:T(2,128)(2,1)S(1)}, u32[]{:S(2)}, u32[]{:S(2)}) async-start(bf16[8,2,9344]{2,1,0:T(2,128)(2,1)} %shard_map.76), calls=%async_computation | async-start | bytes 598016 | tf_op jit(solution)/shard_map/all_to_all | solution.py:430
  10.2 1.2 %copy-start = (bf16[50,9216]{1,0:T(8,128)(2,1)S(1)}, bf16[50,9216]{1,0:T(8,128)(2,1)}, u32[]{:S(2)}) copy-start(bf16[50,9216]{1,0:T(8,128)(2,1)} %classes_ref.1) | copy-start | bytes 2764804
  20.3 12.6 %collective-permute-start.1 = (bf16[16,9344]{1,0:T(8,128)(2,1)S(1)}, bf16[16,9344]{1,0:T(8,128)(2,1)S(1)}, u32[]{:S(2)}, u32[]{:S(2)}) collective-permute-start(bf16[16,9344]{1,0:T(8,128)(2,1)S(1)} %reshape.16.rows_ref), channel_id=1, source_target_pairs={{0,128},{128,0},{1,129},{129,1},{2,130},{130,2},{3,131},{131,3},{4... | collective-permute-start | bytes 897032 | tf_op jit(solution)/shard_map/ppermute | solution.py:433
  26.7 14.5 %all-to-all-start.1 = ((f32[32,2,128]{2,1,0:T(2,128)}), f32[32,2,128]{2,1,0:T(2,128)S(1)}, u32[]{:S(2)}, u32[]{:S(2)}) async-start(f32[32,2,128]{2,1,0:T(2,128)} %get-tuple-element.38), calls=%async_computation.1 | async-start | bytes 65536 | tf_op jit(solution)/shard_map/all_to_all | solution.py:430
  35.0 4.0 %collective-permute-start = (bf16[288,1152]{1,0:T(8,128)(2,1)S(1)}, bf16[288,1152]{1,0:T(8,128)(2,1)S(1)}, u32[]{:S(2)}, u32[]{:S(2)}) collective-permute-start(bf16[288,1152]{1,0:T(8,128)(2,1)S(1)} %get-tuple-element.16), channel_id=1, source_target_pairs={{0,8},{8,0},{1,9},{9,1},{2,10},{10,2},{3,11},{11,3},{4,12},{12,4},... | collective-permute-start | bytes 1990664 | tf_op jit(solution)/shard_map/cond/branch_1_fun/ppermute | solution.py:433
  43.8 24.2 %all-to-all-start.2 = ((bf16[16,88,128]{2,1,0:T(8,128)(2,1)}), bf16[16,88,128]{2,1,0:T(8,128)(2,1)S(1)}, u32[]{:S(2)}, u32[]{:S(2)}) async-start(bf16[16,88,128]{2,1,0:T(8,128)(2,1)} %get-tuple-element.42), calls=%async_computation.2 | async-start | bytes 720896 | tf_op jit(solution)/shard_map/all_to_all | solution.py:430

commit v8 on v7

--- a/solution.py
+++ b/solution.py
@@ -75,7 +75,9 @@
     first = jnp.broadcast_to(cands[0:1, :], (ROWS, part))
     second = jnp.broadcast_to(cands[1:2, :], (ROWS, part))
     row = rows_of((ROWS, part))
-    low = (row // 2) * class_block
+    second_core = lax.axis_index("core") == 1
+    owner = jnp.where(second_core, ROWS // 2 - 1 - row // 2, row // 2)
+    low = owner * class_block
     hit = ((first >= low) & (first < low + class_block)) | (
         (second >= low) & (second < low + class_block)
     )
@@ -159,7 +161,9 @@
     marks = jnp.where(lane >= P_LANE, meta, 0.0)
     valid = jnp.sum(marks, axis=1, keepdims=True)
     own = jnp.sum(marks * (lane - P_LANE).astype(F32), axis=1, keepdims=True)
-    source = (rows_of(meta.shape) % ROWS // 2 * 4).astype(F32)
+    source = rows_of(meta.shape) % ROWS // 2
+    source = jnp.where(lax.axis_index("core") == 1, ROWS // 2 - 1 - source, source)
+    source = (source * 4).astype(F32)
     spot = (lane.astype(F32) == source + own) & (valid > 0.5)
     return flags, spot
 
@@ -347,7 +351,10 @@
         pay_ref[d, 0:HALF, :] = spare
         pay_ref[d, PAY_ROWS : PAY_ROWS + 16, :] = tail
     copies = [
-        pltpu.make_async_copy(pay_ref.at[d], out_any.at[d], sems.at[d]) for d in range(TARGETS)
+        pltpu.make_async_copy(
+            pay_ref.at[d], out_any.at[jnp.where(core == 1, TARGETS - 1 - d, d)], sems.at[d]
+        )
+        for d in range(TARGETS)
     ]
     started = 0
     base = (ROTATIONS - CHUNKS * near) * 2 * ROWS
@@ -429,6 +436,18 @@
     def swap(value, axes):
         return lax.all_to_all(value, axes, split_axis=0, concat_axis=0, tiled=True)
 
+    def swap_rows(value):
+        groups = [list(range(8)), list(range(15, 7, -1))]
+        return lax.all_to_all(value, ("core", "cls"), 0, 0, axis_index_groups=groups, tiled=True)
+
+    def swap_both_ways(value, axes):
+        count = value.shape[0]
+        ahead = [2 * i for i in range(count)]
+        groups = [ahead, [i + 1 for i in reversed(ahead)]]
+        return lax.all_to_all(
+            value, axes + ("core",), 0, 0, axis_index_groups=groups, tiled=True
+        )
+
     def flip(value, axis):
         return lax.ppermute(value, axis, [(0, 1), (1, 0)])
 
@@ -454,7 +473,7 @@
             pltpu.SemaphoreType.DMA((8,)),
         ],
     )
-    rows = swap(packed, "cls").reshape(ROWS, width)
+    rows = swap_rows(packed).reshape(ROWS, width)
     table, energy = call(
         prep_body,
         (shape((BLOCK, ROTATIONS // 4 * BLOCK), BF16), shape((LANES, LANES), F32)),
@@ -505,7 +524,7 @@
             pltpu.SemaphoreType.DMA((TARGETS,)),
         ],
     )
-    parts = swap(pay, ("xh", "z"))
+    parts = swap_both_ways(pay, ("xh", "z"))
     sums, weight_sums = call(
         final_body, (shape((CLASSES, SLICE), F32), shape((CLASSES, CYCLES), F32)), parts
     )

time: 69.8 us -> 67.8 us (0.971)
  waiting for transfers between devices: 23.6 us -> 16.5 us
  starting transfers between devices: 32.8 us -> 38.3 us
    all_to_all x0 -> x2, starting transfers between devices: none -> 22.3 us  [the longest x1 14.4 us: swap_both_ways(): lax.all_to_all(value, axes + ('core',), 0, 0, axis_index_groups=groups, t...]
    all_to_all x3 -> x1, waiting for transfers between devices: 21.8 us -> 1.66 us  [swap(): return lax.all_to_all(value, axes, split_axis=0, concat_axis=0, tiled=True)]
    all_to_all x3 -> x1, starting transfers between devices: 26.2 us -> 9.82 us  [swap(): return lax.all_to_all(value, axes, split_axis=0, concat_axis=0, tiled=True)]
    all_to_all x0 -> x2, waiting for transfers between devices: none -> 13.1 us  [the longest x1 8.91 us: swap_both_ways(): lax.all_to_all(value, axes + ('core',), 0, 0, axis_index_groups=groups, t...]
  transfers between devices with their start and end apart: 5 -> 5, of which waited for: 4 -> 4; matrix products, arithmetic and copies ran while one was open for 1% -> 1% of each run, Pallas kernels for 6% -> 7%
where the time goes in v8:
time: 67.8 us; the launch traced here: 67.3 us
  starting transfers between devices  38.3 us (56%)
  waiting for transfers between devices  16.5 us (24%)
  Pallas kernels  9.89 us (15%)
  local copies, waits for them, and re-layouts  1.91 us (3%)
  between operations  0.69 us (1%)
    all_to_all x1, starting transfers between devices, swap_both_ways(): lax.all_to_all(value, axes + ('core',), 0, 0, axis_index_groups=groups, t...  14.4 us
    pallas_call x8, Pallas kernels, call(): pl.pallas_call(body, out_shape=outs, scratch_shapes=list(scratch), compil...  9.89 us
    all_to_all x1, starting transfers between devices, swap(): return lax.all_to_all(value, axes, split_axis=0, concat_axis=0, tiled=True)  9.82 us
    all_to_all x1, waiting for transfers between devices, swap_both_ways(): lax.all_to_all(value, axes + ('core',), 0, 0, axis_index_groups=groups, t...  8.91 us
    all_to_all x1, starting transfers between devices, swap_rows(): lax.all_to_all(value, ('core', 'cls'), 0, 0, axis_index_groups=groups, ti...  7.94 us
    ppermute x2, starting transfers between devices, flip(): return lax.ppermute(value, axis, [(0, 1), (1, 0)])  6.21 us
    all_to_all x1, waiting for transfers between devices, swap_rows(): lax.all_to_all(value, ('core', 'cls'), 0, 0, axis_index_groups=groups, ti...  4.17 us
    ppermute x2, waiting for transfers between devices, flip(): return lax.ppermute(value, axis, [(0, 1), (1, 0)])  1.72 us
  transfers between devices with their start and end apart: 5, of which 4 were waited for; matrix products, arithmetic and copies ran while one was open for 1% of the time, Pallas kernels for 7%

profile of v8, /device:TPU:1, one launch (start us, length us, event | category | flops | bytes accessed | tf_op | source)
XLA Modules:
  0.0 67.3 jit_solution(8571867668498812497)
XLA Ops:
  0.6 1.9 %shard_map.76 = bf16[8,2,9344]{2,1,0:T(2,128)(2,1)} custom-call(bf16[4,9216]{1,0:T(4,128)(2,1)} %refs_0_.1, f32[4,64]{1,0:T(4,128)} %refs_1_.1, f32[1,64]{1,0:T(1,128)} %bitcast.6, s32[2,4]{1,0:T(2,128)} %bitcast.5), custom_call_target="tpu_custom_call" | custom-call | tf_op jit(solution)/shard_map/pallas_call | solution.py:42
  2.6 7.9 %all-to-all-start = ((bf16[8,2,9344]{2,1,0:T(2,128)(2,1)}), bf16[8,2,9344]{2,1,0:T(2,128)(2,1)S(1)}, u32[]{:S(2)}, u32[]{:S(2)}) async-start(bf16[8,2,9344]{2,1,0:T(2,128)(2,1)} %shard_map.76), calls=%async_computation | async-start | bytes 598016 | tf_op jit(solution)/shard_map/all_to_all | solution.py:441
  10.5 0.0 copy-start
  10.5 1.2 %copy-done = bf16[50,9216]{1,0:T(8,128)(2,1)S(1)} copy-done((bf16[50,9216]{1,0:T(8,128)(2,1)S(1)}, bf16[50,9216]{1,0:T(8,128)(2,1)}, u32[]{:S(2)}) %copy-start) | copy-done | bytes 921624
  11.7 0.3 shard_map.77
  12.1 4.2 %all-to-all-done = bf16[8,2,9344]{2,1,0:T(2,128)(2,1)S(1)} async-done(((bf16[8,2,9344]{2,1,0:T(2,128)(2,1)}), bf16[8,2,9344]{2,1,0:T(2,128)(2,1)S(1)}, u32[]{:S(2)}, u32[]{:S(2)}) %all-to-all-start) | async-done | bytes 299040 | tf_op jit(solution)/shard_map/all_to_all | solution.py:441
  16.2 0.1 reshape.16.rows_ref
  16.4 3.5 %collective-permute-start.1 = (bf16[16,9344]{1,0:T(8,128)(2,1)S(1)}, bf16[16,9344]{1,0:T(8,128)(2,1)S(1)}, u32[]{:S(2)}, u32[]{:S(2)}) collective-permute-start(bf16[16,9344]{1,0:T(8,128)(2,1)S(1)} %reshape.16.rows_ref), channel_id=1, source_target_pairs={{0,128},{128,0},{1,129},{129,1},{2,130},{130,2},{3,131},{131,3},{4... | collective-permute-start | bytes 897032 | tf_op jit(solution)/shard_map/ppermute | solution.py:452
  19.9 1.9 %shard_map.78 = (f32[576,128]{1,0:T(8,128)S(1)}, f32[32,2,128]{2,1,0:T(2,128)}) custom-call(bf16[16,9344]{1,0:T(8,128)(2,1)S(1)} %reshape.16.rows_ref, bf16[256,2304]{1,0:T(8,128)(2,1)S(1)} %get-tuple-element.36.table_ref, f32[128,128]{1,0:T(8,128)S(1)} %get-tuple-element.37.energy_ref), custom_call_target="tpu_custom_call" | custom-call | tf_op jit(solution)/shard_map/pallas_call | solution.py:42
  21.8 9.8 %all-to-all-start.1 = ((f32[32,2,128]{2,1,0:T(2,128)}), f32[32,2,128]{2,1,0:T(2,128)S(1)}, u32[]{:S(2)}, u32[]{:S(2)}) async-start(f32[32,2,128]{2,1,0:T(2,128)} %get-tuple-element.38), calls=%async_computation.1 | async-start | bytes 65536 | tf_op jit(solution)/shard_map/all_to_all | solution.py:437
  31.7 0.0 collective-permute-done.1
  31.7 6.6 %conditional.1 = (bf16[288,1152]{1,0:T(8,128)(2,1)S(1)}, bf16[288,1152]{1,0:T(8,128)(2,1)S(1)}) conditional(s32[]{:T(128)} %convert_element_type.3, () %tuple.18, (bf16[16,9344]{1,0:T(8,128)(2,1)S(1)}, bf16[256,2304]{1,0:T(8,128)(2,1)S(1)}, f32[128,128]{1,0:T(8,128)S(1)}, bf16[16,9344]{1,0:T(8,128)(2,1)S(1)}, f32[576,128]{1,0:T(8,128)S(1)}) %tuple.19), branch_computations={%region_0.0_spmd, %region_1.0_spmd} | conditional | bytes 2654264 | solution.py:512
  31.7 1.1 %branch_1_fun.3.two_logits_ref = f32[576,128]{1,0:T(8,128)S(1)} custom-call(bf16[16,9344]{1,0:T(8,128)(2,1)S(1)} %get-tuple-element.11.rows_ref.two_ref, bf16[256,2304]{1,0:T(8,128)(2,1)S(1)} %get-tuple-element.13.table_ref, f32[128,128]{1,0:T(8,128)S(1)} %get-tuple-element.14.energy_ref), custom_call_target="tpu_custom_call" | custom-call | tf_op jit(solution)/shard_map/cond/branch_1_fun/pallas_call | solution.py:42
  32.8 1.1 %branch_1_fun.4 = (bf16[288,1152]{1,0:T(8,128)(2,1)S(1)}, bf16[288,1152]{1,0:T(8,128)(2,1)S(1)}) custom-call(bf16[16,9344]{1,0:T(8,128)(2,1)S(1)} %get-tuple-element.10.one_ref, bf16[16,9344]{1,0:T(8,128)(2,1)S(1)} %get-tuple-element.11.rows_ref.two_ref, f32[576,128]{1,0:T(8,128)S(1)} %get-tuple-element.12.one_logits_ref, ...), custom_call_target="tpu_custom_call" | custom-call | tf_op jit(solution)/shard_map/cond/branch_1_fun/pallas_call | solution.py:42
  33.9 2.7 %collective-permute-start = (bf16[288,1152]{1,0:T(8,128)(2,1)S(1)}, bf16[288,1152]{1,0:T(8,128)(2,1)S(1)}, u32[]{:S(2)}, u32[]{:S(2)}) collective-permute-start(bf16[288,1152]{1,0:T(8,128)(2,1)S(1)} %get-tuple-element.16), channel_id=1, source_target_pairs={{0,8},{8,0},{1,9},{9,1},{2,10},{10,2},{3,11},{11,3},{4,12},{12,4},... | collective-permute-start | bytes 1990664 | tf_op jit(solution)/shard_map/cond/branch_1_fun/ppermute | solution.py:452
  36.5 1.7 %collective-permute-done.value_ref = bf16[288,1152]{1,0:T(8,128)(2,1)S(1)} collective-permute-done((bf16[288,1152]{1,0:T(8,128)(2,1)S(1)}, bf16[288,1152]{1,0:T(8,128)(2,1)S(1)}, u32[]{:S(2)}, u32[]{:S(2)}) %collective-permute-start) | collective-permute-done | bytes 663584 | tf_op jit(solution)/shard_map/cond/branch_1_fun/ppermute | solution.py:452
  38.3 1.7 %all-to-all-done.1.stats_ref = f32[32,2,128]{2,1,0:T(2,128)S(1)} async-done(((f32[32,2,128]{2,1,0:T(2,128)}), f32[32,2,128]{2,1,0:T(2,128)S(1)}, u32[]{:S(2)}, u32[]{:S(2)}) %all-to-all-start.1) | async-done | bytes 32800 | tf_op jit(solution)/shard_map/all_to_all | solution.py:437
  40.0 2.7 %shard_map.79 = (bf16[16,88,128]{2,1,0:T(8,128)(2,1)}, f32[1,128]{1,0:T(1,128)S(1)}) custom-call(f32[32,2,128]{2,1,0:T(2,128)S(1)} %all-to-all-done.1.stats_ref, bf16[288,1152]{1,0:T(8,128)(2,1)S(1)} %get-tuple-element.40.mine_ref, bf16[288,1152]{1,0:T(8,128)(2,1)S(1)} %get-tuple-element.41.other_ref), custom_call_target="tpu_custom_call" | custom-call | tf_op jit(solution)/shard_map/pallas_call | solution.py:42
  42.7 14.4 %all-to-all-start.2 = ((bf16[16,88,128]{2,1,0:T(8,128)(2,1)}), bf16[16,88,128]{2,1,0:T(8,128)(2,1)S(1)}, u32[]{:S(2)}, u32[]{:S(2)}) async-start(bf16[16,88,128]{2,1,0:T(8,128)(2,1)} %get-tuple-element.42), calls=%async_computation.2 | async-start | bytes 720896 | tf_op jit(solution)/shard_map/all_to_all | solution.py:447
  57.0 0.6 dynamic-slice_bitcast_fusion
  57.6 8.9 %all-to-all-done.2.parts_ref = bf16[16,88,128]{2,1,0:T(8,128)(2,1)S(1)} async-done(((bf16[16,88,128]{2,1,0:T(8,128)(2,1)}), bf16[16,88,128]{2,1,0:T(8,128)(2,1)S(1)}, u32[]{:S(2)}, u32[]{:S(2)}) %all-to-all-start.2) | async-done | bytes 360480 | tf_op jit(solution)/shard_map/all_to_all | solution.py:447
  66.5 0.8 %shard_map.80 = (f32[50,144]{1,0:T(8,128)}, f32[50,64]{1,0:T(8,128)}) custom-call(bf16[16,88,128]{2,1,0:T(8,128)(2,1)S(1)} %all-to-all-done.2.parts_ref), custom_call_target="tpu_custom_call" | custom-call | tf_op jit(solution)/shard_map/pallas_call | solution.py:42
  (1 shorter events, 0.0 us)
Async XLA Ops:
  2.6 13.7 %all-to-all-start = ((bf16[8,2,9344]{2,1,0:T(2,128)(2,1)}), bf16[8,2,9344]{2,1,0:T(2,128)(2,1)S(1)}, u32[]{:S(2)}, u32[]{:S(2)}) async-start(bf16[8,2,9344]{2,1,0:T(2,128)(2,1)} %shard_map.76), calls=%async_computation | async-start | bytes 598016 | tf_op jit(solution)/shard_map/all_to_all | solution.py:441
  10.5 1.2 %copy-start = (bf16[50,9216]{1,0:T(8,128)(2,1)S(1)}, bf16[50,9216]{1,0:T(8,128)(2,1)}, u32[]{:S(2)}) copy-start(bf16[50,9216]{1,0:T(8,128)(2,1)} %classes_ref.1) | copy-start | bytes 2764804
  16.4 15.3 %collective-permute-start.1 = (bf16[16,9344]{1,0:T(8,128)(2,1)S(1)}, bf16[16,9344]{1,0:T(8,128)(2,1)S(1)}, u32[]{:S(2)}, u32[]{:S(2)}) collective-permute-start(bf16[16,9344]{1,0:T(8,128)(2,1)S(1)} %reshape.16.rows_ref), channel_id=1, source_target_pairs={{0,128},{128,0},{1,129},{129,1},{2,130},{130,2},{3,131},{131,3},{4... | collective-permute-start | bytes 897032 | tf_op jit(solution)/shard_map/ppermute | solution.py:452
  21.8 18.1 %all-to-all-start.1 = ((f32[32,2,128]{2,1,0:T(2,128)}), f32[32,2,128]{2,1,0:T(2,128)S(1)}, u32[]{:S(2)}, u32[]{:S(2)}) async-start(f32[32,2,128]{2,1,0:T(2,128)} %get-tuple-element.38), calls=%async_computation.1 | async-start | bytes 65536 | tf_op jit(solution)/shard_map/all_to_all | solution.py:437
  33.9 4.4 %collective-permute-start = (bf16[288,1152]{1,0:T(8,128)(2,1)S(1)}, bf16[288,1152]{1,0:T(8,128)(2,1)S(1)}, u32[]{:S(2)}, u32[]{:S(2)}) collective-permute-start(bf16[288,1152]{1,0:T(8,128)(2,1)S(1)} %get-tuple-element.16), channel_id=1, source_target_pairs={{0,8},{8,0},{1,9},{9,1},{2,10},{10,2},{3,11},{11,3},{4,12},{12,4},... | collective-permute-start | bytes 1990664 | tf_op jit(solution)/shard_map/cond/branch_1_fun/ppermute | solution.py:452
  42.7 23.9 %all-to-all-start.2 = ((bf16[16,88,128]{2,1,0:T(8,128)(2,1)}), bf16[16,88,128]{2,1,0:T(8,128)(2,1)S(1)}, u32[]{:S(2)}, u32[]{:S(2)}) async-start(bf16[16,88,128]{2,1,0:T(8,128)(2,1)} %get-tuple-element.42), calls=%async_computation.2 | async-start | bytes 720896 | tf_op jit(solution)/shard_map/all_to_all | solution.py:447

commit v9 on v8

--- a/solution.py
+++ b/solution.py
@@ -15,6 +15,11 @@
 TURNS = 2 * ROTATIONS - 4
 GROUPS = 64
 TARGETS = GROUPS // 4
+ROW_ORDER = ((1, 0), (7, 3))
+SUM_ORDER = (
+    [0, 1, 2, 3, 4, 5, 6, 7, 8, 9, 10, 11, 12, 13, 14, 15],
+    [15, 14, 13, 12, 11, 10, 9, 8, 7, 6, 5, 4, 3, 2, 1, 0],
+)
 DEPTH = 2 * ROTATIONS * ROWS
 CLASSES = 50
 SLICE = FEATURES // GROUPS
@@ -76,7 +81,7 @@
     second = jnp.broadcast_to(cands[1:2, :], (ROWS, part))
     row = rows_of((ROWS, part))
     second_core = lax.axis_index("core") == 1
-    owner = jnp.where(second_core, ROWS // 2 - 1 - row // 2, row // 2)
+    owner = (row // 2 * jnp.where(second_core, ROW_ORDER[1][0], ROW_ORDER[0][0]) + jnp.where(second_core, ROW_ORDER[1][1], ROW_ORDER[0][1])) % 8
     low = owner * class_block
     hit = ((first >= low) & (first < low + class_block)) | (
         (second >= low) & (second < low + class_block)
@@ -162,7 +167,8 @@
     valid = jnp.sum(marks, axis=1, keepdims=True)
     own = jnp.sum(marks * (lane - P_LANE).astype(F32), axis=1, keepdims=True)
     source = rows_of(meta.shape) % ROWS // 2
-    source = jnp.where(lax.axis_index("core") == 1, ROWS // 2 - 1 - source, source)
+    second_core = lax.axis_index("core") == 1
+    source = (source * jnp.where(second_core, ROW_ORDER[1][0], ROW_ORDER[0][0]) + jnp.where(second_core, ROW_ORDER[1][1], ROW_ORDER[0][1])) % 8
     source = (source * 4).astype(F32)
     spot = (lane.astype(F32) == source + own) & (valid > 0.5)
     return flags, spot
@@ -352,7 +358,7 @@
         pay_ref[d, PAY_ROWS : PAY_ROWS + 16, :] = tail
     copies = [
         pltpu.make_async_copy(
-            pay_ref.at[d], out_any.at[jnp.where(core == 1, TARGETS - 1 - d, d)], sems.at[d]
+            pay_ref.at[d], out_any.at[jnp.where(core == 1, SUM_ORDER[1].index(d), SUM_ORDER[0].index(d))], sems.at[d]
         )
         for d in range(TARGETS)
     ]
@@ -437,13 +443,11 @@
         return lax.all_to_all(value, axes, split_axis=0, concat_axis=0, tiled=True)
 
     def swap_rows(value):
-        groups = [list(range(8)), list(range(15, 7, -1))]
+        groups = [[8 * c + (ROW_ORDER[c][0] * p + ROW_ORDER[c][1]) % 8 for p in range(8)] for c in range(2)]
         return lax.all_to_all(value, ("core", "cls"), 0, 0, axis_index_groups=groups, tiled=True)
 
     def swap_both_ways(value, axes):
-        count = value.shape[0]
-        ahead = [2 * i for i in range(count)]
-        groups = [ahead, [i + 1 for i in reversed(ahead)]]
+        groups = [[2 * SUM_ORDER[c][p] + c for p in range(TARGETS)] for c in range(2)]
         return lax.all_to_all(
             value, axes + ("core",), 0, 0, axis_index_groups=groups, tiled=True
         )

time: 67.8 us -> 67.8 us (level)
    all_to_all x1, waiting for transfers between devices: 4.17 us -> 4.99 us  [swap_rows(): lax.all_to_all(value, ('core', 'cls'), 0, 0, axis_index_groups=groups, ti...]
    all_to_all x1, starting transfers between devices: 9.82 us -> 9.03 us  [swap(): return lax.all_to_all(value, axes, split_axis=0, concat_axis=0, tiled=True)]
where the time goes in v9:
time: 67.8 us; the launch traced here: 67.3 us
  starting transfers between devices  37.7 us (56%)
  waiting for transfers between devices  17.1 us (25%)
  Pallas kernels  9.91 us (15%)
  local copies, waits for them, and re-layouts  1.91 us (3%)
  between operations  0.69 us (1%)
    all_to_all x1, starting transfers between devices, swap_both_ways(): lax.all_to_all(value, axes + ('core',), 0, 0, axis_index_groups=groups, t...  14.5 us
    pallas_call x8, Pallas kernels, call(): pl.pallas_call(body, out_shape=outs, scratch_shapes=list(scratch), compil...  9.91 us
    all_to_all x1, starting transfers between devices, swap(): return lax.all_to_all(value, axes, split_axis=0, concat_axis=0, tiled=True)  9.03 us
    all_to_all x1, waiting for transfers between devices, swap_both_ways(): lax.all_to_all(value, axes + ('core',), 0, 0, axis_index_groups=groups, t...  8.91 us
    all_to_all x1, starting transfers between devices, swap_rows(): lax.all_to_all(value, ('core', 'cls'), 0, 0, axis_index_groups=groups, ti...  8.28 us
    ppermute x2, starting transfers between devices, flip(): return lax.ppermute(value, axis, [(0, 1), (1, 0)])  5.84 us
    all_to_all x1, waiting for transfers between devices, swap_rows(): lax.all_to_all(value, ('core', 'cls'), 0, 0, axis_index_groups=groups, ti...  4.99 us
    ppermute x2, waiting for transfers between devices, flip(): return lax.ppermute(value, axis, [(0, 1), (1, 0)])  1.72 us
  transfers between devices with their start and end apart: 5, of which 4 were waited for; matrix products, arithmetic and copies ran while one was open for 1% of the time, Pallas kernels for 7%

profile of v9, /device:TPU:1, one launch (start us, length us, event | category | flops | bytes accessed | tf_op | source)
XLA Modules:
  0.0 67.3 jit_solution(975320604178867801)
XLA Ops:
  0.6 1.9 %shard_map.76 = bf16[8,2,9344]{2,1,0:T(2,128)(2,1)} custom-call(bf16[4,9216]{1,0:T(4,128)(2,1)} %refs_0_.1, f32[4,64]{1,0:T(4,128)} %refs_1_.1, f32[1,64]{1,0:T(1,128)} %bitcast.6, s32[2,4]{1,0:T(2,128)} %bitcast.5), custom_call_target="tpu_custom_call" | custom-call | tf_op jit(solution)/shard_map/pallas_call | solution.py:47
  2.6 8.3 %all-to-all-start = ((bf16[8,2,9344]{2,1,0:T(2,128)(2,1)}), bf16[8,2,9344]{2,1,0:T(2,128)(2,1)S(1)}, u32[]{:S(2)}, u32[]{:S(2)}) async-start(bf16[8,2,9344]{2,1,0:T(2,128)(2,1)} %shard_map.76), calls=%async_computation | async-start | bytes 598016 | tf_op jit(solution)/shard_map/all_to_all | solution.py:447
  10.8 0.0 copy-start
  10.9 1.2 %copy-done = bf16[50,9216]{1,0:T(8,128)(2,1)S(1)} copy-done((bf16[50,9216]{1,0:T(8,128)(2,1)S(1)}, bf16[50,9216]{1,0:T(8,128)(2,1)}, u32[]{:S(2)}) %copy-start) | copy-done | bytes 921624
  12.1 0.3 shard_map.77
  12.4 5.0 %all-to-all-done = bf16[8,2,9344]{2,1,0:T(2,128)(2,1)S(1)} async-done(((bf16[8,2,9344]{2,1,0:T(2,128)(2,1)}), bf16[8,2,9344]{2,1,0:T(2,128)(2,1)S(1)}, u32[]{:S(2)}, u32[]{:S(2)}) %all-to-all-start) | async-done | bytes 299040 | tf_op jit(solution)/shard_map/all_to_all | solution.py:447
  17.4 0.1 reshape.16.rows_ref
  17.5 3.1 %collective-permute-start.1 = (bf16[16,9344]{1,0:T(8,128)(2,1)S(1)}, bf16[16,9344]{1,0:T(8,128)(2,1)S(1)}, u32[]{:S(2)}, u32[]{:S(2)}) collective-permute-start(bf16[16,9344]{1,0:T(8,128)(2,1)S(1)} %reshape.16.rows_ref), channel_id=1, source_target_pairs={{0,128},{128,0},{1,129},{129,1},{2,130},{130,2},{3,131},{131,3},{4... | collective-permute-start | bytes 897032 | tf_op jit(solution)/shard_map/ppermute | solution.py:456
  20.7 1.9 %shard_map.78 = (f32[576,128]{1,0:T(8,128)S(1)}, f32[32,2,128]{2,1,0:T(2,128)}) custom-call(bf16[16,9344]{1,0:T(8,128)(2,1)S(1)} %reshape.16.rows_ref, bf16[256,2304]{1,0:T(8,128)(2,1)S(1)} %get-tuple-element.36.table_ref, f32[128,128]{1,0:T(8,128)S(1)} %get-tuple-element.37.energy_ref), custom_call_target="tpu_custom_call" | custom-call | tf_op jit(solution)/shard_map/pallas_call | solution.py:47
  22.6 9.0 %all-to-all-start.1 = ((f32[32,2,128]{2,1,0:T(2,128)}), f32[32,2,128]{2,1,0:T(2,128)S(1)}, u32[]{:S(2)}, u32[]{:S(2)}) async-start(f32[32,2,128]{2,1,0:T(2,128)} %get-tuple-element.38), calls=%async_computation.1 | async-start | bytes 65536 | tf_op jit(solution)/shard_map/all_to_all | solution.py:443
  31.6 0.0 collective-permute-done.1
  31.6 6.7 %conditional.1 = (bf16[288,1152]{1,0:T(8,128)(2,1)S(1)}, bf16[288,1152]{1,0:T(8,128)(2,1)S(1)}) conditional(s32[]{:T(128)} %convert_element_type.3, () %tuple.18, (bf16[16,9344]{1,0:T(8,128)(2,1)S(1)}, bf16[256,2304]{1,0:T(8,128)(2,1)S(1)}, f32[128,128]{1,0:T(8,128)S(1)}, bf16[16,9344]{1,0:T(8,128)(2,1)S(1)}, f32[576,128]{1,0:T(8,128)S(1)}) %tuple.19), branch_computations={%region_0.0_spmd, %region_1.0_spmd} | conditional | bytes 2654264 | solution.py:516
  31.6 1.1 %branch_1_fun.3.two_logits_ref = f32[576,128]{1,0:T(8,128)S(1)} custom-call(bf16[16,9344]{1,0:T(8,128)(2,1)S(1)} %get-tuple-element.11.rows_ref.two_ref, bf16[256,2304]{1,0:T(8,128)(2,1)S(1)} %get-tuple-element.13.table_ref, f32[128,128]{1,0:T(8,128)S(1)} %get-tuple-element.14.energy_ref), custom_call_target="tpu_custom_call" | custom-call | tf_op jit(solution)/shard_map/cond/branch_1_fun/pallas_call | solution.py:47
  32.7 1.1 %branch_1_fun.4 = (bf16[288,1152]{1,0:T(8,128)(2,1)S(1)}, bf16[288,1152]{1,0:T(8,128)(2,1)S(1)}) custom-call(bf16[16,9344]{1,0:T(8,128)(2,1)S(1)} %get-tuple-element.10.one_ref, bf16[16,9344]{1,0:T(8,128)(2,1)S(1)} %get-tuple-element.11.rows_ref.two_ref, f32[576,128]{1,0:T(8,128)S(1)} %get-tuple-element.12.one_logits_ref, ...), custom_call_target="tpu_custom_call" | custom-call | tf_op jit(solution)/shard_map/cond/branch_1_fun/pallas_call | solution.py:47
  33.8 2.7 %collective-permute-start = (bf16[288,1152]{1,0:T(8,128)(2,1)S(1)}, bf16[288,1152]{1,0:T(8,128)(2,1)S(1)}, u32[]{:S(2)}, u32[]{:S(2)}) collective-permute-start(bf16[288,1152]{1,0:T(8,128)(2,1)S(1)} %get-tuple-element.16), channel_id=1, source_target_pairs={{0,8},{8,0},{1,9},{9,1},{2,10},{10,2},{3,11},{11,3},{4,12},{12,4},... | collective-permute-start | bytes 1990664 | tf_op jit(solution)/shard_map/cond/branch_1_fun/ppermute | solution.py:456
  36.5 1.7 %collective-permute-done.value_ref = bf16[288,1152]{1,0:T(8,128)(2,1)S(1)} collective-permute-done((bf16[288,1152]{1,0:T(8,128)(2,1)S(1)}, bf16[288,1152]{1,0:T(8,128)(2,1)S(1)}, u32[]{:S(2)}, u32[]{:S(2)}) %collective-permute-start) | collective-permute-done | bytes 663584 | tf_op jit(solution)/shard_map/cond/branch_1_fun/ppermute | solution.py:456
  38.3 1.5 %all-to-all-done.1.stats_ref = f32[32,2,128]{2,1,0:T(2,128)S(1)} async-done(((f32[32,2,128]{2,1,0:T(2,128)}), f32[32,2,128]{2,1,0:T(2,128)S(1)}, u32[]{:S(2)}, u32[]{:S(2)}) %all-to-all-start.1) | async-done | bytes 32800 | tf_op jit(solution)/shard_map/all_to_all | solution.py:443
  39.8 2.7 %shard_map.79 = (bf16[16,88,128]{2,1,0:T(8,128)(2,1)}, f32[1,128]{1,0:T(1,128)S(1)}) custom-call(f32[32,2,128]{2,1,0:T(2,128)S(1)} %all-to-all-done.1.stats_ref, bf16[288,1152]{1,0:T(8,128)(2,1)S(1)} %get-tuple-element.40.mine_ref, bf16[288,1152]{1,0:T(8,128)(2,1)S(1)} %get-tuple-element.41.other_ref), custom_call_target="tpu_custom_call" | custom-call | tf_op jit(solution)/shard_map/pallas_call | solution.py:47
  42.5 14.5 %all-to-all-start.2 = ((bf16[16,88,128]{2,1,0:T(8,128)(2,1)}), bf16[16,88,128]{2,1,0:T(8,128)(2,1)S(1)}, u32[]{:S(2)}, u32[]{:S(2)}) async-start(bf16[16,88,128]{2,1,0:T(8,128)(2,1)} %get-tuple-element.42), calls=%async_computation.2 | async-start | bytes 720896 | tf_op jit(solution)/shard_map/all_to_all | solution.py:451
  57.1 0.6 dynamic-slice_bitcast_fusion
  57.6 8.9 %all-to-all-done.2.parts_ref = bf16[16,88,128]{2,1,0:T(8,128)(2,1)S(1)} async-done(((bf16[16,88,128]{2,1,0:T(8,128)(2,1)}), bf16[16,88,128]{2,1,0:T(8,128)(2,1)S(1)}, u32[]{:S(2)}, u32[]{:S(2)}) %all-to-all-start.2) | async-done | bytes 360480 | tf_op jit(solution)/shard_map/all_to_all | solution.py:451
  66.5 0.8 %shard_map.80 = (f32[50,144]{1,0:T(8,128)}, f32[50,64]{1,0:T(8,128)}) custom-call(bf16[16,88,128]{2,1,0:T(8,128)(2,1)S(1)} %all-to-all-done.2.parts_ref), custom_call_target="tpu_custom_call" | custom-call | tf_op jit(solution)/shard_map/pallas_call | solution.py:47
  (1 shorter events, 0.0 us)
Async XLA Ops:
  2.6 14.8 %all-to-all-start = ((bf16[8,2,9344]{2,1,0:T(2,128)(2,1)}), bf16[8,2,9344]{2,1,0:T(2,128)(2,1)S(1)}, u32[]{:S(2)}, u32[]{:S(2)}) async-start(bf16[8,2,9344]{2,1,0:T(2,128)(2,1)} %shard_map.76), calls=%async_computation | async-start | bytes 598016 | tf_op jit(solution)/shard_map/all_to_all | solution.py:447
  10.8 1.2 %copy-start = (bf16[50,9216]{1,0:T(8,128)(2,1)S(1)}, bf16[50,9216]{1,0:T(8,128)(2,1)}, u32[]{:S(2)}) copy-start(bf16[50,9216]{1,0:T(8,128)(2,1)} %classes_ref.1) | copy-start | bytes 2764804
  17.5 14.1 %collective-permute-start.1 = (bf16[16,9344]{1,0:T(8,128)(2,1)S(1)}, bf16[16,9344]{1,0:T(8,128)(2,1)S(1)}, u32[]{:S(2)}, u32[]{:S(2)}) collective-permute-start(bf16[16,9344]{1,0:T(8,128)(2,1)S(1)} %reshape.16.rows_ref), channel_id=1, source_target_pairs={{0,128},{128,0},{1,129},{129,1},{2,130},{130,2},{3,131},{131,3},{4... | collective-permute-start | bytes 897032 | tf_op jit(solution)/shard_map/ppermute | solution.py:456
  22.6 17.2 %all-to-all-start.1 = ((f32[32,2,128]{2,1,0:T(2,128)}), f32[32,2,128]{2,1,0:T(2,128)S(1)}, u32[]{:S(2)}, u32[]{:S(2)}) async-start(f32[32,2,128]{2,1,0:T(2,128)} %get-tuple-element.38), calls=%async_computation.1 | async-start | bytes 65536 | tf_op jit(solution)/shard_map/all_to_all | solution.py:443
  33.8 4.4 %collective-permute-start = (bf16[288,1152]{1,0:T(8,128)(2,1)S(1)}, bf16[288,1152]{1,0:T(8,128)(2,1)S(1)}, u32[]{:S(2)}, u32[]{:S(2)}) collective-permute-start(bf16[288,1152]{1,0:T(8,128)(2,1)S(1)} %get-tuple-element.16), channel_id=1, source_target_pairs={{0,8},{8,0},{1,9},{9,1},{2,10},{10,2},{3,11},{11,3},{4,12},{12,4},... | collective-permute-start | bytes 1990664 | tf_op jit(solution)/shard_map/cond/branch_1_fun/ppermute | solution.py:456
  42.5 24.0 %all-to-all-start.2 = ((bf16[16,88,128]{2,1,0:T(8,128)(2,1)}), bf16[16,88,128]{2,1,0:T(8,128)(2,1)S(1)}, u32[]{:S(2)}, u32[]{:S(2)}) async-start(bf16[16,88,128]{2,1,0:T(8,128)(2,1)} %get-tuple-element.42), calls=%async_computation.2 | async-start | bytes 720896 | tf_op jit(solution)/shard_map/all_to_all | solution.py:451

commit v10 on v8

--- a/solution.py
+++ b/solution.py
@@ -128,8 +128,8 @@
     for t in range(FEATURES // step):
         part_w = (images_ref[:, t * step : (t + 1) * step].astype(F32) * wide).astype(BF16)
         put(jnp.dot(packing, part_w, preferred_element_type=F32), t * step, step)
-        if t % 6 == 5:
-            leave((t - 5) * step, 6 * step)
+        if t % 3 == 2:
+            leave((t - 2) * step, 3 * step)
     for copy in sent:
         copy.wait()
 
@@ -470,7 +470,7 @@
             pltpu.VMEM((1, CYCLES), F32),
             pltpu.VMEM((2, part), jnp.int32),
             pltpu.VMEM((8, 2, width), BF16),
-            pltpu.SemaphoreType.DMA((8,)),
+            pltpu.SemaphoreType.DMA((11,)),
         ],
     )
     rows = swap_rows(packed).reshape(ROWS, width)

time: 67.8 us -> 67.8 us (level)
  no operation moved by 1% of the time
where the time goes in v10:
time: 67.8 us; the launch traced here: 67.3 us
  starting transfers between devices  38.3 us (56%)
  waiting for transfers between devices  16.5 us (24%)
  Pallas kernels  9.9 us (15%)
  local copies, waits for them, and re-layouts  1.91 us (3%)
  between operations  0.69 us (1%)
    all_to_all x1, starting transfers between devices, swap_both_ways(): lax.all_to_all(value, axes + ('core',), 0, 0, axis_index_groups=groups, t...  14.4 us
    pallas_call x8, Pallas kernels, call(): pl.pallas_call(body, out_shape=outs, scratch_shapes=list(scratch), compil...  9.9 us
    all_to_all x1, starting transfers between devices, swap(): return lax.all_to_all(value, axes, split_axis=0, concat_axis=0, tiled=True)  9.81 us
    all_to_all x1, waiting for transfers between devices, swap_both_ways(): lax.all_to_all(value, axes + ('core',), 0, 0, axis_index_groups=groups, t...  8.91 us
    all_to_all x1, starting transfers between devices, swap_rows(): lax.all_to_all(value, ('core', 'cls'), 0, 0, axis_index_groups=groups, ti...  7.94 us
    ppermute x2, starting transfers between devices, flip(): return lax.ppermute(value, axis, [(0, 1), (1, 0)])  6.21 us
    all_to_all x1, waiting for transfers between devices, swap_rows(): lax.all_to_all(value, ('core', 'cls'), 0, 0, axis_index_groups=groups, ti...  4.17 us
    ppermute x2, waiting for transfers between devices, flip(): return lax.ppermute(value, axis, [(0, 1), (1, 0)])  1.72 us
  transfers between devices with their start and end apart: 5, of which 4 were waited for; matrix products, arithmetic and copies ran while one was open for 1% of the time, Pallas kernels for 7%

profile of v10, /device:TPU:1, one launch (start us, length us, event | category | flops | bytes accessed | tf_op | source)
XLA Modules:
  0.0 67.3 jit_solution(15581614350735422016)
XLA Ops:
  0.6 1.9 %shard_map.76 = bf16[8,2,9344]{2,1,0:T(2,128)(2,1)} custom-call(bf16[4,9216]{1,0:T(4,128)(2,1)} %refs_0_.1, f32[4,64]{1,0:T(4,128)} %refs_1_.1, f32[1,64]{1,0:T(1,128)} %bitcast.6, s32[2,4]{1,0:T(2,128)} %bitcast.5), custom_call_target="tpu_custom_call" | custom-call | tf_op jit(solution)/shard_map/pallas_call | solution.py:42
  2.6 7.9 %all-to-all-start = ((bf16[8,2,9344]{2,1,0:T(2,128)(2,1)}), bf16[8,2,9344]{2,1,0:T(2,128)(2,1)S(1)}, u32[]{:S(2)}, u32[]{:S(2)}) async-start(bf16[8,2,9344]{2,1,0:T(2,128)(2,1)} %shard_map.76), calls=%async_computation | async-start | bytes 598016 | tf_op jit(solution)/shard_map/all_to_all | solution.py:441
  10.5 0.0 copy-start
  10.5 1.2 %copy-done = bf16[50,9216]{1,0:T(8,128)(2,1)S(1)} copy-done((bf16[50,9216]{1,0:T(8,128)(2,1)S(1)}, bf16[50,9216]{1,0:T(8,128)(2,1)}, u32[]{:S(2)}) %copy-start) | copy-done | bytes 921624
  11.7 0.3 shard_map.77
  12.1 4.2 %all-to-all-done = bf16[8,2,9344]{2,1,0:T(2,128)(2,1)S(1)} async-done(((bf16[8,2,9344]{2,1,0:T(2,128)(2,1)}), bf16[8,2,9344]{2,1,0:T(2,128)(2,1)S(1)}, u32[]{:S(2)}, u32[]{:S(2)}) %all-to-all-start) | async-done | bytes 299040 | tf_op jit(solution)/shard_map/all_to_all | solution.py:441
  16.2 0.1 reshape.16.rows_ref
  16.4 3.6 %collective-permute-start.1 = (bf16[16,9344]{1,0:T(8,128)(2,1)S(1)}, bf16[16,9344]{1,0:T(8,128)(2,1)S(1)}, u32[]{:S(2)}, u32[]{:S(2)}) collective-permute-start(bf16[16,9344]{1,0:T(8,128)(2,1)S(1)} %reshape.16.rows_ref), channel_id=1, source_target_pairs={{0,128},{128,0},{1,129},{129,1},{2,130},{130,2},{3,131},{131,3},{4... | collective-permute-start | bytes 897032 | tf_op jit(solution)/shard_map/ppermute | solution.py:452
  19.9 1.9 %shard_map.78 = (f32[576,128]{1,0:T(8,128)S(1)}, f32[32,2,128]{2,1,0:T(2,128)}) custom-call(bf16[16,9344]{1,0:T(8,128)(2,1)S(1)} %reshape.16.rows_ref, bf16[256,2304]{1,0:T(8,128)(2,1)S(1)} %get-tuple-element.36.table_ref, f32[128,128]{1,0:T(8,128)S(1)} %get-tuple-element.37.energy_ref), custom_call_target="tpu_custom_call" | custom-call | tf_op jit(solution)/shard_map/pallas_call | solution.py:42
  21.9 9.8 %all-to-all-start.1 = ((f32[32,2,128]{2,1,0:T(2,128)}), f32[32,2,128]{2,1,0:T(2,128)S(1)}, u32[]{:S(2)}, u32[]{:S(2)}) async-start(f32[32,2,128]{2,1,0:T(2,128)} %get-tuple-element.38), calls=%async_computation.1 | async-start | bytes 65536 | tf_op jit(solution)/shard_map/all_to_all | solution.py:437
  31.7 0.0 collective-permute-done.1
  31.7 6.6 %conditional.1 = (bf16[288,1152]{1,0:T(8,128)(2,1)S(1)}, bf16[288,1152]{1,0:T(8,128)(2,1)S(1)}) conditional(s32[]{:T(128)} %convert_element_type.3, () %tuple.18, (bf16[16,9344]{1,0:T(8,128)(2,1)S(1)}, bf16[256,2304]{1,0:T(8,128)(2,1)S(1)}, f32[128,128]{1,0:T(8,128)S(1)}, bf16[16,9344]{1,0:T(8,128)(2,1)S(1)}, f32[576,128]{1,0:T(8,128)S(1)}) %tuple.19), branch_computations={%region_0.0_spmd, %region_1.0_spmd} | conditional | bytes 2654264 | solution.py:512
  31.7 1.1 %branch_1_fun.3.two_logits_ref = f32[576,128]{1,0:T(8,128)S(1)} custom-call(bf16[16,9344]{1,0:T(8,128)(2,1)S(1)} %get-tuple-element.11.rows_ref.two_ref, bf16[256,2304]{1,0:T(8,128)(2,1)S(1)} %get-tuple-element.13.table_ref, f32[128,128]{1,0:T(8,128)S(1)} %get-tuple-element.14.energy_ref), custom_call_target="tpu_custom_call" | custom-call | tf_op jit(solution)/shard_map/cond/branch_1_fun/pallas_call | solution.py:42
  32.8 1.1 %branch_1_fun.4 = (bf16[288,1152]{1,0:T(8,128)(2,1)S(1)}, bf16[288,1152]{1,0:T(8,128)(2,1)S(1)}) custom-call(bf16[16,9344]{1,0:T(8,128)(2,1)S(1)} %get-tuple-element.10.one_ref, bf16[16,9344]{1,0:T(8,128)(2,1)S(1)} %get-tuple-element.11.rows_ref.two_ref, f32[576,128]{1,0:T(8,128)S(1)} %get-tuple-element.12.one_logits_ref, ...), custom_call_target="tpu_custom_call" | custom-call | tf_op jit(solution)/shard_map/cond/branch_1_fun/pallas_call | solution.py:42
  33.9 2.7 %collective-permute-start = (bf16[288,1152]{1,0:T(8,128)(2,1)S(1)}, bf16[288,1152]{1,0:T(8,128)(2,1)S(1)}, u32[]{:S(2)}, u32[]{:S(2)}) collective-permute-start(bf16[288,1152]{1,0:T(8,128)(2,1)S(1)} %get-tuple-element.16), channel_id=1, source_target_pairs={{0,8},{8,0},{1,9},{9,1},{2,10},{10,2},{3,11},{11,3},{4,12},{12,4},... | collective-permute-start | bytes 1990664 | tf_op jit(solution)/shard_map/cond/branch_1_fun/ppermute | solution.py:452
  36.5 1.7 %collective-permute-done.value_ref = bf16[288,1152]{1,0:T(8,128)(2,1)S(1)} collective-permute-done((bf16[288,1152]{1,0:T(8,128)(2,1)S(1)}, bf16[288,1152]{1,0:T(8,128)(2,1)S(1)}, u32[]{:S(2)}, u32[]{:S(2)}) %collective-permute-start) | collective-permute-done | bytes 663584 | tf_op jit(solution)/shard_map/cond/branch_1_fun/ppermute | solution.py:452
  38.3 1.7 %all-to-all-done.1.stats_ref = f32[32,2,128]{2,1,0:T(2,128)S(1)} async-done(((f32[32,2,128]{2,1,0:T(2,128)}), f32[32,2,128]{2,1,0:T(2,128)S(1)}, u32[]{:S(2)}, u32[]{:S(2)}) %all-to-all-start.1) | async-done | bytes 32800 | tf_op jit(solution)/shard_map/all_to_all | solution.py:437
  40.0 2.7 %shard_map.79 = (bf16[16,88,128]{2,1,0:T(8,128)(2,1)}, f32[1,128]{1,0:T(1,128)S(1)}) custom-call(f32[32,2,128]{2,1,0:T(2,128)S(1)} %all-to-all-done.1.stats_ref, bf16[288,1152]{1,0:T(8,128)(2,1)S(1)} %get-tuple-element.40.mine_ref, bf16[288,1152]{1,0:T(8,128)(2,1)S(1)} %get-tuple-element.41.other_ref), custom_call_target="tpu_custom_call" | custom-call | tf_op jit(solution)/shard_map/pallas_call | solution.py:42
  42.7 14.4 %all-to-all-start.2 = ((bf16[16,88,128]{2,1,0:T(8,128)(2,1)}), bf16[16,88,128]{2,1,0:T(8,128)(2,1)S(1)}, u32[]{:S(2)}, u32[]{:S(2)}) async-start(bf16[16,88,128]{2,1,0:T(8,128)(2,1)} %get-tuple-element.42), calls=%async_computation.2 | async-start | bytes 720896 | tf_op jit(solution)/shard_map/all_to_all | solution.py:447
  57.0 0.6 dynamic-slice_bitcast_fusion
  57.6 8.9 %all-to-all-done.2.parts_ref = bf16[16,88,128]{2,1,0:T(8,128)(2,1)S(1)} async-done(((bf16[16,88,128]{2,1,0:T(8,128)(2,1)}), bf16[16,88,128]{2,1,0:T(8,128)(2,1)S(1)}, u32[]{:S(2)}, u32[]{:S(2)}) %all-to-all-start.2) | async-done | bytes 360480 | tf_op jit(solution)/shard_map/all_to_all | solution.py:447
  66.5 0.8 %shard_map.80 = (f32[50,144]{1,0:T(8,128)}, f32[50,64]{1,0:T(8,128)}) custom-call(bf16[16,88,128]{2,1,0:T(8,128)(2,1)S(1)} %all-to-all-done.2.parts_ref), custom_call_target="tpu_custom_call" | custom-call | tf_op jit(solution)/shard_map/pallas_call | solution.py:42
  (1 shorter events, 0.0 us)
Async XLA Ops:
  2.6 13.7 %all-to-all-start = ((bf16[8,2,9344]{2,1,0:T(2,128)(2,1)}), bf16[8,2,9344]{2,1,0:T(2,128)(2,1)S(1)}, u32[]{:S(2)}, u32[]{:S(2)}) async-start(bf16[8,2,9344]{2,1,0:T(2,128)(2,1)} %shard_map.76), calls=%async_computation | async-start | bytes 598016 | tf_op jit(solution)/shard_map/all_to_all | solution.py:441
  10.5 1.2 %copy-start = (bf16[50,9216]{1,0:T(8,128)(2,1)S(1)}, bf16[50,9216]{1,0:T(8,128)(2,1)}, u32[]{:S(2)}) copy-start(bf16[50,9216]{1,0:T(8,128)(2,1)} %classes_ref.1) | copy-start | bytes 2764804
  16.4 15.3 %collective-permute-start.1 = (bf16[16,9344]{1,0:T(8,128)(2,1)S(1)}, bf16[16,9344]{1,0:T(8,128)(2,1)S(1)}, u32[]{:S(2)}, u32[]{:S(2)}) collective-permute-start(bf16[16,9344]{1,0:T(8,128)(2,1)S(1)} %reshape.16.rows_ref), channel_id=1, source_target_pairs={{0,128},{128,0},{1,129},{129,1},{2,130},{130,2},{3,131},{131,3},{4... | collective-permute-start | bytes 897032 | tf_op jit(solution)/shard_map/ppermute | solution.py:452
  21.9 18.1 %all-to-all-start.1 = ((f32[32,2,128]{2,1,0:T(2,128)}), f32[32,2,128]{2,1,0:T(2,128)S(1)}, u32[]{:S(2)}, u32[]{:S(2)}) async-start(f32[32,2,128]{2,1,0:T(2,128)} %get-tuple-element.38), calls=%async_computation.1 | async-start | bytes 65536 | tf_op jit(solution)/shard_map/all_to_all | solution.py:437
  33.9 4.4 %collective-permute-start = (bf16[288,1152]{1,0:T(8,128)(2,1)S(1)}, bf16[288,1152]{1,0:T(8,128)(2,1)S(1)}, u32[]{:S(2)}, u32[]{:S(2)}) collective-permute-start(bf16[288,1152]{1,0:T(8,128)(2,1)S(1)} %get-tuple-element.16), channel_id=1, source_target_pairs={{0,8},{8,0},{1,9},{9,1},{2,10},{10,2},{3,11},{11,3},{4,12},{12,4},... | collective-permute-start | bytes 1990664 | tf_op jit(solution)/shard_map/cond/branch_1_fun/ppermute | solution.py:452
  42.7 23.9 %all-to-all-start.2 = ((bf16[16,88,128]{2,1,0:T(8,128)(2,1)}), bf16[16,88,128]{2,1,0:T(8,128)(2,1)S(1)}, u32[]{:S(2)}, u32[]{:S(2)}) async-start(bf16[16,88,128]{2,1,0:T(8,128)(2,1)} %get-tuple-element.42), calls=%async_computation.2 | async-start | bytes 720896 | tf_op jit(solution)/shard_map/all_to_all | solution.py:447
